TPU v7x, 128 devices: a whole 4x4x4 slice. The times are simulated.
128 devices in a mesh: px: 8 (over y, core), py: 16 (over z, x).
Axes of the slice: x: 4, y: 4, z: 4, core: 2. Of those that a mesh axis runs over, the one named last changes fastest.
Arguments:
- fine_residual: bfloat16 [524288, 256], P(('px', 'py')), may hold values from -6 to 6
- dest_owner: int32 [524288], P(('px', 'py')), may hold values from 0 to 127, as said below
- coarse_slot: int32 [524288], P(('px', 'py')), may hold values from 0 to 511, as said below
- ghost_slot: int32 [512, 32], P(('px', 'py')), may hold values from 0 to 511, as said below
- child_type: int32 [524288], P(('px', 'py')), may hold values from 0 to 7
- restrict_table: bfloat16 [8, 64, 64], replicated, may hold values from -0.75 to 0.75
- inverse_blocks: bfloat16 [65536, 4096], P(('px', 'py')), may hold values from -0.45 to 1.05
- face_table: bfloat16 [6, 64, 64], replicated, may hold values from -0.75 to 0.75
- face_coef: float32 [16], replicated, may hold values from 0.2 to 2
- coef_index: int32 [6, 65536], P(None, ('px', 'py')), may hold values from 0 to 15
- neighbours: int32 [6, 65536], P(None, ('px', 'py')), may hold values from 0 to 65535, as said below
Outputs:
- coarse_solution: float32 [65536, 256], P(('px', 'py'))
- fine_correction: bfloat16 [524288, 256], P(('px', 'py'))
Inputs may be any that keep to these rules, and one draw needn't show every extreme that they name: `dest_owner`: the owner is the element's own device or a device one step away along py (same px index) or along px (same py index); every coarse element has exactly 8 fine children, with distinct child_type. `coarse_slot`: for an element whose parent lives on another device the value is below 32. `ghost_slot`: j = 0, 1, 2, 3 stands for the device one lower along py, one higher along py, one lower along px, one higher along px; a device's four lists hold distinct elements; each remote child of a device's coarse element is found in the list toward the child's device, at the row that its coarse_slot names; between two neighbouring devices at most 32 parents have children across, and some pair has exactly 32. `neighbours`: the element across a face lives on the same device or on a device one step away along py or along px, never outside the grid.
All inputs are finite; a program needn't handle non-finite values.
Results may differ from a plain program's by a relative error of at most 0.0073.
Values may be sent and summed in bfloat16 or wider, within the bound.
No kernel may reach another device: no remote copies, remote signals or barrier semaphores. Data moves between devices by JAX's collectives and lax.ppermute only.
A program may use at most 64 MiB of HBM per device.

v0:
```python
import math

import jax
import jax.numpy as jnp
from jax import lax
from jax.sharding import PartitionSpec as P

omega = 0.5


def extended_2(shard, sides, width):
    edges = {}
    for axis, dim in sides:
        size, length = (lax.axis_size(axis), shard.shape[dim])
        up = [(i, (i + 1) % size) for i in range(size - 1)]
        last = lax.slice_in_dim(shard, length - width, length, axis=dim)
        first = lax.slice_in_dim(shard, 0, width, axis=dim)
        edges[dim] = (
            lax.ppermute(last, axis, up),
            lax.ppermute(first, axis, [(b, a) for a, b in up]),
        )
    done = []
    for _, dim in sides:
        low, high = edges[dim]
        around = [(width, width) if d in done else (0, 0) for d in range(shard.ndim)]
        shard = jnp.concatenate([jnp.pad(low, around), shard, jnp.pad(high, around)], axis=dim)
        done.append(dim)
    return shard


def stacked_table(matrices, flipped):
    order_dim = matrices.shape[1]
    if flipped:
        arranged = jnp.transpose(matrices, (1, 0, 2))
    else:
        arranged = jnp.transpose(matrices, (2, 0, 1))
    return arranged.reshape(order_dim, matrices.shape[0] * order_dim)


def typed_product(blocks, child_type, matrices, flipped):
    item_count = blocks.shape[0]
    row_width = blocks.shape[1]
    order_dim = matrices.shape[1]
    kind_count = matrices.shape[0]
    columns = blocks.reshape(item_count * (row_width // order_dim), order_dim)
    products = jnp.dot(
        columns, stacked_table(matrices, flipped), preferred_element_type=jnp.float32
    )
    products = products.reshape(item_count, row_width // order_dim, kind_count, order_dim)
    selector = (child_type[:, None] == jnp.arange(kind_count, dtype=jnp.int32)[None, :]).astype(
        jnp.float32
    )
    picked = jnp.sum(products * selector[:, None, :, None], axis=2)
    return picked.reshape(item_count, row_width)


def pick_rows(table, index):
    count = index.shape[0]
    table_rows = table.shape[0]
    block = math.gcd(count, 1024)

    def one_block(block_index):
        onehot = (block_index[:, None] == jnp.arange(table_rows, dtype=jnp.int32)[None, :]).astype(
            jnp.bfloat16
        )
        return jnp.dot(onehot, table, preferred_element_type=jnp.float32).astype(table.dtype)

    picked = lax.map(one_block, index.reshape(count // block, block))
    return picked.reshape(count, table.shape[1])


def compact_blocks(extended, coarse_count, row_width):
    return jnp.stack(
        [extended[0, 1], extended[1, 0], extended[1, 1], extended[1, 2], extended[2, 1]]
    ).reshape(5 * coarse_count, row_width)


def compact_number(block_number):
    return jnp.where(
        block_number == 1,
        0,
        jnp.where(
            block_number == 3,
            1,
            jnp.where(block_number == 4, 2, jnp.where(block_number == 5, 3, 4)),
        ),
    ).astype(jnp.int32)


def pack_joint(lists):
    return jnp.stack([jnp.stack([lists[2], lists[1]]), jnp.stack([lists[0], lists[3]])])


def unpack_joint(extended):
    return jnp.stack([extended[1, 0], extended[2, 3], extended[0, 2], extended[3, 1]])


def shards(
    fine_residual,
    dest_owner,
    coarse_slot,
    ghost_slot,
    child_type,
    restrict_table,
    inverse_blocks,
    face_table,
    face_coef,
    coef_index,
    neighbours,
):
    fine_count, row_width = fine_residual.shape
    coarse_count = inverse_blocks.shape[0]
    ghost_rows = ghost_slot.shape[1]
    order_dim = restrict_table.shape[1]
    rhs_count = row_width // order_dim
    width_py = lax.axis_size("py")
    index_px = lax.axis_index("px")
    index_py = lax.axis_index("py")
    own_index = index_px * width_py + index_py
    contrib = typed_product(fine_residual, child_type, restrict_table, False).astype(jnp.bfloat16)
    offset = dest_owner - own_index
    is_local = offset == 0
    direction = jnp.where(
        offset == -1, 0, jnp.where(offset == 1, 1, jnp.where(offset < 0, 2, 3))
    ).astype(jnp.int32)
    slot_onehot = (
        (coarse_slot[:, None] == jnp.arange(coarse_count, dtype=jnp.int32)[None, :])
        & is_local[:, None]
    ).astype(jnp.bfloat16)
    coarse_local = lax.dot_general(
        slot_onehot, contrib, (((0,), (0,)), ((), ())), preferred_element_type=jnp.float32
    )
    ghost_target = jnp.where(is_local, 4 * ghost_rows, direction * ghost_rows + coarse_slot)
    target_onehot = (
        ghost_target[:, None] == jnp.arange(4 * ghost_rows, dtype=jnp.int32)[None, :]
    ).astype(jnp.bfloat16)
    outgoing = lax.dot_general(
        target_onehot, contrib, (((0,), (0,)), ((), ())), preferred_element_type=jnp.float32
    )
    outgoing = outgoing.reshape(4, ghost_rows, row_width)
    incoming = unpack_joint(extended_2(pack_joint(outgoing), (("px", 0), ("py", 1)), 1))
    list_onehot = (
        ghost_slot.reshape(-1)[:, None] == jnp.arange(coarse_count, dtype=jnp.int32)[None, :]
    ).astype(jnp.float32)
    arrived = lax.dot_general(
        list_onehot,
        incoming.reshape(4 * ghost_rows, row_width),
        (((0,), (0,)), ((), ())),
        precision=lax.Precision.HIGHEST,
        preferred_element_type=jnp.float32,
    )
    coarse_rhs = (coarse_local + arrived).astype(jnp.bfloat16)
    inverse = inverse_blocks.reshape(coarse_count, order_dim, order_dim)
    first_sweep = jnp.einsum(
        "cij,csj->csi",
        inverse,
        coarse_rhs.reshape(coarse_count, rhs_count, order_dim),
        preferred_element_type=jnp.float32,
    )
    first_sweep = first_sweep.reshape(coarse_count, row_width).astype(jnp.bfloat16)
    extended = extended_2(
        first_sweep.reshape(1, 1, coarse_count, row_width), (("px", 0), ("py", 1)), 1
    )
    nearby = compact_blocks(extended, coarse_count, row_width)
    across_owner = neighbours // coarse_count
    block_number = (across_owner // width_py - index_px + 1) * 3 + (
        across_owner % width_py - index_py + 1
    )
    local_index = compact_number(block_number) * coarse_count + neighbours % coarse_count
    beside = pick_rows(nearby, local_index.reshape(-1))
    faces_count = face_table.shape[0]
    kind_count = face_coef.shape[0]
    face_scale = jnp.sum(
        jnp.where(
            coef_index[:, :, None] == jnp.arange(kind_count, dtype=jnp.int32)[None, None, :],
            face_coef[None, None, :],
            jnp.float32(0.0),
        ),
        axis=2,
    )
    face_terms = jnp.einsum(
        "fcsj,fij->fcsi",
        beside.reshape(faces_count, coarse_count, rhs_count, order_dim),
        face_table,
        preferred_element_type=jnp.float32,
    )
    coupled = jnp.sum(face_terms * face_scale[:, :, None, None], axis=0).astype(jnp.bfloat16)
    correction = jnp.einsum(
        "cij,csj->csi", inverse, coupled, preferred_element_type=jnp.float32
    ).reshape(coarse_count, row_width)
    coarse_solution = first_sweep.astype(jnp.float32) - omega * correction
    answer = coarse_solution.astype(jnp.bfloat16)
    ghost_row = jnp.where(is_local, 0, coarse_slot)
    replies = pick_rows(answer, ghost_slot.reshape(-1)).reshape(4, ghost_rows, row_width)
    returned = unpack_joint(extended_2(pack_joint(replies), (("px", 0), ("py", 1)), 1))
    table = jnp.concatenate([returned.reshape(4 * ghost_rows, row_width), answer], axis=0)
    which = jnp.where(is_local, 4 * ghost_rows + coarse_slot, direction * ghost_rows + ghost_row)
    fetched = pick_rows(table, which)
    fine_correction = typed_product(fetched, child_type, restrict_table, True).astype(jnp.bfloat16)
    return (coarse_solution, fine_correction)


def solution(mesh):
    in_specs = (
        P(("px", "py"), None),
        P(("px", "py")),
        P(("px", "py")),
        P(("px", "py"), None),
        P(("px", "py")),
        P(),
        P(("px", "py"), None),
        P(),
        P(),
        P(None, ("px", "py")),
        P(None, ("px", "py")),
    )
    out_specs = (P(("px", "py"), None), P(("px", "py"), None))
    return jax.shard_map(shards, mesh=mesh, in_specs=in_specs, out_specs=out_specs, check_vma=False)
```

profile of v0, /device:TPU:112, one launch (start us, length us, event | category | flops | bytes accessed | tf_op | source)
XLA Modules:
  0.0 137.7 jit_solution(15572384721840626129)
XLA Ops:
  0.7 0.8 fusion.28
  1.5 3.0 %copy.88 = bf16[4096,256]{0,1:T(8,128)(2,1)S(1)} copy(bf16[4096,256]{1,0:T(8,128)(2,1)} %param.15) | data formatting | bytes 4194304 | tf_op args[0]
  4.5 5.5 %multiply_reduce_fusion.1 = bf16[4096,4,64]{0,2,1:T(8,128)(2,1)S(1)} fusion(f32[4096,8]{0,1:T(8,128)S(1)} %fusion.28, bf16[4096,4,64,1]{0,2,3,1:T(8,128)(2,1)S(1)} %bitcast.130, bf16[8,64,64]{2,1,0:T(8,128)(2,1)S(1)} %copy-done.3), kind=kOutput, calls=%fused_computation.15 | convolution fusion | flops 1089470464 | bytes 4390912 | tf_op jit(solution)/shard_map/dot_general | solution.py:46
  10.1 1.5 %fusion.22 = f32[128,256]{1,0:T(8,128)S(1)} fusion(bf16[4096,256]{0,1:T(8,128)(2,1)S(1)} %bitcast.141, s32[4096]{0:T(1024)S(1)} %get-tuple-element.119), kind=kOutput, calls=%fused_computation.30 | convolution fusion | flops 269484032 | bytes 2244608 | tf_op jit(solution)/shard_map/dot_general | solution.py:137
  11.6 1.9 %collective-permute-start.2 = (f32[1,2,32,256]{3,2,1,0:T(8,128)S(1)}, f32[1,2,32,256]{3,2,1,0:T(8,128)S(1)}, u32[]{:S(2)}, u32[]{:S(2)}) collective-permute-start(f32[1,2,32,256]{3,2,1,0:T(8,128)S(1)} %maximum_bitcast_fusion.1), channel_id=1, source_target_pairs={{0,16},{16,32},{32,48},{48,64},{64,80},{80,96},{96,112},{1,17},{17... | collective-permute-start | bytes 196616 | tf_op jit(solution)/shard_map/ppermute | solution.py:19
  13.5 3.6 %collective-permute-start.3 = (f32[1,2,32,256]{3,2,1,0:T(8,128)S(1)}, f32[1,2,32,256]{3,2,1,0:T(8,128)S(1)}, u32[]{:S(2)}, u32[]{:S(2)}) collective-permute-start(f32[1,2,32,256]{3,2,1,0:T(8,128)S(1)} %maximum_bitcast_fusion), channel_id=1, source_target_pairs={{16,0},{32,16},{48,32},{64,48},{80,64},{96,80},{112,96},{17,1},{33... | collective-permute-start | bytes 196616 | tf_op jit(solution)/shard_map/ppermute | solution.py:20
  17.2 4.5 %collective-permute-start.1 = (f32[2,1,32,256]{3,2,1,0:T(8,128)S(1)}, f32[2,1,32,256]{3,2,1,0:T(8,128)S(1)}, u32[]{:S(2)}, u32[]{:S(2)}) collective-permute-start(f32[2,1,32,256]{3,2,1,0:T(8,128)S(1)} %get-tuple-element.107), channel_id=1, source_target_pairs={{1,0},{2,1},{3,2},{4,3},{5,4},{6,5},{7,6},{8,7},{9,8},{10,9},{11,1... | collective-permute-start | bytes 196616 | tf_op jit(solution)/shard_map/ppermute | solution.py:20
  21.7 1.9 %collective-permute-start = (f32[2,1,32,256]{3,2,1,0:T(8,128)S(1)}, f32[2,1,32,256]{3,2,1,0:T(8,128)S(1)}, u32[]{:S(2)}, u32[]{:S(2)}) collective-permute-start(f32[2,1,32,256]{3,2,1,0:T(8,128)S(1)} %get-tuple-element.106), channel_id=1, source_target_pairs={{0,1},{1,2},{2,3},{3,4},{4,5},{5,6},{6,7},{7,8},{8,9},{9,10},{10,1... | collective-permute-start | bytes 196616 | tf_op jit(solution)/shard_map/ppermute | solution.py:19
  23.7 1.9 %fusion.11 = f32[512,256]{0,1:T(8,128)S(1)} fusion(bf16[4096,256]{0,1:T(8,128)(2,1)S(1)} %bitcast.142, s32[4096]{0:T(1024)S(1)} %copy-done.8, pred[4096]{0:T(1024)(128)(4,1)S(1)} %subtract_compare_fusion), kind=kOutput, calls=%fused_computation.18 | convolution fusion | flops 1077936128 | bytes 2641920 | tf_op jit(solution)/shard_map/dot_general | solution.py:130
  25.7 6.5 %copy.89 = bf16[512,4096]{0,1:T(8,128)(2,1)} copy(bf16[512,4096]{1,0:T(8,128)(2,1)} %param.21) | data formatting | bytes 8388608 | tf_op args[6]
  32.1 13.0 %copy.91 = bf16[512,64,64]{2,1,0:T(8,128)(2,1)} copy(bf16[512,64,64]{0,2,1:T(8,128)(2,1)} %bitcast.123) | data formatting | bytes 8388608 | tf_op jit(solution)/shard_map/reshape | solution.py:153
  45.2 0.5 fusion.21
  45.7 0.3 copy.90
  46.1 7.8 %fusion.44 = bf16[512,4,64]{2,1,0:T(4,128)(2,1)S(1)} fusion(bf16[512,4,64]{2,1,0:T(4,128)(2,1)S(1)} %copy.90, bf16[512,64,64]{2,1,0:T(8,128)(2,1)} %copy.91), kind=kOutput, calls=%fused_computation.107 | convolution fusion | flops 16777216 | bytes 4718592 | tf_op jit(solution)/shard_map/cij,csj->csi/dot_general | solution.py:154
  53.9 0.3 copy.92
  54.2 1.9 %collective-permute-start.4 = (bf16[1,1,512,256]{2,3,1,0:T(8,128)(2,1)S(1)}, bf16[1,1,512,256]{2,3,1,0:T(8,128)(2,1)S(1)}, u32[]{:S(2)}, u32[]{:S(2)}) collective-permute-start(bf16[1,1,512,256]{2,3,1,0:T(8,128)(2,1)S(1)} %bitcast.125), channel_id=1, source_target_pairs={{0,16},{16,32},{32,48},{48,64},{64,80},{80,96},{96,112},{1,17},{17... | collective-permute-start | bytes 786440 | tf_op jit(solution)/shard_map/ppermute | solution.py:19
  56.2 2.8 %collective-permute-start.5 = (bf16[1,1,512,256]{2,3,1,0:T(8,128)(2,1)S(1)}, bf16[1,1,512,256]{2,3,1,0:T(8,128)(2,1)S(1)}, u32[]{:S(2)}, u32[]{:S(2)}) collective-permute-start(bf16[1,1,512,256]{2,3,1,0:T(8,128)(2,1)S(1)} %bitcast.126), channel_id=1, source_target_pairs={{0,1},{1,2},{2,3},{3,4},{4,5},{5,6},{6,7},{7,8},{8,9},{9,10},{10,1... | collective-permute-start | bytes 786440 | tf_op jit(solution)/shard_map/ppermute | solution.py:19
  59.2 5.1 %collective-permute-start.6 = (bf16[1,1,512,256]{2,3,1,0:T(8,128)(2,1)S(1)}, bf16[1,1,512,256]{2,3,1,0:T(8,128)(2,1)S(1)}, u32[]{:S(2)}, u32[]{:S(2)}) collective-permute-start(bf16[1,1,512,256]{2,3,1,0:T(8,128)(2,1)S(1)} %bitcast.127), channel_id=1, source_target_pairs={{1,0},{2,1},{3,2},{4,3},{5,4},{6,5},{7,6},{8,7},{9,8},{10,9},{11,1... | collective-permute-start | bytes 786440 | tf_op jit(solution)/shard_map/ppermute | solution.py:20
  64.3 3.5 %collective-permute-start.7 = (bf16[1,1,512,256]{2,3,1,0:T(8,128)(2,1)S(1)}, bf16[1,1,512,256]{2,3,1,0:T(8,128)(2,1)S(1)}, u32[]{:S(2)}, u32[]{:S(2)}) collective-permute-start(bf16[1,1,512,256]{2,3,1,0:T(8,128)(2,1)S(1)} %bitcast.128), channel_id=1, source_target_pairs={{16,0},{32,16},{48,32},{64,48},{80,64},{96,80},{112,96},{17,1},{33... | collective-permute-start | bytes 786440 | tf_op jit(solution)/shard_map/ppermute | solution.py:20
  67.9 0.8 collective-permute-done.5
  68.7 1.9 %collective-permute-done.6 = bf16[1,1,512,256]{2,3,1,0:T(8,128)(2,1)S(1)} collective-permute-done((bf16[1,1,512,256]{2,3,1,0:T(8,128)(2,1)S(1)}, bf16[1,1,512,256]{2,3,1,0:T(8,128)(2,1)S(1)}, u32[]{:S(2)}, u32[]{:S(2)}) %collective-permute-start.6) | collective-permute-done | bytes 262176 | tf_op jit(solution)/shard_map/ppermute | solution.py:20
  70.6 1.0 collective-permute-done.7
  71.6 0.6 copy.93
  72.2 8.0 %while.24 = (s32[]{:T(128)}, bf16[3,1024,256]{2,1,0:T(8,128)(2,1)}, s32[3,1024]{1,0:T(4,128)S(1)}, bf16[2560,256]{1,0:T(8,128)(2,1)S(1)}, s32[]{:T(128)}) while((s32[]{:T(128)}, bf16[3,1024,256]{2,1,0:T(8,128)(2,1)}, s32[3,1024]{1,0:T(4,128)S(1)}, bf16[2560,256]{1,0:T(8,128)(2,1)S(1)}, s32[]{:T(128)}) %tuple.62), condition=%wide.region_2.3_spmd, body=%wide.region_1.2_spmd.sunk | while | flops 1345060864 | bytes 1847873 | solution.py:68
  72.2 2.6 %fusion.63 = bf16[3,1024,256]{2,1,0:T(8,128)(2,1)} fusion(bf16[3,1024,256]{2,1,0:T(8,128)(2,1)} %get-tuple-element.176, s32[]{:T(128)} %get-tuple-element.175, bf16[2560,256]{1,0:T(8,128)(2,1)S(1)} %get-tuple-element.183, s32[1024]{0:T(1024)S(1)} %bitcast.139), kind=kOutput, calls=%fused_computation.5.clone.1 | convolution fusion | flops 1345060864 | bytes 1839616 | tf_op jit(solution)/shard_map/while/body/eval_jaxpr/dot_general | solution.py:66
  74.9 2.6 %fusion.63 = bf16[3,1024,256]{2,1,0:T(8,128)(2,1)} fusion(bf16[3,1024,256]{2,1,0:T(8,128)(2,1)} %get-tuple-element.176, s32[]{:T(128)} %get-tuple-element.175, bf16[2560,256]{1,0:T(8,128)(2,1)S(1)} %get-tuple-element.183, s32[1024]{0:T(1024)S(1)} %bitcast.139), kind=kOutput, calls=%fused_computation.5.clone.1 | convolution fusion | flops 1345060864 | bytes 1839616 | tf_op jit(solution)/shard_map/while/body/eval_jaxpr/dot_general | solution.py:66
  77.5 2.6 %fusion.63 = bf16[3,1024,256]{2,1,0:T(8,128)(2,1)} fusion(bf16[3,1024,256]{2,1,0:T(8,128)(2,1)} %get-tuple-element.176, s32[]{:T(128)} %get-tuple-element.175, bf16[2560,256]{1,0:T(8,128)(2,1)S(1)} %get-tuple-element.183, s32[1024]{0:T(1024)S(1)} %bitcast.139), kind=kOutput, calls=%fused_computation.5.clone.1 | convolution fusion | flops 1345060864 | bytes 1839616 | tf_op jit(solution)/shard_map/while/body/eval_jaxpr/dot_general | solution.py:66
  80.2 4.6 %reshape.129 = bf16[6,512,4,64]{3,2,1,0:T(4,128)(2,1)S(1)} reshape(bf16[3,1024,256]{2,1,0:T(8,128)(2,1)} %get-tuple-element.58) | data formatting | bytes 3145728 | tf_op jit(solution)/shard_map/reshape;reshape | solution.py:183
  84.8 1.9 %multiply_reduce_fusion.2 = bf16[512,4,64]{0,2,1:T(8,128)(2,1)} fusion(bf16[6,512,4,64]{3,2,1,0:T(4,128)(2,1)S(1)} %reshape.129, f32[6,512]{1,0:T(8,128)S(1)} %select_reduce_fusion, bf16[6,64,64]{2,1,0:T(8,128)(2,1)S(1)} %copy-done), kind=kOutput, calls=%fused_computation.23 | convolution fusion | flops 102105088 | bytes 1896448 | tf_op jit(solution)/shard_map/fcsj,fij->fcsi/dot_general | solution.py:181
  86.7 1.3 copy.96
  88.0 7.8 %fusion.45 = f32[512,4,64]{2,1,0:T(4,128)S(1)} fusion(bf16[512,4,64]{2,1,0:T(4,128)(2,1)S(1)} %copy.96, bf16[512,64,64]{2,1,0:T(8,128)(2,1)} %copy.91), kind=kOutput, calls=%fused_computation.108 | convolution fusion | flops 16777216 | bytes 4980736 | tf_op jit(solution)/shard_map/cij,csj->csi/dot_general | solution.py:188
  95.7 0.4 copy.98
  96.2 0.2 convolution_convert_fusion
  96.5 5.6 %collective-permute-start.9 = (bf16[2,1,32,256]{3,2,1,0:T(8,128)(2,1)S(1)}, bf16[2,1,32,256]{3,2,1,0:T(8,128)(2,1)S(1)}, u32[]{:S(2)}, u32[]{:S(2)}) collective-permute-start(bf16[2,1,32,256]{3,2,1,0:T(8,128)(2,1)S(1)} %get-tuple-element.113), channel_id=1, source_target_pairs={{1,0},{2,1},{3,2},{4,3},{5,4},{6,5},{7,6},{8,7},{9,8},{10,9},{11,1... | collective-permute-start | bytes 98312 | tf_op jit(solution)/shard_map/ppermute | solution.py:20
  102.5 1.9 %collective-permute-start.10 = (bf16[1,2,32,256]{3,2,1,0:T(8,128)(2,1)S(1)}, bf16[1,2,32,256]{3,2,1,0:T(8,128)(2,1)S(1)}, u32[]{:S(2)}, u32[]{:S(2)}) collective-permute-start(bf16[1,2,32,256]{3,2,1,0:T(8,128)(2,1)S(1)} %maximum_bitcast_fusion.3), channel_id=1, source_target_pairs={{0,16},{16,32},{32,48},{48,64},{64,80},{80,96},{96,112},{1,17},{17... | collective-permute-start | bytes 98312 | tf_op jit(solution)/shard_map/ppermute | solution.py:19
  104.4 3.6 %collective-permute-start.11 = (bf16[1,2,32,256]{3,2,1,0:T(8,128)(2,1)S(1)}, bf16[1,2,32,256]{3,2,1,0:T(8,128)(2,1)S(1)}, u32[]{:S(2)}, u32[]{:S(2)}) collective-permute-start(bf16[1,2,32,256]{3,2,1,0:T(8,128)(2,1)S(1)} %maximum_bitcast_fusion.2), channel_id=1, source_target_pairs={{16,0},{32,16},{48,32},{64,48},{80,64},{96,80},{112,96},{17,1},{33... | collective-permute-start | bytes 98312 | tf_op jit(solution)/shard_map/ppermute | solution.py:20
  108.1 2.1 %collective-permute-start.8 = (bf16[2,1,32,256]{3,2,1,0:T(8,128)(2,1)S(1)}, bf16[2,1,32,256]{3,2,1,0:T(8,128)(2,1)S(1)}, u32[]{:S(2)}, u32[]{:S(2)}) collective-permute-start(bf16[2,1,32,256]{3,2,1,0:T(8,128)(2,1)S(1)} %get-tuple-element.112), channel_id=1, source_target_pairs={{0,1},{1,2},{2,3},{3,4},{4,5},{5,6},{6,7},{7,8},{8,9},{9,10},{10,1... | collective-permute-start | bytes 98312 | tf_op jit(solution)/shard_map/ppermute | solution.py:19
  110.2 1.0 copy.104
  111.2 4.8 %collective-permute-done.8 = bf16[2,1,32,256]{3,2,1,0:T(8,128)(2,1)S(1)} collective-permute-done((bf16[2,1,32,256]{3,2,1,0:T(8,128)(2,1)S(1)}, bf16[2,1,32,256]{3,2,1,0:T(8,128)(2,1)S(1)}, u32[]{:S(2)}, u32[]{:S(2)}) %collective-permute-start.8) | collective-permute-done | bytes 32800 | tf_op jit(solution)/shard_map/ppermute | solution.py:19
  116.4 5.8 %while.25 = (s32[]{:T(128)}, bf16[4,1024,256]{2,1,0:T(8,128)(2,1)}, s32[4,1024]{1,0:T(4,128)S(1)}, bf16[640,256]{1,0:T(8,128)(2,1)S(1)}, s32[]{:T(128)}) while((s32[]{:T(128)}, bf16[4,1024,256]{2,1,0:T(8,128)(2,1)}, s32[4,1024]{1,0:T(4,128)S(1)}, bf16[640,256]{1,0:T(8,128)(2,1)S(1)}, s32[]{:T(128)}) %tuple.59), condition=%wide.region_6.7_spmd, body=%wide.region_5.6_spmd.sunk | while | flops 336461824 | bytes 864833 | solution.py:68
  116.4 1.4 %fusion.65 = bf16[4,1024,256]{2,1,0:T(8,128)(2,1)} fusion(bf16[4,1024,256]{2,1,0:T(8,128)(2,1)} %get-tuple-element.191, s32[]{:T(128)} %get-tuple-element.190, bf16[640,256]{1,0:T(8,128)(2,1)S(1)} %get-tuple-element.198, s32[1024]{0:T(1024)S(1)} %bitcast.140), kind=kOutput, calls=%fused_computation.12.clone.1 | convolution fusion | flops 336461824 | bytes 856576 | tf_op jit(solution)/shard_map/while/body/eval_jaxpr/dot_general | solution.py:66
  117.9 1.4 %fusion.65 = bf16[4,1024,256]{2,1,0:T(8,128)(2,1)} fusion(bf16[4,1024,256]{2,1,0:T(8,128)(2,1)} %get-tuple-element.191, s32[]{:T(128)} %get-tuple-element.190, bf16[640,256]{1,0:T(8,128)(2,1)S(1)} %get-tuple-element.198, s32[1024]{0:T(1024)S(1)} %bitcast.140), kind=kOutput, calls=%fused_computation.12.clone.1 | convolution fusion | flops 336461824 | bytes 856576 | tf_op jit(solution)/shard_map/while/body/eval_jaxpr/dot_general | solution.py:66
  119.3 1.4 %fusion.65 = bf16[4,1024,256]{2,1,0:T(8,128)(2,1)} fusion(bf16[4,1024,256]{2,1,0:T(8,128)(2,1)} %get-tuple-element.191, s32[]{:T(128)} %get-tuple-element.190, bf16[640,256]{1,0:T(8,128)(2,1)S(1)} %get-tuple-element.198, s32[1024]{0:T(1024)S(1)} %bitcast.140), kind=kOutput, calls=%fused_computation.12.clone.1 | convolution fusion | flops 336461824 | bytes 856576 | tf_op jit(solution)/shard_map/while/body/eval_jaxpr/dot_general | solution.py:66
  120.8 1.4 %fusion.65 = bf16[4,1024,256]{2,1,0:T(8,128)(2,1)} fusion(bf16[4,1024,256]{2,1,0:T(8,128)(2,1)} %get-tuple-element.191, s32[]{:T(128)} %get-tuple-element.190, bf16[640,256]{1,0:T(8,128)(2,1)S(1)} %get-tuple-element.198, s32[1024]{0:T(1024)S(1)} %bitcast.140), kind=kOutput, calls=%fused_computation.12.clone.1 | convolution fusion | flops 336461824 | bytes 856576 | tf_op jit(solution)/shard_map/while/body/eval_jaxpr/dot_general | solution.py:66
  122.2 3.4 %copy.101 = bf16[4,1024,256]{1,0,2:T(4,128)(2,1)S(1)} copy(bf16[4,1024,256]{2,1,0:T(8,128)(2,1)} %get-tuple-element.59) | data formatting | bytes 4194304 | tf_op jit(solution)/shard_map/while | solution.py:68
  125.6 2.8 %reshape.127 = bf16[4096,4,64,1]{0,2,1,3:T(8,128)(2,1)} reshape(bf16[4,1024,256]{1,0,2:T(4,128)(2,1)S(1)} %copy.101) | data formatting | bytes 4194304 | tf_op jit(solution)/shard_map/dot_general | solution.py:46
  128.4 6.8 %multiply_reduce_fusion = bf16[4096,4,64]{0,2,1:T(8,128)(2,1)S(1)} fusion(f32[4096,8]{0,1:T(8,128)S(1)} %copy-done.2, bf16[8,64,64,1]{2,1,0,3:T(8,128)(2,1)S(1)} %bitcast.137, bf16[4096,4,64,1]{0,2,1,3:T(8,128)(2,1)} %reshape.127), kind=kOutput, calls=%fused_computation.14 | convolution fusion | flops 1089470464 | bytes 4390912 | tf_op jit(solution)/shard_map/dot_general | solution.py:46
  135.2 2.5 %copy.105 = bf16[4096,256]{1,0:T(8,128)(2,1)} copy(bf16[4096,256]{0,1:T(8,128)(2,1)S(1)} %bitcast.131) | data formatting | bytes 4194304
  (77 shorter events, 1.4 us)
Async XLA Ops:
  0.6 84.1 %copy-start = (bf16[6,64,64]{2,1,0:T(8,128)(2,1)S(1)}, bf16[6,64,64]{2,1,0:T(8,128)(2,1)}, u32[]{:S(2)}) copy-start(bf16[6,64,64]{2,1,0:T(8,128)(2,1)} %param.22) | copy-start | bytes 147460
  1.4 3.1 %copy-start.1 = (f32[4096,8]{0,1:T(8,128)}, f32[4096,8]{0,1:T(8,128)S(1)}, u32[]{:S(2)}) copy-start(f32[4096,8]{0,1:T(8,128)S(1)} %fusion.28) | copy-start | bytes 393220
  1.4 3.1 %copy-start.5 = (s32[4096]{0:T(1024)S(1)}, s32[4096]{0:T(1024)}, u32[]{:S(2)}) copy-start(s32[4096]{0:T(1024)} %param.16) | copy-start | bytes 49156
  1.4 3.1 %copy-start.8 = (s32[4096]{0:T(1024)S(1)}, s32[4096]{0:T(1024)}, u32[]{:S(2)}) copy-start(s32[4096]{0:T(1024)} %param.17) | copy-start | bytes 49156
  1.5 3.1 %copy-start.3 = (bf16[8,64,64]{2,1,0:T(8,128)(2,1)S(1)}, bf16[8,64,64]{2,1,0:T(8,128)(2,1)}, u32[]{:S(2)}) copy-start(bf16[8,64,64]{2,1,0:T(8,128)(2,1)} %param.20) | copy-start | bytes 196612
  11.6 33.6 %collective-permute-start.2 = (f32[1,2,32,256]{3,2,1,0:T(8,128)S(1)}, f32[1,2,32,256]{3,2,1,0:T(8,128)S(1)}, u32[]{:S(2)}, u32[]{:S(2)}) collective-permute-start(f32[1,2,32,256]{3,2,1,0:T(8,128)S(1)} %maximum_bitcast_fusion.1), channel_id=1, source_target_pairs={{0,16},{16,32},{32,48},{48,64},{64,80},{80,96},{96,112},{1,17},{17... | collective-permute-start | bytes 196616 | tf_op jit(solution)/shard_map/ppermute | solution.py:19
  13.5 31.6 %collective-permute-start.3 = (f32[1,2,32,256]{3,2,1,0:T(8,128)S(1)}, f32[1,2,32,256]{3,2,1,0:T(8,128)S(1)}, u32[]{:S(2)}, u32[]{:S(2)}) collective-permute-start(f32[1,2,32,256]{3,2,1,0:T(8,128)S(1)} %maximum_bitcast_fusion), channel_id=1, source_target_pairs={{16,0},{32,16},{48,32},{64,48},{80,64},{96,80},{112,96},{17,1},{33... | collective-permute-start | bytes 196616 | tf_op jit(solution)/shard_map/ppermute | solution.py:20
  17.2 27.9 %collective-permute-start.1 = (f32[2,1,32,256]{3,2,1,0:T(8,128)S(1)}, f32[2,1,32,256]{3,2,1,0:T(8,128)S(1)}, u32[]{:S(2)}, u32[]{:S(2)}) collective-permute-start(f32[2,1,32,256]{3,2,1,0:T(8,128)S(1)} %get-tuple-element.107), channel_id=1, source_target_pairs={{1,0},{2,1},{3,2},{4,3},{5,4},{6,5},{7,6},{8,7},{9,8},{10,9},{11,1... | collective-permute-start | bytes 196616 | tf_op jit(solution)/shard_map/ppermute | solution.py:20
  21.7 23.4 %collective-permute-start = (f32[2,1,32,256]{3,2,1,0:T(8,128)S(1)}, f32[2,1,32,256]{3,2,1,0:T(8,128)S(1)}, u32[]{:S(2)}, u32[]{:S(2)}) collective-permute-start(f32[2,1,32,256]{3,2,1,0:T(8,128)S(1)} %get-tuple-element.106), channel_id=1, source_target_pairs={{0,1},{1,2},{2,3},{3,4},{4,5},{5,6},{6,7},{7,8},{8,9},{9,10},{10,1... | collective-permute-start | bytes 196616 | tf_op jit(solution)/shard_map/ppermute | solution.py:19
  23.7 1.9 %copy-start.9 = (s32[4,32]{1,0:T(4,128)S(1)}, s32[4,32]{1,0:T(4,128)}, u32[]{:S(2)}) copy-start(s32[4,32]{1,0:T(4,128)} %param.18) | copy-start | bytes 1540
  46.0 10.1 %copy-start.6 = (s32[6,512]{1,0:T(8,128)S(1)}, s32[6,512]{1,0:T(8,128)}, u32[]{:S(2)}) copy-start(s32[6,512]{1,0:T(8,128)} %param.25) | copy-start | bytes 36868
  46.0 13.0 %copy-start.7 = (s32[6,512]{1,0:T(8,128)S(1)}, s32[6,512]{1,0:T(8,128)}, u32[]{:S(2)}) copy-start(s32[6,512]{1,0:T(8,128)} %param.24) | copy-start | bytes 36868
  46.0 13.0 %copy-start.10 = (f32[16]{0:T(128)S(1)}, f32[16]{0:T(128)}, u32[]{:S(2)}) copy-start(f32[16]{0:T(128)} %param.23) | copy-start | bytes 196
  54.2 13.7 %collective-permute-start.4 = (bf16[1,1,512,256]{2,3,1,0:T(8,128)(2,1)S(1)}, bf16[1,1,512,256]{2,3,1,0:T(8,128)(2,1)S(1)}, u32[]{:S(2)}, u32[]{:S(2)}) collective-permute-start(bf16[1,1,512,256]{2,3,1,0:T(8,128)(2,1)S(1)} %bitcast.125), channel_id=1, source_target_pairs={{0,16},{16,32},{32,48},{48,64},{64,80},{80,96},{96,112},{1,17},{17... | collective-permute-start | bytes 786440 | tf_op jit(solution)/shard_map/ppermute | solution.py:19
  56.2 12.5 %collective-permute-start.5 = (bf16[1,1,512,256]{2,3,1,0:T(8,128)(2,1)S(1)}, bf16[1,1,512,256]{2,3,1,0:T(8,128)(2,1)S(1)}, u32[]{:S(2)}, u32[]{:S(2)}) collective-permute-start(bf16[1,1,512,256]{2,3,1,0:T(8,128)(2,1)S(1)} %bitcast.126), channel_id=1, source_target_pairs={{0,1},{1,2},{2,3},{3,4},{4,5},{5,6},{6,7},{7,8},{8,9},{9,10},{10,1... | collective-permute-start | bytes 786440 | tf_op jit(solution)/shard_map/ppermute | solution.py:19
  59.2 11.4 %collective-permute-start.6 = (bf16[1,1,512,256]{2,3,1,0:T(8,128)(2,1)S(1)}, bf16[1,1,512,256]{2,3,1,0:T(8,128)(2,1)S(1)}, u32[]{:S(2)}, u32[]{:S(2)}) collective-permute-start(bf16[1,1,512,256]{2,3,1,0:T(8,128)(2,1)S(1)} %bitcast.127), channel_id=1, source_target_pairs={{1,0},{2,1},{3,2},{4,3},{5,4},{6,5},{7,6},{8,7},{9,8},{10,9},{11,1... | collective-permute-start | bytes 786440 | tf_op jit(solution)/shard_map/ppermute | solution.py:20
  64.3 7.2 %collective-permute-start.7 = (bf16[1,1,512,256]{2,3,1,0:T(8,128)(2,1)S(1)}, bf16[1,1,512,256]{2,3,1,0:T(8,128)(2,1)S(1)}, u32[]{:S(2)}, u32[]{:S(2)}) collective-permute-start(bf16[1,1,512,256]{2,3,1,0:T(8,128)(2,1)S(1)} %bitcast.128), channel_id=1, source_target_pairs={{16,0},{32,16},{48,32},{64,48},{80,64},{96,80},{112,96},{17,1},{33... | collective-permute-start | bytes 786440 | tf_op jit(solution)/shard_map/ppermute | solution.py:20
  95.7 6.4 %copy-start.4 = (bf16[8,64,64]{2,1,0:T(8,128)(2,1)S(1)}, bf16[8,64,64]{2,1,0:T(8,128)(2,1)}, u32[]{:S(2)}) copy-start(bf16[8,64,64]{2,1,0:T(8,128)(2,1)} %param.20) | copy-start | bytes 196612
  96.5 14.7 %collective-permute-start.9 = (bf16[2,1,32,256]{3,2,1,0:T(8,128)(2,1)S(1)}, bf16[2,1,32,256]{3,2,1,0:T(8,128)(2,1)S(1)}, u32[]{:S(2)}, u32[]{:S(2)}) collective-permute-start(bf16[2,1,32,256]{3,2,1,0:T(8,128)(2,1)S(1)} %get-tuple-element.113), channel_id=1, source_target_pairs={{1,0},{2,1},{3,2},{4,3},{5,4},{6,5},{7,6},{8,7},{9,8},{10,9},{11,1... | collective-permute-start | bytes 98312 | tf_op jit(solution)/shard_map/ppermute | solution.py:20
  102.5 13.5 %collective-permute-start.10 = (bf16[1,2,32,256]{3,2,1,0:T(8,128)(2,1)S(1)}, bf16[1,2,32,256]{3,2,1,0:T(8,128)(2,1)S(1)}, u32[]{:S(2)}, u32[]{:S(2)}) collective-permute-start(bf16[1,2,32,256]{3,2,1,0:T(8,128)(2,1)S(1)} %maximum_bitcast_fusion.3), channel_id=1, source_target_pairs={{0,16},{16,32},{32,48},{48,64},{64,80},{80,96},{96,112},{1,17},{17... | collective-permute-start | bytes 98312 | tf_op jit(solution)/shard_map/ppermute | solution.py:19
  104.4 11.6 %collective-permute-start.11 = (bf16[1,2,32,256]{3,2,1,0:T(8,128)(2,1)S(1)}, bf16[1,2,32,256]{3,2,1,0:T(8,128)(2,1)S(1)}, u32[]{:S(2)}, u32[]{:S(2)}) collective-permute-start(bf16[1,2,32,256]{3,2,1,0:T(8,128)(2,1)S(1)} %maximum_bitcast_fusion.2), channel_id=1, source_target_pairs={{16,0},{32,16},{48,32},{64,48},{80,64},{96,80},{112,96},{17,1},{33... | collective-permute-start | bytes 98312 | tf_op jit(solution)/shard_map/ppermute | solution.py:20
  108.1 7.9 %collective-permute-start.8 = (bf16[2,1,32,256]{3,2,1,0:T(8,128)(2,1)S(1)}, bf16[2,1,32,256]{3,2,1,0:T(8,128)(2,1)S(1)}, u32[]{:S(2)}, u32[]{:S(2)}) collective-permute-start(bf16[2,1,32,256]{3,2,1,0:T(8,128)(2,1)S(1)} %get-tuple-element.112), channel_id=1, source_target_pairs={{0,1},{1,2},{2,3},{3,4},{4,5},{5,6},{6,7},{7,8},{8,9},{9,10},{10,1... | collective-permute-start | bytes 98312 | tf_op jit(solution)/shard_map/ppermute | solution.py:19
  125.6 2.8 %copy-start.2 = (f32[4096,8]{0,1:T(8,128)S(1)}, f32[4096,8]{0,1:T(8,128)}, u32[]{:S(2)}) copy-start(f32[4096,8]{0,1:T(8,128)} %copy-done.1) | copy-start | bytes 393220
where the time goes:
time: 139 us; the launch traced here: 138 us
  matrix products  47.6 us (34%)
  local copies, waits for them, and re-layouts  40.5 us (29%)
  starting transfers between devices  38.7 us (28%)
  waiting for transfers between devices  8.37 us (6%)
    ppermute x6, starting transfers between devices, extended_2(): lax.ppermute(first, axis, [(b, a) for a, b in up])  26 us
    dot_general x8, matrix products, one_block(): jnp.dot(onehot, table, preferred_element_type=jnp.float32)  13.9 us
    unnamed x30, local copies, waits for them, and re-layouts  13.1 us
    reshape x1, local copies, waits for them, and re-layouts, shards(): inverse = inverse_blocks.reshape(coarse_count, order_dim, order_dim)  13 us
    ppermute x6, starting transfers between devices, extended_2(): lax.ppermute(last, axis, up)  12.6 us
    dot_general x2, matrix products, typed_product(): jnp.dot(columns, stacked_table(matrices, flipped), preferred_element_type...  12.3 us
    dot_general x1, matrix products, shards(): jnp.einsum('cij,csj->csi', inverse, coarse_rhs.reshape(coarse_count, rhs_...  7.8 us
    dot_general x1, matrix products, shards(): jnp.einsum('cij,csj->csi', inverse, coupled, preferred_element_type=jnp.f...  7.78 us
  transfers between devices with their start and end apart: 12, of which 4 were waited for; matrix products, arithmetic and copies ran while one was open for 17% of the time, Pallas kernels for 0%

commit v1 on v0

v1 whole, which is shorter than its diff:
```python
import jax
import jax.numpy as jnp
from jax import lax
from jax.experimental import pallas as pl
from jax.experimental.pallas import tpu as pltpu
from jax.sharding import PartitionSpec as P

bf16 = jnp.bfloat16
f32 = jnp.float32
i32 = jnp.int32

OMEGA = 0.5
DOF = 64
RHS = 4
W = 256
NTYPE = 8
FACES = 6
KINDS = 16
GHOST = 32
LANES = 128
CHUNK = 1024


def swap_pairs(n_px, n_py):
    def at(a, b):
        return (a % n_px) * n_py + b % n_py

    perms = []
    for start in (0, 1):
        perm = []
        for b in range(n_py):
            for a in range(start, n_px + start, 2):
                perm += [(at(a, b), at(a + 1, b)), (at(a + 1, b), at(a, b))]
        perms.append(sorted(perm))
    for start in (0, 1):
        perm = []
        for a in range(n_px):
            for b in range(start, n_py + start, 2):
                perm += [(at(a, b), at(a, b + 1)), (at(a, b + 1), at(a, b))]
        perms.append(sorted(perm))
    return perms


def exchange(arrays, perms):
    return [lax.ppermute(x, ("px", "py"), perm) for x, perm in zip(arrays, perms)]


def wide(column):
    return jnp.concatenate([column, column], axis=1)


def block_diagonal(matrix, flipped):
    row = lax.broadcasted_iota(i32, (W, DOF), 0) % DOF
    col = lax.broadcasted_iota(i32, (W, DOF), 1)
    spread = (row == col).astype(f32).astype(bf16)
    dims = (((1,), (1 if flipped else 0,)), ((), ()))
    half = lax.dot_general(spread, matrix, dims, preferred_element_type=f32).astype(bf16)
    full = lax.dot_general(half, spread, (((1,), (1,)), ((), ())), preferred_element_type=f32)
    r = lax.broadcasted_iota(i32, (W, W), 0) // DOF
    c = lax.broadcasted_iota(i32, (W, W), 1) // DOF
    return jnp.where(r == c, full, 0.0).astype(bf16)


def targets(where_ref, dest, slot, coarse_count):
    own = where_ref[0]
    even_x = where_ref[1]
    even_y = where_ref[2]
    off = dest - own
    q_px = jnp.where((off > 0) == (even_x == 1), 0, 1)
    q_py = jnp.where((off > 0) == (even_y == 1), 2, 3)
    q = jnp.where((off == 1) | (off == -1), q_py, q_px)
    return jnp.where(off == 0, slot, coarse_count + q * GHOST + slot)


def columns(rows):
    flipped = rows.T
    return [jnp.broadcast_to(flipped[:, r : r + 1], (LANES, LANES)) for r in range(rows.shape[0])]


def typed(x_rows, type_column, table):
    kinds = wide(type_column.astype(f32).astype(bf16))
    parts = [jnp.where(kinds == float(t), x_rows, jnp.zeros((), bf16)) for t in range(NTYPE)]
    return jnp.dot(jnp.concatenate(parts, axis=1), table, preferred_element_type=f32)


def restrict_kernel(where_ref, x_ref, dest_ref, slot_ref, type_ref, table_ref, local_ref, g0, g1, g2, g3, w_ref, contrib_ref, acc_ref):
    step = pl.program_id(0)
    rows_out = acc_ref.shape[0]
    coarse_count = rows_out - 4 * GHOST

    @pl.when(step == 0)
    def _():
        for t in range(NTYPE):
            w_ref[t * W : (t + 1) * W, :] = block_diagonal(table_ref[t], True)
        acc_ref[...] = jnp.zeros_like(acc_ref)

    table = w_ref[...]
    kinds = columns(type_ref[...])
    for r in range(CHUNK // LANES):
        rows = slice(r * LANES, (r + 1) * LANES)
        contrib_ref[rows, :] = typed(x_ref[rows, :], kinds[r], table).astype(bf16)
    target = targets(where_ref, dest_ref[...], slot_ref[...], coarse_count)
    row_id = lax.broadcasted_iota(i32, (rows_out, LANES), 0)
    hits = [
        (row_id == jnp.broadcast_to(target[r : r + 1, :], (rows_out, LANES))).astype(f32).astype(bf16)
        for r in range(CHUNK // LANES)
    ]
    acc_ref[...] += jnp.dot(jnp.concatenate(hits, axis=1), contrib_ref[...], preferred_element_type=f32)

    @pl.when(step == pl.num_programs(0) - 1)
    def _():
        local_ref[...] = acc_ref[:coarse_count, :]
        for q, out in enumerate((g0, g1, g2, g3)):
            first = coarse_count + q * GHOST
            out[...] = acc_ref[first : first + GHOST, :].astype(bf16)


def apply_blocks(inv_ref, v):
    count = v.shape[0]
    lane = lax.broadcasted_iota(i32, (count, LANES), 1)
    outs = []
    row = lax.broadcasted_iota(i32, (W, DOF), 0)
    col = lax.broadcasted_iota(i32, (W, DOF), 1)
    doubled = []
    for s in range(RHS):
        tile = v[:, (s // 2) * LANES : (s // 2 + 1) * LANES].astype(f32)
        turned = pltpu.roll(tile, DOF, 1)
        low, high = (tile, turned) if s % 2 == 0 else (turned, tile)
        doubled.append(wide(jnp.where(lane < DOF, low, high).astype(bf16)))
    acc = [jnp.zeros((count, DOF), f32) for _ in range(RHS)]
    for k in range(DOF * DOF // W):
        summing = (col == row // DOF + k * (W // DOF)).astype(f32).astype(bf16)
        block = inv_ref[:, k * W : (k + 1) * W]
        for s in range(RHS):
            acc[s] = acc[s] + jnp.dot(block * doubled[s], summing, preferred_element_type=f32)
    return jnp.concatenate(acc, axis=1)


def sweep_kernel(local_ref, i0, i1, i2, i3, slots_ref, inv_ref, out_ref):
    count = local_ref.shape[0]
    row_id = lax.broadcasted_iota(i32, (count, LANES), 0)
    hits = (row_id == jnp.broadcast_to(slots_ref[0:1, :], (count, LANES))).astype(f32).astype(bf16)
    incoming = jnp.concatenate([i0[...], i1[...], i2[...], i3[...]], axis=0)
    rhs = local_ref[...] + jnp.dot(hits, incoming, preferred_element_type=f32)
    out_ref[...] = apply_blocks(inv_ref, rhs.astype(bf16)).astype(bf16)


def couple_kernel(
    where_ref, fs_ref, h0, h1, h2, h3, nb_ref, ci_ref, coef_ref, face_ref, slots_ref, inv_ref,
    sol_ref, ans_ref, r0, r1, r2, r3,
):
    count = fs_ref.shape[0]
    own = where_ref[0]
    even_x = where_ref[1]
    even_y = where_ref[2]
    nb = nb_ref[...]
    off = nb // count - own
    q_px = jnp.where((off > 0) == (even_x == 1), 1, 2)
    q_py = jnp.where((off > 0) == (even_y == 1), 3, 4)
    block = jnp.where(off == 0, 0, jnp.where((off == 1) | (off == -1), q_py, q_px))
    index = block * count + nb % count
    scale = jnp.zeros(nb.shape, f32)
    for k in range(KINDS):
        scale = jnp.where(ci_ref[...] == k, coef_ref[k], scale)
    index_t = index.T
    scale_t = scale.T
    sources = [fs_ref, h0, h1, h2, h3]
    lane = lax.broadcasted_iota(i32, (count, W), 1)
    coupled = jnp.zeros((count, W), f32)
    for f in range(FACES):
        column = jnp.broadcast_to(index_t[:, f : f + 1], (count, LANES))
        column = wide(column)
        acc = jnp.zeros((count, W), f32)
        for b in range(5):
            for h in range(count // W):
                hit = (lane + (b * count + h * W) == column).astype(f32).astype(bf16)
                acc = acc + jnp.dot(hit, sources[b][h * W : (h + 1) * W, :], preferred_element_type=f32)
        term = jnp.dot(acc.astype(bf16), block_diagonal(face_ref[f], True), preferred_element_type=f32)
        coupled = coupled + term * wide(jnp.broadcast_to(scale_t[:, f : f + 1], (count, LANES)))
    correction = apply_blocks(inv_ref, coupled.astype(bf16))
    solution_rows = fs_ref[...].astype(f32) - OMEGA * correction
    sol_ref[...] = solution_rows
    answer = solution_rows.astype(bf16)
    ans_ref[...] = answer
    row_id = lax.broadcasted_iota(i32, (count, LANES), 0)
    hits = (row_id == jnp.broadcast_to(slots_ref[0:1, :], (count, LANES))).astype(f32).astype(bf16)
    replies = lax.dot_general(hits, answer, (((0,), (0,)), ((), ())), preferred_element_type=f32).astype(bf16)
    for q, out in enumerate((r0, r1, r2, r3)):
        out[...] = replies[q * GHOST : (q + 1) * GHOST, :]


def prolong_kernel(where_ref, ans_ref, r0, r1, r2, r3, dest_ref, slot_ref, type_ref, table_ref, out_ref, w_ref, t_ref):
    step = pl.program_id(0)
    rows_in = t_ref.shape[0]
    coarse_count = rows_in - 4 * GHOST

    @pl.when(step == 0)
    def _():
        for t in range(NTYPE):
            w_ref[t * W : (t + 1) * W, :] = block_diagonal(table_ref[t], False)
        t_ref[:coarse_count, :] = ans_ref[...]
        for q, r in enumerate((r0, r1, r2, r3)):
            first = coarse_count + q * GHOST
            t_ref[first : first + GHOST, :] = r[...]

    table = w_ref[...]
    source = t_ref[...]
    kinds = columns(type_ref[...])
    target = columns(targets(where_ref, dest_ref[...], slot_ref[...], coarse_count))
    lane = lax.broadcasted_iota(i32, (LANES, LANES), 1)
    for r in range(CHUNK // LANES):
        hits = [
            (lane + k * LANES == target[r]).astype(f32).astype(bf16) for k in range(rows_in // LANES)
        ]
        fetched = jnp.dot(jnp.concatenate(hits, axis=1), source, preferred_element_type=f32).astype(bf16)
        out_ref[r * LANES : (r + 1) * LANES, :] = typed(fetched, kinds[r], table).astype(bf16)


def whole(shape):
    return pl.BlockSpec(shape, lambda *_: (0,) * len(shape))


def shards(
    fine_residual, dest_owner, coarse_slot, ghost_slot, child_type, restrict_table, inverse_blocks,
    face_table, face_coef, coef_index, neighbours,
):
    fine_count = fine_residual.shape[0]
    count = inverse_blocks.shape[0]
    n_px, n_py = lax.axis_size("px"), lax.axis_size("py")
    a, b = lax.axis_index("px"), lax.axis_index("py")
    even_x, even_y = 1 - a % 2, 1 - b % 2
    where = jnp.stack([a * n_py + b, even_x, even_y]).astype(i32)
    perms = swap_pairs(n_px, n_py)
    lists = jnp.stack([
        jnp.where(even_x == 1, ghost_slot[3], ghost_slot[2]),
        jnp.where(even_x == 1, ghost_slot[2], ghost_slot[3]),
        jnp.where(even_y == 1, ghost_slot[1], ghost_slot[0]),
        jnp.where(even_y == 1, ghost_slot[0], ghost_slot[1]),
    ]).reshape(1, 4 * GHOST)
    meta = [m.reshape(fine_count // LANES, LANES) for m in (dest_owner, coarse_slot, child_type)]
    steps = fine_count // CHUNK
    smem = pl.BlockSpec(memory_space=pltpu.SMEM)
    meta_spec = pl.BlockSpec((CHUNK // LANES, LANES), lambda i: (i, 0))
    ghost_shape = [jax.ShapeDtypeStruct((GHOST, W), bf16)] * 4
    ghost_spec = [whole((GHOST, W))] * 4
    rows = count + 4 * GHOST

    local, *outgoing = pl.pallas_call(
        restrict_kernel,
        grid=(steps,),
        in_specs=[smem, pl.BlockSpec((CHUNK, W), lambda i: (i, 0)), meta_spec, meta_spec, meta_spec, whole(restrict_table.shape)],
        out_specs=[whole((count, W))] + ghost_spec,
        out_shape=[jax.ShapeDtypeStruct((count, W), f32)] + ghost_shape,
        scratch_shapes=[pltpu.VMEM((NTYPE * W, W), bf16), pltpu.VMEM((CHUNK, W), bf16), pltpu.VMEM((rows, W), f32)],
        name="restrict",
    )(where, fine_residual, *meta, restrict_table)
    incoming = exchange(outgoing, perms)
    first_sweep = pl.pallas_call(
        sweep_kernel,
        out_shape=jax.ShapeDtypeStruct((count, W), bf16),
        name="sweep",
    )(local, *incoming, lists, inverse_blocks)
    halo = exchange([first_sweep] * 4, perms)
    coarse_solution, answer, *replies = pl.pallas_call(
        couple_kernel,
        in_specs=[smem] + [pl.BlockSpec()] * 7 + [smem] + [pl.BlockSpec()] * 3,
        out_shape=[jax.ShapeDtypeStruct((count, W), f32), jax.ShapeDtypeStruct((count, W), bf16)] + ghost_shape,
        name="couple",
    )(where, first_sweep, *halo, neighbours, coef_index, face_coef, face_table, lists, inverse_blocks)
    returned = exchange(replies, perms)
    fine_correction = pl.pallas_call(
        prolong_kernel,
        grid=(steps,),
        in_specs=[smem, whole((count, W))] + ghost_spec + [meta_spec, meta_spec, meta_spec, whole(restrict_table.shape)],
        out_specs=pl.BlockSpec((CHUNK, W), lambda i: (i, 0)),
        out_shape=jax.ShapeDtypeStruct((fine_count, W), bf16),
        scratch_shapes=[pltpu.VMEM((NTYPE * W, W), bf16), pltpu.VMEM((rows, W), bf16)],
        name="prolong",
    )(where, answer, *returned, *meta, restrict_table)
    return (coarse_solution, fine_correction)


def solution(mesh):
    both = ("px", "py")
    in_specs = (
        P(both, None), P(both), P(both), P(both, None), P(both), P(), P(both, None), P(), P(), P(None, both), P(None, both),
    )
    out_specs = (P(both, None), P(both, None))
    return jax.shard_map(shards, mesh=mesh, in_specs=in_specs, out_specs=out_specs, check_vma=False)
```

time: 139 us -> 86.2 us (0.62)
  the two profiles are of different devices: /device:TPU:112 before, /device:TPU:8 now
where the time goes in v1:
time: 86.2 us; the launch traced here: 86 us
  Pallas kernels  47.4 us (55%)
  starting transfers between devices  19.6 us (23%)
  waiting for transfers between devices  14.3 us (17%)
  local copies, waits for them, and re-layouts  3.35 us (4%)
    ppermute x12, starting transfers between devices, exchange(): lax.ppermute(x, ('px', 'py'), perm)  19.6 us
    pallas_call x1, Pallas kernels, shards(): pl.pallas_call(couple_kernel, in_specs=[smem] + [pl.BlockSpec()] * 7 + [s...  17.6 us
    ppermute x12, waiting for transfers between devices, exchange(): lax.ppermute(x, ('px', 'py'), perm)  14.3 us
    pallas_call x1, Pallas kernels, shards(): pl.pallas_call(prolong_kernel, grid=(steps,), in_specs=[smem, whole((coun...  11.9 us
    pallas_call x1, Pallas kernels, shards(): pl.pallas_call(restrict_kernel, grid=(steps,), in_specs=[smem, pl.BlockSp...  10 us
    pallas_call x1, Pallas kernels, shards(): pl.pallas_call(sweep_kernel, out_shape=jax.ShapeDtypeStruct((count, W), b...  7.88 us
    unnamed x26, local copies, waits for them, and re-layouts  2.68 us
  transfers between devices with their start and end apart: 12, of which 5 were waited for; matrix products, arithmetic and copies ran while one was open for 1% of the time, Pallas kernels for 0%

profile of v1, /device:TPU:8, one launch (start us, length us, event | category | flops | bytes accessed | tf_op | source)
XLA Modules:
  0.0 86.0 jit_solution(5468166824635234599)
XLA Ops:
  0.6 0.0 copy-start.12
  0.7 0.6 pad_add_fusion.1.where_ref
  1.3 10.0 %restrict.1 = (f32[512,256]{1,0:T(8,128)}, bf16[32,256]{1,0:T(8,128)(2,1)}, bf16[32,256]{1,0:T(8,128)(2,1)}, bf16[32,256]{1,0:T(8,128)(2,1)}, bf16[32,256]{1,0:T(8,128)(2,1)}) custom-call(s32[3]{0:T(128)} %pad_add_fusion.1.where_ref, bf16[4096,256]{1,0:T(8,128)(2,1)} %x_ref.1, s32[32,128]{1,0:T(8,128)} %bitcast.6, s32[32,128]{1,0:T(8,128)} %bitcast.8, ...), custom_call_target="tpu_custom_call" | custom-call | tf_op jit(solution)/shard_map/restrict/pallas_call | solution.py:248
  11.3 0.1 collective-permute-start
  11.4 0.4 collective-permute-start.1
  11.8 1.6 %collective-permute-start.2 = (bf16[32,256]{1,0:T(8,128)(2,1)}, bf16[32,256]{1,0:T(8,128)(2,1)S(1)}, u32[]{:S(2)}, u32[]{:S(2)}) collective-permute-start(bf16[32,256]{1,0:T(8,128)(2,1)} %get-tuple-element.16), channel_id=1, source_target_pairs={{0,1},{1,0},{2,3},{3,2},{4,5},{5,4},{6,7},{7,6},{8,9},{9,8},{10,11... | collective-permute-start | bytes 49160 | tf_op jit(solution)/shard_map/ppermute | solution.py:45
  13.4 5.6 %collective-permute-start.3 = (bf16[32,256]{1,0:T(8,128)(2,1)}, bf16[32,256]{1,0:T(8,128)(2,1)S(1)}, u32[]{:S(2)}, u32[]{:S(2)}) collective-permute-start(bf16[32,256]{1,0:T(8,128)(2,1)} %get-tuple-element.17), channel_id=1, source_target_pairs={{0,15},{1,2},{2,1},{3,4},{4,3},{5,6},{6,5},{7,8},{8,7},{9,10},{10,... | collective-permute-start | bytes 49160 | tf_op jit(solution)/shard_map/ppermute | solution.py:45
  19.0 0.0 copy-done.12
  19.0 0.7 reshape.19.slots_ref
  19.7 0.0 collective-permute-done.i0
  19.7 0.0 copy-start.4
  19.7 0.0 collective-permute-done.1.i1
  19.7 0.0 copy-start.5
  19.7 0.0 collective-permute-done.2.i2
  19.7 0.0 copy-start.6
  19.7 1.2 %collective-permute-done.3.i3 = bf16[32,256]{1,0:T(8,128)(2,1)S(1)} collective-permute-done((bf16[32,256]{1,0:T(8,128)(2,1)}, bf16[32,256]{1,0:T(8,128)(2,1)S(1)}, u32[]{:S(2)}, u32[]{:S(2)}) %collective-permute-start.3) | collective-permute-done | bytes 16416 | tf_op jit(solution)/shard_map/ppermute | solution.py:45
  20.9 0.0 copy-done.4
  20.9 0.0 copy-done.5
  20.9 0.0 copy-done.6
  20.9 0.6 copy-done.7
  21.5 7.9 %sweep.1.fs_ref = bf16[512,256]{1,0:T(8,128)(2,1)} custom-call(f32[512,256]{1,0:T(8,128)} %get-tuple-element.13.local_ref, bf16[32,256]{1,0:T(8,128)(2,1)} %copy-done.4, bf16[32,256]{1,0:T(8,128)(2,1)} %copy-done.5, bf16[32,256]{1,0:T(8,128)(2,1)} %copy-done.6, bf16[32,256]{1,0:T(8,128)(2,1)} %copy-done.7, s32[1,128]{1,0:T(1,128)} %reshape.19.slots_ref, ...), custom_call_target="tpu_custom_call" | custom-call | tf_op jit(solution)/shard_map/sweep/pallas_call | solution.py:258
  29.4 5.5 %collective-permute-start.7 = (bf16[512,256]{1,0:T(8,128)(2,1)}, bf16[512,256]{1,0:T(8,128)(2,1)S(1)}, u32[]{:S(2)}, u32[]{:S(2)}) collective-permute-start(bf16[512,256]{1,0:T(8,128)(2,1)} %sweep.1.fs_ref), channel_id=1, source_target_pairs={{0,15},{1,2},{2,1},{3,4},{4,3},{5,6},{6,5},{7,8},{8,7},{9,10},{10,... | collective-permute-start | bytes 786440 | tf_op jit(solution)/shard_map/ppermute | solution.py:45
  34.9 0.0 collective-permute-start.6
  34.9 0.0 collective-permute-start.5
  34.9 1.5 %collective-permute-start.4 = (bf16[512,256]{1,0:T(8,128)(2,1)}, bf16[512,256]{1,0:T(8,128)(2,1)S(1)}, u32[]{:S(2)}, u32[]{:S(2)}) collective-permute-start(bf16[512,256]{1,0:T(8,128)(2,1)} %sweep.1.fs_ref), channel_id=1, source_target_pairs={{0,16},{1,17},{2,18},{3,19},{4,20},{5,21},{6,22},{7,23},{8,24},{9,... | collective-permute-start | bytes 786440 | tf_op jit(solution)/shard_map/ppermute | solution.py:45
  36.4 5.2 %collective-permute-done.7.h3 = bf16[512,256]{1,0:T(8,128)(2,1)S(1)} collective-permute-done((bf16[512,256]{1,0:T(8,128)(2,1)}, bf16[512,256]{1,0:T(8,128)(2,1)S(1)}, u32[]{:S(2)}, u32[]{:S(2)}) %collective-permute-start.7) | collective-permute-done | bytes 262176 | tf_op jit(solution)/shard_map/ppermute | solution.py:45
  41.6 1.5 %collective-permute-done.6.h2 = bf16[512,256]{1,0:T(8,128)(2,1)S(1)} collective-permute-done((bf16[512,256]{1,0:T(8,128)(2,1)}, bf16[512,256]{1,0:T(8,128)(2,1)S(1)}, u32[]{:S(2)}, u32[]{:S(2)}) %collective-permute-start.6) | collective-permute-done | bytes 262176 | tf_op jit(solution)/shard_map/ppermute | solution.py:45
  43.1 0.0 collective-permute-done.5.h1
  43.1 0.0 collective-permute-done.4.h0
  43.1 0.0 copy-done
  43.1 0.7 copy-done.1
  43.8 0.1 copy-done.2
  43.9 0.7 copy-done.3
  44.6 17.6 %couple.1 = (f32[512,256]{1,0:T(8,128)}, bf16[512,256]{1,0:T(8,128)(2,1)}, bf16[32,256]{1,0:T(8,128)(2,1)}, bf16[32,256]{1,0:T(8,128)(2,1)}, bf16[32,256]{1,0:T(8,128)(2,1)}, /*index=5*/bf16[32,256]{1,0:T(8,128)(2,1)}) custom-call(s32[3]{0:T(128)} %pad_add_fusion.1.where_ref, bf16[512,256]{1,0:T(8,128)(2,1)} %sweep.1.fs_ref, bf16[512,256]{1,0:T(8,128)(2,1)} %copy-done.3, ...), custom_call_target="tpu_custom_call" | custom-call | tf_op jit(solution)/shard_map/couple/pallas_call | solution.py:264
  62.2 0.1 collective-permute-start.8
  62.3 1.9 %collective-permute-start.9 = (bf16[32,256]{1,0:T(8,128)(2,1)}, bf16[32,256]{1,0:T(8,128)(2,1)S(1)}, u32[]{:S(2)}, u32[]{:S(2)}) collective-permute-start(bf16[32,256]{1,0:T(8,128)(2,1)} %get-tuple-element.21), channel_id=1, source_target_pairs={{0,112},{1,113},{2,114},{3,115},{4,116},{5,117},{6,118},{7,119},{8... | collective-permute-start | bytes 49160 | tf_op jit(solution)/shard_map/ppermute | solution.py:45
  64.2 2.0 %collective-permute-start.10 = (bf16[32,256]{1,0:T(8,128)(2,1)}, bf16[32,256]{1,0:T(8,128)(2,1)S(1)}, u32[]{:S(2)}, u32[]{:S(2)}) collective-permute-start(bf16[32,256]{1,0:T(8,128)(2,1)} %get-tuple-element.22), channel_id=1, source_target_pairs={{0,1},{1,0},{2,3},{3,2},{4,5},{5,4},{6,7},{7,6},{8,9},{9,8},{10,11... | collective-permute-start | bytes 49160 | tf_op jit(solution)/shard_map/ppermute | solution.py:45
  66.2 0.8 collective-permute-start.11
  67.1 0.0 collective-permute-done.8.r0
  67.1 0.0 collective-permute-done.9.r1
  67.1 0.0 copy-start.9
  67.1 1.1 %collective-permute-done.10.r2 = bf16[32,256]{1,0:T(8,128)(2,1)S(1)} collective-permute-done((bf16[32,256]{1,0:T(8,128)(2,1)}, bf16[32,256]{1,0:T(8,128)(2,1)S(1)}, u32[]{:S(2)}, u32[]{:S(2)}) %collective-permute-start.10) | collective-permute-done | bytes 16416 | tf_op jit(solution)/shard_map/ppermute | solution.py:45
  68.2 5.3 %collective-permute-done.11.r3 = bf16[32,256]{1,0:T(8,128)(2,1)S(1)} collective-permute-done((bf16[32,256]{1,0:T(8,128)(2,1)}, bf16[32,256]{1,0:T(8,128)(2,1)S(1)}, u32[]{:S(2)}, u32[]{:S(2)}) %collective-permute-start.11) | collective-permute-done | bytes 16416 | tf_op jit(solution)/shard_map/ppermute | solution.py:45
  73.5 0.0 copy-done.8
  73.5 0.0 copy-done.9
  73.5 0.0 copy-done.10
  73.5 0.6 copy-done.11
  74.1 11.9 %prolong.1 = bf16[4096,256]{1,0:T(8,128)(2,1)} custom-call(s32[3]{0:T(128)} %pad_add_fusion.1.where_ref, bf16[512,256]{1,0:T(8,128)(2,1)} %get-tuple-element.19.ans_ref, bf16[32,256]{1,0:T(8,128)(2,1)} %copy-done.8, bf16[32,256]{1,0:T(8,128)(2,1)} %copy-done.9, bf16[32,256]{1,0:T(8,128)(2,1)} %copy-done.10, bf16[32,256]{1,0:T(8,128)(2,1)} %copy-done.11, ...), custom_call_target="tpu_custom_call" | custom-call | tf_op jit(solution)/shard_map/prolong/pallas_call | solution.py:271
  (10 shorter events, 0.0 us)
Async XLA Ops:
  0.6 18.3 %copy-start.12 = (s32[4,32]{1,0:T(4,128)S(1)}, s32[4,32]{1,0:T(4,128)}, u32[]{:S(2)}) copy-start(s32[4,32]{1,0:T(4,128)} %param.14) | copy-start | bytes 1540
  11.3 8.4 %collective-permute-start = (bf16[32,256]{1,0:T(8,128)(2,1)}, bf16[32,256]{1,0:T(8,128)(2,1)S(1)}, u32[]{:S(2)}, u32[]{:S(2)}) collective-permute-start(bf16[32,256]{1,0:T(8,128)(2,1)} %get-tuple-element.14), channel_id=1, source_target_pairs={{0,16},{1,17},{2,18},{3,19},{4,20},{5,21},{6,22},{7,23},{8,24},{9,... | collective-permute-start | bytes 49160 | tf_op jit(solution)/shard_map/ppermute | solution.py:45
  11.4 8.3 %collective-permute-start.1 = (bf16[32,256]{1,0:T(8,128)(2,1)}, bf16[32,256]{1,0:T(8,128)(2,1)S(1)}, u32[]{:S(2)}, u32[]{:S(2)}) collective-permute-start(bf16[32,256]{1,0:T(8,128)(2,1)} %get-tuple-element.15), channel_id=1, source_target_pairs={{0,112},{1,113},{2,114},{3,115},{4,116},{5,117},{6,118},{7,119},{8... | collective-permute-start | bytes 49160 | tf_op jit(solution)/shard_map/ppermute | solution.py:45
  11.8 7.9 %collective-permute-start.2 = (bf16[32,256]{1,0:T(8,128)(2,1)}, bf16[32,256]{1,0:T(8,128)(2,1)S(1)}, u32[]{:S(2)}, u32[]{:S(2)}) collective-permute-start(bf16[32,256]{1,0:T(8,128)(2,1)} %get-tuple-element.16), channel_id=1, source_target_pairs={{0,1},{1,0},{2,3},{3,2},{4,5},{5,4},{6,7},{7,6},{8,9},{9,8},{10,11... | collective-permute-start | bytes 49160 | tf_op jit(solution)/shard_map/ppermute | solution.py:45
  13.4 7.5 %collective-permute-start.3 = (bf16[32,256]{1,0:T(8,128)(2,1)}, bf16[32,256]{1,0:T(8,128)(2,1)S(1)}, u32[]{:S(2)}, u32[]{:S(2)}) collective-permute-start(bf16[32,256]{1,0:T(8,128)(2,1)} %get-tuple-element.17), channel_id=1, source_target_pairs={{0,15},{1,2},{2,1},{3,4},{4,3},{5,6},{6,5},{7,8},{8,7},{9,10},{10,... | collective-permute-start | bytes 49160 | tf_op jit(solution)/shard_map/ppermute | solution.py:45
  19.7 1.2 %copy-start.4 = (bf16[32,256]{1,0:T(8,128)(2,1)}, bf16[32,256]{1,0:T(8,128)(2,1)S(1)}, u32[]{:S(2)}) copy-start(bf16[32,256]{1,0:T(8,128)(2,1)S(1)} %collective-permute-done.i0) | copy-start | bytes 49156
  19.7 1.2 %copy-start.5 = (bf16[32,256]{1,0:T(8,128)(2,1)}, bf16[32,256]{1,0:T(8,128)(2,1)S(1)}, u32[]{:S(2)}) copy-start(bf16[32,256]{1,0:T(8,128)(2,1)S(1)} %collective-permute-done.1.i1) | copy-start | bytes 49156
  19.7 1.2 %copy-start.6 = (bf16[32,256]{1,0:T(8,128)(2,1)}, bf16[32,256]{1,0:T(8,128)(2,1)S(1)}, u32[]{:S(2)}) copy-start(bf16[32,256]{1,0:T(8,128)(2,1)S(1)} %collective-permute-done.2.i2) | copy-start | bytes 49156
  20.9 0.6 copy-start.7
  29.4 12.3 %collective-permute-start.7 = (bf16[512,256]{1,0:T(8,128)(2,1)}, bf16[512,256]{1,0:T(8,128)(2,1)S(1)}, u32[]{:S(2)}, u32[]{:S(2)}) collective-permute-start(bf16[512,256]{1,0:T(8,128)(2,1)} %sweep.1.fs_ref), channel_id=1, source_target_pairs={{0,15},{1,2},{2,1},{3,4},{4,3},{5,6},{6,5},{7,8},{8,7},{9,10},{10,... | collective-permute-start | bytes 786440 | tf_op jit(solution)/shard_map/ppermute | solution.py:45
  34.9 8.2 %collective-permute-start.6 = (bf16[512,256]{1,0:T(8,128)(2,1)}, bf16[512,256]{1,0:T(8,128)(2,1)S(1)}, u32[]{:S(2)}, u32[]{:S(2)}) collective-permute-start(bf16[512,256]{1,0:T(8,128)(2,1)} %sweep.1.fs_ref), channel_id=1, source_target_pairs={{0,1},{1,0},{2,3},{3,2},{4,5},{5,4},{6,7},{7,6},{8,9},{9,8},{10,11... | collective-permute-start | bytes 786440 | tf_op jit(solution)/shard_map/ppermute | solution.py:45
  34.9 8.2 %collective-permute-start.5 = (bf16[512,256]{1,0:T(8,128)(2,1)}, bf16[512,256]{1,0:T(8,128)(2,1)S(1)}, u32[]{:S(2)}, u32[]{:S(2)}) collective-permute-start(bf16[512,256]{1,0:T(8,128)(2,1)} %sweep.1.fs_ref), channel_id=1, source_target_pairs={{0,112},{1,113},{2,114},{3,115},{4,116},{5,117},{6,118},{7,119},{8... | collective-permute-start | bytes 786440 | tf_op jit(solution)/shard_map/ppermute | solution.py:45
  34.9 8.2 %collective-permute-start.4 = (bf16[512,256]{1,0:T(8,128)(2,1)}, bf16[512,256]{1,0:T(8,128)(2,1)S(1)}, u32[]{:S(2)}, u32[]{:S(2)}) collective-permute-start(bf16[512,256]{1,0:T(8,128)(2,1)} %sweep.1.fs_ref), channel_id=1, source_target_pairs={{0,16},{1,17},{2,18},{3,19},{4,20},{5,21},{6,22},{7,23},{8,24},{9,... | collective-permute-start | bytes 786440 | tf_op jit(solution)/shard_map/ppermute | solution.py:45
  41.6 1.5 %copy-start = (bf16[512,256]{1,0:T(8,128)(2,1)}, bf16[512,256]{1,0:T(8,128)(2,1)S(1)}, u32[]{:S(2)}) copy-start(bf16[512,256]{1,0:T(8,128)(2,1)S(1)} %collective-permute-done.7.h3) | copy-start | bytes 786436
  43.1 0.7 copy-start.1
  43.1 0.8 copy-start.2
  43.9 0.7 copy-start.3
  62.2 4.8 %collective-permute-start.8 = (bf16[32,256]{1,0:T(8,128)(2,1)}, bf16[32,256]{1,0:T(8,128)(2,1)S(1)}, u32[]{:S(2)}, u32[]{:S(2)}) collective-permute-start(bf16[32,256]{1,0:T(8,128)(2,1)} %get-tuple-element.20), channel_id=1, source_target_pairs={{0,16},{1,17},{2,18},{3,19},{4,20},{5,21},{6,22},{7,23},{8,24},{9,... | collective-permute-start | bytes 49160 | tf_op jit(solution)/shard_map/ppermute | solution.py:45
  62.3 4.7 %collective-permute-start.9 = (bf16[32,256]{1,0:T(8,128)(2,1)}, bf16[32,256]{1,0:T(8,128)(2,1)S(1)}, u32[]{:S(2)}, u32[]{:S(2)}) collective-permute-start(bf16[32,256]{1,0:T(8,128)(2,1)} %get-tuple-element.21), channel_id=1, source_target_pairs={{0,112},{1,113},{2,114},{3,115},{4,116},{5,117},{6,118},{7,119},{8... | collective-permute-start | bytes 49160 | tf_op jit(solution)/shard_map/ppermute | solution.py:45
  64.2 3.9 %collective-permute-start.10 = (bf16[32,256]{1,0:T(8,128)(2,1)}, bf16[32,256]{1,0:T(8,128)(2,1)S(1)}, u32[]{:S(2)}, u32[]{:S(2)}) collective-permute-start(bf16[32,256]{1,0:T(8,128)(2,1)} %get-tuple-element.22), channel_id=1, source_target_pairs={{0,1},{1,0},{2,3},{3,2},{4,5},{5,4},{6,7},{7,6},{8,9},{9,8},{10,11... | collective-permute-start | bytes 49160 | tf_op jit(solution)/shard_map/ppermute | solution.py:45
  66.2 7.3 %collective-permute-start.11 = (bf16[32,256]{1,0:T(8,128)(2,1)}, bf16[32,256]{1,0:T(8,128)(2,1)S(1)}, u32[]{:S(2)}, u32[]{:S(2)}) collective-permute-start(bf16[32,256]{1,0:T(8,128)(2,1)} %get-tuple-element.23), channel_id=1, source_target_pairs={{0,15},{1,2},{2,1},{3,4},{4,3},{5,6},{6,5},{7,8},{8,7},{9,10},{10,... | collective-permute-start | bytes 49160 | tf_op jit(solution)/shard_map/ppermute | solution.py:45
  67.1 6.4 %copy-start.8 = (bf16[32,256]{1,0:T(8,128)(2,1)}, bf16[32,256]{1,0:T(8,128)(2,1)S(1)}, u32[]{:S(2)}) copy-start(bf16[32,256]{1,0:T(8,128)(2,1)S(1)} %collective-permute-done.8.r0) | copy-start | bytes 49156
  67.1 6.4 %copy-start.9 = (bf16[32,256]{1,0:T(8,128)(2,1)}, bf16[32,256]{1,0:T(8,128)(2,1)S(1)}, u32[]{:S(2)}) copy-start(bf16[32,256]{1,0:T(8,128)(2,1)S(1)} %collective-permute-done.9.r1) | copy-start | bytes 49156
  68.2 5.4 %copy-start.10 = (bf16[32,256]{1,0:T(8,128)(2,1)}, bf16[32,256]{1,0:T(8,128)(2,1)S(1)}, u32[]{:S(2)}) copy-start(bf16[32,256]{1,0:T(8,128)(2,1)S(1)} %collective-permute-done.10.r2) | copy-start | bytes 49156
  73.5 0.6 copy-start.11

commit v2 on v1

v2 whole, which is shorter than its diff:
```python
import jax
import jax.numpy as jnp
from jax import lax
from jax.experimental import pallas as pl
from jax.experimental.pallas import tpu as pltpu
from jax.sharding import PartitionSpec as P


bf16 = jnp.bfloat16
f32 = jnp.float32
i32 = jnp.int32
i16 = jnp.int16

OMEGA = 0.5
DOF = 64
RHS = 4
W = 256
NTYPE = 8
FACES = 6
KINDS = 16
GHOST = 32
LANES = 128
CHUNK = 1024


def swap_pairs(n_px, n_py):
    def at(a, b):
        return (a % n_px) * n_py + b % n_py

    perms = []
    for start in (0, 1):
        perm = []
        for b in range(n_py):
            for a in range(start, n_px + start, 2):
                perm += [(at(a, b), at(a + 1, b)), (at(a + 1, b), at(a, b))]
        perms.append(sorted(perm))
    for start in (0, 1):
        perm = []
        for a in range(n_px):
            for b in range(start, n_py + start, 2):
                perm += [(at(a, b), at(a, b + 1)), (at(a, b + 1), at(a, b))]
        perms.append(sorted(perm))
    return perms


def exchange(arrays, perms):
    moved = []
    for x, perm in zip(arrays, perms):
        moved.append(pltpu.with_memory_space_constraint(lax.ppermute(x, ("px", "py"), perm), pltpu.VMEM))
    return moved


def wide(column):
    return jnp.concatenate([column, column], axis=1)


def block_diagonal(matrix, flipped):
    row = lax.broadcasted_iota(i32, (W, DOF), 0) % DOF
    col = lax.broadcasted_iota(i32, (W, DOF), 1)
    spread = (row == col).astype(f32).astype(bf16)
    dims = (((1,), (1 if flipped else 0,)), ((), ()))
    half = lax.dot_general(spread, matrix, dims, preferred_element_type=f32).astype(bf16)
    full = lax.dot_general(half, spread, (((1,), (1,)), ((), ())), preferred_element_type=f32)
    r = lax.broadcasted_iota(i32, (W, W), 0) // DOF
    c = lax.broadcasted_iota(i32, (W, W), 1) // DOF
    return jnp.where(r == c, full, 0.0).astype(bf16)


def position():
    a, b = lax.axis_index("px"), lax.axis_index("py")
    n_py = lax.axis_size("py")
    return a * n_py + b, lax.rem(a, 2) == 0, lax.rem(b, 2) == 0


def partner(off, even_x, even_y):
    q_px = jnp.where((off > 0) == even_x, 0, 1)
    q_py = jnp.where((off > 0) == even_y, 2, 3)
    return jnp.where((off == 1) | (off == -1), q_py, q_px)


def targets(dest, slot, coarse_count):
    own, even_x, even_y = position()
    off = dest - own
    return jnp.where(off == 0, slot, coarse_count + partner(off, even_x, even_y) * GHOST + slot)


def list_rows(ghost):
    _, even_x, even_y = position()
    low_y, high_y, low_x, high_x = (ghost[j : j + 1, :] for j in range(4))
    ordered = [
        jnp.where(even_x, high_x, low_x),
        jnp.where(even_x, low_x, high_x),
        jnp.where(even_y, high_y, low_y),
        jnp.where(even_y, low_y, high_y),
    ]
    return jnp.broadcast_to(jnp.concatenate(ordered, axis=1), (8, 4 * GHOST))


def ones_where(mask):
    return jnp.where(mask, jnp.ones((), bf16), jnp.zeros((), bf16))


def one_hot_rows(values, row_count):
    row_id = lax.broadcasted_iota(i32, (row_count, LANES), 0).astype(i16)
    hits = []
    for r in range(values.shape[0]):
        wanted = jnp.broadcast_to(values[r : r + 1, :], (16, LANES)).astype(i16)
        wanted = jnp.concatenate([wanted] * (row_count // 16), axis=0)
        hits.append(ones_where(row_id == wanted))
    return jnp.concatenate(hits, axis=1)


def columns(rows):
    flipped = rows.T
    parts = [
        jnp.broadcast_to(flipped[:, r : r + 1], (LANES, LANES)).astype(i16) for r in range(rows.shape[0])
    ]
    return jnp.concatenate(parts, axis=0)


def one_hot_columns(column, row_count):
    lane = lax.broadcasted_iota(i32, column.shape, 1).astype(i16)
    return jnp.concatenate(
        [ones_where(column - jnp.asarray(k * LANES, i16) == lane) for k in range(row_count // LANES)], axis=1
    )


def typed(x_rows, kinds, table):
    kinds = wide(kinds)
    parts = [jnp.where(kinds == jnp.asarray(t, i16), x_rows, jnp.zeros((), bf16)) for t in range(NTYPE)]
    return jnp.dot(jnp.concatenate(parts, axis=1), table, preferred_element_type=f32)


def restrict_kernel(x_ref, dest_ref, slot_ref, type_ref, table_ref, local_ref, g0, g1, g2, g3, w_ref, acc_ref):
    step = pl.program_id(0)
    rows_out = acc_ref.shape[0]
    coarse_count = rows_out - 4 * GHOST

    @pl.when(step == 0)
    def _():
        for t in range(NTYPE):
            w_ref[t * W : (t + 1) * W, :] = block_diagonal(table_ref[t], True)
        acc_ref[...] = jnp.zeros_like(acc_ref)

    contrib = typed(x_ref[...], columns(type_ref[...]), w_ref[...]).astype(bf16)
    hits = one_hot_rows(targets(dest_ref[...], slot_ref[...], coarse_count), rows_out)
    acc_ref[...] += jnp.dot(hits, contrib, preferred_element_type=f32)

    @pl.when(step == pl.num_programs(0) - 1)
    def _():
        local_ref[...] = acc_ref[:coarse_count, :]
        for q, out in enumerate((g0, g1, g2, g3)):
            first = coarse_count + q * GHOST
            out[...] = acc_ref[first : first + GHOST, :].astype(bf16)


def apply_blocks(inv_ref, v):
    count = v.shape[0]
    lane = lax.broadcasted_iota(i32, (count, LANES), 1)
    row = lax.broadcasted_iota(i32, (DOF * DOF, DOF), 0)
    col = lax.broadcasted_iota(i32, (DOF * DOF, DOF), 1)
    summing = (col == row // DOF).astype(f32).astype(bf16)
    outs = []
    for s in range(RHS):
        tile = v[:, (s // 2) * LANES : (s // 2 + 1) * LANES].astype(f32)
        turned = pltpu.roll(tile, DOF, 1)
        low, high = (tile, turned) if s % 2 == 0 else (turned, tile)
        doubled = jnp.where(lane < DOF, low, high).astype(bf16)
        products = jnp.concatenate(
            [inv_ref[:, k * LANES : (k + 1) * LANES] * doubled for k in range(DOF * DOF // LANES)], axis=1
        )
        outs.append(jnp.dot(products, summing, preferred_element_type=f32))
    return jnp.concatenate(outs, axis=1)


def sweep_kernel(local_ref, i0, i1, i2, i3, ghost_ref, inv_ref, out_ref):
    count = local_ref.shape[0]
    hits = one_hot_rows(list_rows(ghost_ref[...])[:1], count)
    incoming = jnp.concatenate([i0[...], i1[...], i2[...], i3[...]], axis=0)
    rhs = local_ref[...] + jnp.dot(hits, incoming, preferred_element_type=f32)
    out_ref[...] = apply_blocks(inv_ref, rhs.astype(bf16)).astype(bf16)


def couple_kernel(
    coef_ref, fs_ref, h0, h1, h2, h3, nb_ref, ci_ref, face_ref, ghost_ref, inv_ref,
    sol_ref, ans_ref, r0, r1, r2, r3, t_ref,
):
    count = fs_ref.shape[0]
    own, even_x, even_y = position()
    nb = nb_ref[...]
    off = nb // count - own
    block = jnp.where(off == 0, 0, 1 + partner(off, even_x, even_y))
    index = block * count + nb % count
    scale = jnp.zeros(nb.shape, f32)
    for k in range(KINDS):
        scale = jnp.where(ci_ref[...] == k, coef_ref[k], scale)
    index_t = index.T
    scale_t = scale.T
    for b, source in enumerate((fs_ref, h0, h1, h2, h3)):
        t_ref[b * count : (b + 1) * count, :] = source[...]
    coupled = jnp.zeros((count, W), f32)
    for f in range(FACES):
        column = jnp.broadcast_to(index_t[:, f : f + 1], (count, LANES)).astype(i16)
        beside = jnp.dot(one_hot_columns(column, 5 * count), t_ref[...], preferred_element_type=f32)
        term = jnp.dot(beside.astype(bf16), block_diagonal(face_ref[f], True), preferred_element_type=f32)
        coupled = coupled + term * wide(jnp.broadcast_to(scale_t[:, f : f + 1], (count, LANES)))
    correction = apply_blocks(inv_ref, coupled.astype(bf16))
    solution_rows = fs_ref[...].astype(f32) - OMEGA * correction
    sol_ref[...] = solution_rows
    answer = solution_rows.astype(bf16)
    ans_ref[...] = answer
    listed = jnp.broadcast_to(list_rows(ghost_ref[...]).T[:, :1], (4 * GHOST, LANES)).astype(i16)
    replies = jnp.dot(one_hot_columns(listed, count), answer, preferred_element_type=f32).astype(bf16)
    for q, out in enumerate((r0, r1, r2, r3)):
        out[...] = replies[q * GHOST : (q + 1) * GHOST, :]


def prolong_kernel(ans_ref, r0, r1, r2, r3, dest_ref, slot_ref, type_ref, table_ref, out_ref, w_ref, t_ref):
    step = pl.program_id(0)
    rows_in = t_ref.shape[0]
    coarse_count = rows_in - 4 * GHOST

    @pl.when(step == 0)
    def _():
        for t in range(NTYPE):
            w_ref[t * W : (t + 1) * W, :] = block_diagonal(table_ref[t], False)
        t_ref[:coarse_count, :] = ans_ref[...]
        for q, r in enumerate((r0, r1, r2, r3)):
            first = coarse_count + q * GHOST
            t_ref[first : first + GHOST, :] = r[...]

    target = columns(targets(dest_ref[...], slot_ref[...], coarse_count))
    fetched = jnp.dot(one_hot_columns(target, rows_in), t_ref[...], preferred_element_type=f32).astype(bf16)
    out_ref[...] = typed(fetched, columns(type_ref[...]), w_ref[...]).astype(bf16)


VMEM = pl.BlockSpec(memory_space=pltpu.VMEM)


def ghost_shape():
    return [jax.ShapeDtypeStruct((GHOST, W), bf16)] * 4


def whole(shape):
    return pl.BlockSpec(shape, lambda *_: (0,) * len(shape))


def restrict(x, meta, table, count):
    steps = x.shape[0] // CHUNK
    rows = count + 4 * GHOST
    meta_spec = pl.BlockSpec((CHUNK // LANES, LANES), lambda i: (i, 0))
    return pl.pallas_call(
        restrict_kernel,
        grid=(steps,),
        in_specs=[pl.BlockSpec((CHUNK, W), lambda i: (i, 0)), meta_spec, meta_spec, meta_spec, whole(table.shape)],
        out_specs=[VMEM] * 5,
        out_shape=[jax.ShapeDtypeStruct((count, W), f32)] + ghost_shape(),
        scratch_shapes=[pltpu.VMEM((NTYPE * W, W), bf16), pltpu.VMEM((rows, W), f32)],
        name="restrict",
    )(x, *meta, table)


def sweep(local, incoming, ghost, inverse):
    return pl.pallas_call(
        sweep_kernel,
        in_specs=[VMEM] * 7,
        out_specs=VMEM,
        out_shape=jax.ShapeDtypeStruct(local.shape, bf16),
        name="sweep",
    )(local, *incoming, ghost, inverse)


def couple(coef, first_sweep, halo, neighbours, coef_index, face_table, ghost, inverse):
    count = first_sweep.shape[0]
    return pl.pallas_call(
        couple_kernel,
        in_specs=[pl.BlockSpec(memory_space=pltpu.SMEM)] + [VMEM] * 10,
        out_specs=[VMEM] * 6,
        out_shape=[jax.ShapeDtypeStruct((count, W), f32), jax.ShapeDtypeStruct((count, W), bf16)] + ghost_shape(),
        scratch_shapes=[pltpu.VMEM((5 * count, W), bf16)],
        name="couple",
    )(coef, first_sweep, *halo, neighbours, coef_index, face_table, ghost, inverse)


def prolong(answer, returned, meta, table, fine_count):
    count = answer.shape[0]
    rows = count + 4 * GHOST
    meta_spec = pl.BlockSpec((CHUNK // LANES, LANES), lambda i: (i, 0))
    return pl.pallas_call(
        prolong_kernel,
        grid=(fine_count // CHUNK,),
        in_specs=[VMEM] * 5 + [meta_spec, meta_spec, meta_spec, whole(table.shape)],
        out_specs=pl.BlockSpec((CHUNK, W), lambda i: (i, 0)),
        out_shape=jax.ShapeDtypeStruct((fine_count, W), bf16),
        scratch_shapes=[pltpu.VMEM((NTYPE * W, W), bf16), pltpu.VMEM((rows, W), bf16)],
        name="prolong",
    )(answer, *returned, *meta, table)


def shards(
    fine_residual, dest_owner, coarse_slot, ghost_slot, child_type, restrict_table, inverse_blocks,
    face_table, face_coef, coef_index, neighbours,
):
    fine_count = fine_residual.shape[0]
    count = inverse_blocks.shape[0]
    perms = swap_pairs(lax.axis_size("px"), lax.axis_size("py"))
    meta = [m.reshape(fine_count // LANES, LANES) for m in (dest_owner, coarse_slot, child_type)]
    local, *outgoing = restrict(fine_residual, meta, restrict_table, count)
    incoming = exchange(outgoing, perms)
    first_sweep = sweep(local, incoming, ghost_slot, inverse_blocks)
    halo = exchange([first_sweep] * 4, perms)
    coarse_solution, answer, *replies = couple(
        face_coef, first_sweep, halo, neighbours, coef_index, face_table, ghost_slot, inverse_blocks
    )
    returned = exchange(replies, perms)
    fine_correction = prolong(answer, returned, meta, restrict_table, fine_count)
    return (coarse_solution, fine_correction)


def solution(mesh):
    both = ("px", "py")
    in_specs = (
        P(both, None), P(both), P(both), P(both, None), P(both), P(), P(both, None), P(), P(), P(None, both), P(None, both),
    )
    out_specs = (P(both, None), P(both, None))
    return jax.shard_map(shards, mesh=mesh, in_specs=in_specs, out_specs=out_specs, check_vma=False)
```

time: 86.2 us -> 86.3 us (level)
  Pallas kernels: 47.4 us -> 50.8 us
  local copies, waits for them, and re-layouts: 3.35 us -> 0 us
  waiting for transfers between devices: 14.3 us -> 15.2 us
    pallas_call x4, Pallas kernels: 47.4 us -> 50.8 us  [the longest x1 17.4 us: couple(): pl.pallas_call(couple_kernel, in_specs=[pl.BlockSpec(memory_space=pltpu.S...]
    unnamed x26 -> x0, local copies, waits for them, and re-layouts: 2.68 us -> none
    ppermute x12, waiting for transfers between devices: 14.3 us -> 15.2 us  [exchange(): lax.ppermute(x, ('px', 'py'), perm)]
  transfers between devices with their start and end apart: 12 -> 12, of which waited for: 5 -> 5; matrix products, arithmetic and copies ran while one was open for 1% -> 0% of each run, Pallas kernels for 0% -> 0%
where the time goes in v2:
time: 86.3 us; the launch traced here: 86.1 us
  Pallas kernels  50.8 us (59%)
  starting transfers between devices  19.4 us (22%)
  waiting for transfers between devices  15.2 us (18%)
    ppermute x12, starting transfers between devices, exchange(): lax.ppermute(x, ('px', 'py'), perm)  19.4 us
    pallas_call x1, Pallas kernels, couple(): pl.pallas_call(couple_kernel, in_specs=[pl.BlockSpec(memory_space=pltpu.S...  17.4 us
    ppermute x12, waiting for transfers between devices, exchange(): lax.ppermute(x, ('px', 'py'), perm)  15.2 us
    pallas_call x1, Pallas kernels, prolong(): pl.pallas_call(prolong_kernel, grid=(fine_count // CHUNK,), in_specs=[VME...  13.2 us
    pallas_call x1, Pallas kernels, restrict(): pl.pallas_call(restrict_kernel, grid=(steps,), in_specs=[pl.BlockSpec((CH...  12.2 us
    pallas_call x1, Pallas kernels, sweep(): pl.pallas_call(sweep_kernel, in_specs=[VMEM] * 7, out_specs=VMEM, out_sha...  7.94 us
  transfers between devices with their start and end apart: 12, of which 5 were waited for; matrix products, arithmetic and copies ran while one was open for 0% of the time, Pallas kernels for 0%

profile of v2, /device:TPU:8, one launch (start us, length us, event | category | flops | bytes accessed | tf_op | source)
XLA Modules:
  0.0 86.1 jit_solution(9487888153540594195)
XLA Ops:
  0.6 12.2 %restrict.1 = (f32[512,256]{1,0:T(8,128)}, bf16[32,256]{1,0:T(8,128)(2,1)}, bf16[32,256]{1,0:T(8,128)(2,1)}, bf16[32,256]{1,0:T(8,128)(2,1)}, bf16[32,256]{1,0:T(8,128)(2,1)}) custom-call(bf16[4096,256]{1,0:T(8,128)(2,1)} %x_ref.1, s32[32,128]{1,0:T(8,128)} %bitcast.3, s32[32,128]{1,0:T(8,128)} %bitcast.5, s32[32,128]{1,0:T(8,128)} %bitcast.7, ...), custom_call_target="tpu_custom_call" | custom-call | tf_op jit(solution)/shard_map/restrict/pallas_call | solution.py:252
  12.9 0.1 collective-permute-start
  13.0 0.4 collective-permute-start.1
  13.4 1.6 %collective-permute-start.2 = (bf16[32,256]{1,0:T(8,128)(2,1)}, bf16[32,256]{1,0:T(8,128)(2,1)S(1)}, u32[]{:S(2)}, u32[]{:S(2)}) collective-permute-start(bf16[32,256]{1,0:T(8,128)(2,1)} %get-tuple-element.16), channel_id=1, source_target_pairs={{0,1},{1,0},{2,3},{3,2},{4,5},{5,4},{6,7},{7,6},{8,9},{9,8},{10,11... | collective-permute-start | bytes 49160 | tf_op jit(solution)/shard_map/ppermute | solution.py:49
  15.0 5.6 %collective-permute-start.3 = (bf16[32,256]{1,0:T(8,128)(2,1)}, bf16[32,256]{1,0:T(8,128)(2,1)S(1)}, u32[]{:S(2)}, u32[]{:S(2)}) collective-permute-start(bf16[32,256]{1,0:T(8,128)(2,1)} %get-tuple-element.17), channel_id=1, source_target_pairs={{0,15},{1,2},{2,1},{3,4},{4,3},{5,6},{6,5},{7,8},{8,7},{9,10},{10,... | collective-permute-start | bytes 49160 | tf_op jit(solution)/shard_map/ppermute | solution.py:49
  20.6 0.0 collective-permute-done.i0
  20.6 0.0 collective-permute-done.1.i1
  20.6 0.0 collective-permute-done.2.i2
  20.6 1.9 %collective-permute-done.3.i3 = bf16[32,256]{1,0:T(8,128)(2,1)S(1)} collective-permute-done((bf16[32,256]{1,0:T(8,128)(2,1)}, bf16[32,256]{1,0:T(8,128)(2,1)S(1)}, u32[]{:S(2)}, u32[]{:S(2)}) %collective-permute-start.3) | collective-permute-done | bytes 16416 | tf_op jit(solution)/shard_map/ppermute | solution.py:49
  22.5 7.9 %sweep.1.fs_ref = bf16[512,256]{1,0:T(8,128)(2,1)} custom-call(f32[512,256]{1,0:T(8,128)} %get-tuple-element.13.local_ref, bf16[32,256]{1,0:T(8,128)(2,1)S(1)} %collective-permute-done.i0, bf16[32,256]{1,0:T(8,128)(2,1)S(1)} %collective-permute-done.1.i1, bf16[32,256]{1,0:T(8,128)(2,1)S(1)} %collective-permute-done.2.i2, ...), custom_call_target="tpu_custom_call" | custom-call | tf_op jit(solution)/shard_map/sweep/pallas_call | solution.py:264
  30.5 5.5 %collective-permute-start.7 = (bf16[512,256]{1,0:T(8,128)(2,1)}, bf16[512,256]{1,0:T(8,128)(2,1)S(1)}, u32[]{:S(2)}, u32[]{:S(2)}) collective-permute-start(bf16[512,256]{1,0:T(8,128)(2,1)} %sweep.1.fs_ref), channel_id=1, source_target_pairs={{0,15},{1,2},{2,1},{3,4},{4,3},{5,6},{6,5},{7,8},{8,7},{9,10},{10,... | collective-permute-start | bytes 786440 | tf_op jit(solution)/shard_map/ppermute | solution.py:49
  35.9 0.0 collective-permute-start.6
  35.9 0.0 collective-permute-start.5
  35.9 1.5 %collective-permute-start.4 = (bf16[512,256]{1,0:T(8,128)(2,1)}, bf16[512,256]{1,0:T(8,128)(2,1)S(1)}, u32[]{:S(2)}, u32[]{:S(2)}) collective-permute-start(bf16[512,256]{1,0:T(8,128)(2,1)} %sweep.1.fs_ref), channel_id=1, source_target_pairs={{0,16},{1,17},{2,18},{3,19},{4,20},{5,21},{6,22},{7,23},{8,24},{9,... | collective-permute-start | bytes 786440 | tf_op jit(solution)/shard_map/ppermute | solution.py:49
  37.5 5.2 %collective-permute-done.7.h3 = bf16[512,256]{1,0:T(8,128)(2,1)S(1)} collective-permute-done((bf16[512,256]{1,0:T(8,128)(2,1)}, bf16[512,256]{1,0:T(8,128)(2,1)S(1)}, u32[]{:S(2)}, u32[]{:S(2)}) %collective-permute-start.7) | collective-permute-done | bytes 262176 | tf_op jit(solution)/shard_map/ppermute | solution.py:49
  42.7 1.5 %collective-permute-done.6.h2 = bf16[512,256]{1,0:T(8,128)(2,1)S(1)} collective-permute-done((bf16[512,256]{1,0:T(8,128)(2,1)}, bf16[512,256]{1,0:T(8,128)(2,1)S(1)}, u32[]{:S(2)}, u32[]{:S(2)}) %collective-permute-start.6) | collective-permute-done | bytes 262176 | tf_op jit(solution)/shard_map/ppermute | solution.py:49
  44.2 0.0 collective-permute-done.5.h1
  44.2 0.0 collective-permute-done.4.h0
  44.2 17.4 %couple.1 = (f32[512,256]{1,0:T(8,128)}, bf16[512,256]{1,0:T(8,128)(2,1)}, bf16[32,256]{1,0:T(8,128)(2,1)}, bf16[32,256]{1,0:T(8,128)(2,1)}, bf16[32,256]{1,0:T(8,128)(2,1)}, /*index=5*/bf16[32,256]{1,0:T(8,128)(2,1)}) custom-call(f32[16]{0:T(128)} %coef_ref.1, bf16[512,256]{1,0:T(8,128)(2,1)} %sweep.1.fs_ref, ...), custom_call_target="tpu_custom_call" | custom-call | tf_op jit(solution)/shard_map/couple/pallas_call | solution.py:275
  61.6 0.0 collective-permute-start.8
  61.6 2.0 %collective-permute-start.9 = (bf16[32,256]{1,0:T(8,128)(2,1)}, bf16[32,256]{1,0:T(8,128)(2,1)S(1)}, u32[]{:S(2)}, u32[]{:S(2)}) collective-permute-start(bf16[32,256]{1,0:T(8,128)(2,1)} %get-tuple-element.21), channel_id=1, source_target_pairs={{0,112},{1,113},{2,114},{3,115},{4,116},{5,117},{6,118},{7,119},{8... | collective-permute-start | bytes 49160 | tf_op jit(solution)/shard_map/ppermute | solution.py:49
  63.5 2.0 %collective-permute-start.10 = (bf16[32,256]{1,0:T(8,128)(2,1)}, bf16[32,256]{1,0:T(8,128)(2,1)S(1)}, u32[]{:S(2)}, u32[]{:S(2)}) collective-permute-start(bf16[32,256]{1,0:T(8,128)(2,1)} %get-tuple-element.22), channel_id=1, source_target_pairs={{0,1},{1,0},{2,3},{3,2},{4,5},{5,4},{6,7},{7,6},{8,9},{9,8},{10,11... | collective-permute-start | bytes 49160 | tf_op jit(solution)/shard_map/ppermute | solution.py:49
  65.6 0.7 collective-permute-start.11
  66.2 0.0 collective-permute-done.8.r0
  66.3 0.0 collective-permute-done.9.r1
  66.3 1.2 %collective-permute-done.10.r2 = bf16[32,256]{1,0:T(8,128)(2,1)S(1)} collective-permute-done((bf16[32,256]{1,0:T(8,128)(2,1)}, bf16[32,256]{1,0:T(8,128)(2,1)S(1)}, u32[]{:S(2)}, u32[]{:S(2)}) %collective-permute-start.10) | collective-permute-done | bytes 16416 | tf_op jit(solution)/shard_map/ppermute | solution.py:49
  67.5 5.3 %collective-permute-done.11.r3 = bf16[32,256]{1,0:T(8,128)(2,1)S(1)} collective-permute-done((bf16[32,256]{1,0:T(8,128)(2,1)}, bf16[32,256]{1,0:T(8,128)(2,1)S(1)}, u32[]{:S(2)}, u32[]{:S(2)}) %collective-permute-start.11) | collective-permute-done | bytes 16416 | tf_op jit(solution)/shard_map/ppermute | solution.py:49
  72.8 13.2 %prolong.1 = bf16[4096,256]{1,0:T(8,128)(2,1)} custom-call(bf16[512,256]{1,0:T(8,128)(2,1)} %get-tuple-element.19.ans_ref, bf16[32,256]{1,0:T(8,128)(2,1)S(1)} %collective-permute-done.8.r0, bf16[32,256]{1,0:T(8,128)(2,1)S(1)} %collective-permute-done.9.r1, bf16[32,256]{1,0:T(8,128)(2,1)S(1)} %collective-permute-done.10.r2, ...), custom_call_target="tpu_custom_call" | custom-call | tf_op jit(solution)/shard_map/prolong/pallas_call | solution.py:289
Async XLA Ops:
  12.9 7.7 %collective-permute-start = (bf16[32,256]{1,0:T(8,128)(2,1)}, bf16[32,256]{1,0:T(8,128)(2,1)S(1)}, u32[]{:S(2)}, u32[]{:S(2)}) collective-permute-start(bf16[32,256]{1,0:T(8,128)(2,1)} %get-tuple-element.14), channel_id=1, source_target_pairs={{0,16},{1,17},{2,18},{3,19},{4,20},{5,21},{6,22},{7,23},{8,24},{9,... | collective-permute-start | bytes 49160 | tf_op jit(solution)/shard_map/ppermute | solution.py:49
  13.0 7.6 %collective-permute-start.1 = (bf16[32,256]{1,0:T(8,128)(2,1)}, bf16[32,256]{1,0:T(8,128)(2,1)S(1)}, u32[]{:S(2)}, u32[]{:S(2)}) collective-permute-start(bf16[32,256]{1,0:T(8,128)(2,1)} %get-tuple-element.15), channel_id=1, source_target_pairs={{0,112},{1,113},{2,114},{3,115},{4,116},{5,117},{6,118},{7,119},{8... | collective-permute-start | bytes 49160 | tf_op jit(solution)/shard_map/ppermute | solution.py:49
  13.4 7.2 %collective-permute-start.2 = (bf16[32,256]{1,0:T(8,128)(2,1)}, bf16[32,256]{1,0:T(8,128)(2,1)S(1)}, u32[]{:S(2)}, u32[]{:S(2)}) collective-permute-start(bf16[32,256]{1,0:T(8,128)(2,1)} %get-tuple-element.16), channel_id=1, source_target_pairs={{0,1},{1,0},{2,3},{3,2},{4,5},{5,4},{6,7},{7,6},{8,9},{9,8},{10,11... | collective-permute-start | bytes 49160 | tf_op jit(solution)/shard_map/ppermute | solution.py:49
  15.0 7.5 %collective-permute-start.3 = (bf16[32,256]{1,0:T(8,128)(2,1)}, bf16[32,256]{1,0:T(8,128)(2,1)S(1)}, u32[]{:S(2)}, u32[]{:S(2)}) collective-permute-start(bf16[32,256]{1,0:T(8,128)(2,1)} %get-tuple-element.17), channel_id=1, source_target_pairs={{0,15},{1,2},{2,1},{3,4},{4,3},{5,6},{6,5},{7,8},{8,7},{9,10},{10,... | collective-permute-start | bytes 49160 | tf_op jit(solution)/shard_map/ppermute | solution.py:49
  30.5 12.2 %collective-permute-start.7 = (bf16[512,256]{1,0:T(8,128)(2,1)}, bf16[512,256]{1,0:T(8,128)(2,1)S(1)}, u32[]{:S(2)}, u32[]{:S(2)}) collective-permute-start(bf16[512,256]{1,0:T(8,128)(2,1)} %sweep.1.fs_ref), channel_id=1, source_target_pairs={{0,15},{1,2},{2,1},{3,4},{4,3},{5,6},{6,5},{7,8},{8,7},{9,10},{10,... | collective-permute-start | bytes 786440 | tf_op jit(solution)/shard_map/ppermute | solution.py:49
  35.9 8.2 %collective-permute-start.6 = (bf16[512,256]{1,0:T(8,128)(2,1)}, bf16[512,256]{1,0:T(8,128)(2,1)S(1)}, u32[]{:S(2)}, u32[]{:S(2)}) collective-permute-start(bf16[512,256]{1,0:T(8,128)(2,1)} %sweep.1.fs_ref), channel_id=1, source_target_pairs={{0,1},{1,0},{2,3},{3,2},{4,5},{5,4},{6,7},{7,6},{8,9},{9,8},{10,11... | collective-permute-start | bytes 786440 | tf_op jit(solution)/shard_map/ppermute | solution.py:49
  35.9 8.2 %collective-permute-start.5 = (bf16[512,256]{1,0:T(8,128)(2,1)}, bf16[512,256]{1,0:T(8,128)(2,1)S(1)}, u32[]{:S(2)}, u32[]{:S(2)}) collective-permute-start(bf16[512,256]{1,0:T(8,128)(2,1)} %sweep.1.fs_ref), channel_id=1, source_target_pairs={{0,112},{1,113},{2,114},{3,115},{4,116},{5,117},{6,118},{7,119},{8... | collective-permute-start | bytes 786440 | tf_op jit(solution)/shard_map/ppermute | solution.py:49
  35.9 8.2 %collective-permute-start.4 = (bf16[512,256]{1,0:T(8,128)(2,1)}, bf16[512,256]{1,0:T(8,128)(2,1)S(1)}, u32[]{:S(2)}, u32[]{:S(2)}) collective-permute-start(bf16[512,256]{1,0:T(8,128)(2,1)} %sweep.1.fs_ref), channel_id=1, source_target_pairs={{0,16},{1,17},{2,18},{3,19},{4,20},{5,21},{6,22},{7,23},{8,24},{9,... | collective-permute-start | bytes 786440 | tf_op jit(solution)/shard_map/ppermute | solution.py:49
  61.6 4.7 %collective-permute-start.8 = (bf16[32,256]{1,0:T(8,128)(2,1)}, bf16[32,256]{1,0:T(8,128)(2,1)S(1)}, u32[]{:S(2)}, u32[]{:S(2)}) collective-permute-start(bf16[32,256]{1,0:T(8,128)(2,1)} %get-tuple-element.20), channel_id=1, source_target_pairs={{0,16},{1,17},{2,18},{3,19},{4,20},{5,21},{6,22},{7,23},{8,24},{9,... | collective-permute-start | bytes 49160 | tf_op jit(solution)/shard_map/ppermute | solution.py:49
  61.6 4.7 %collective-permute-start.9 = (bf16[32,256]{1,0:T(8,128)(2,1)}, bf16[32,256]{1,0:T(8,128)(2,1)S(1)}, u32[]{:S(2)}, u32[]{:S(2)}) collective-permute-start(bf16[32,256]{1,0:T(8,128)(2,1)} %get-tuple-element.21), channel_id=1, source_target_pairs={{0,112},{1,113},{2,114},{3,115},{4,116},{5,117},{6,118},{7,119},{8... | collective-permute-start | bytes 49160 | tf_op jit(solution)/shard_map/ppermute | solution.py:49
  63.5 4.0 %collective-permute-start.10 = (bf16[32,256]{1,0:T(8,128)(2,1)}, bf16[32,256]{1,0:T(8,128)(2,1)S(1)}, u32[]{:S(2)}, u32[]{:S(2)}) collective-permute-start(bf16[32,256]{1,0:T(8,128)(2,1)} %get-tuple-element.22), channel_id=1, source_target_pairs={{0,1},{1,0},{2,3},{3,2},{4,5},{5,4},{6,7},{7,6},{8,9},{9,8},{10,11... | collective-permute-start | bytes 49160 | tf_op jit(solution)/shard_map/ppermute | solution.py:49
  65.6 7.3 %collective-permute-start.11 = (bf16[32,256]{1,0:T(8,128)(2,1)}, bf16[32,256]{1,0:T(8,128)(2,1)S(1)}, u32[]{:S(2)}, u32[]{:S(2)}) collective-permute-start(bf16[32,256]{1,0:T(8,128)(2,1)} %get-tuple-element.23), channel_id=1, source_target_pairs={{0,15},{1,2},{2,1},{3,4},{4,3},{5,6},{6,5},{7,8},{8,7},{9,10},{10,... | collective-permute-start | bytes 49160 | tf_op jit(solution)/shard_map/ppermute | solution.py:49

commit v3 on v2

--- a/solution.py
+++ b/solution.py
@@ -21,6 +21,9 @@
 GHOST = 32
 LANES = 128
 CHUNK = 1024
+RB = 128
+PB = 512
+VMEM_BYTES = 40 * 2**20
 
 
 def swap_pairs(n_px, n_py):
@@ -125,24 +128,32 @@
     )
 
 
-def typed(x_rows, kinds, table):
-    kinds = wide(kinds)
-    parts = [jnp.where(kinds == jnp.asarray(t, i16), x_rows, jnp.zeros((), bf16)) for t in range(NTYPE)]
-    return jnp.dot(jnp.concatenate(parts, axis=1), table, preferred_element_type=f32)
-
-
-def restrict_kernel(x_ref, dest_ref, slot_ref, type_ref, table_ref, local_ref, g0, g1, g2, g3, w_ref, acc_ref):
+def typed(x_rows, kinds, table, rows):
+    outs = []
+    for r in range(0, x_rows.shape[0], rows):
+        x, kind = x_rows[r : r + rows], kinds[r : r + rows]
+        parts = [x * wide(ones_where(kind == jnp.asarray(t, i16))) for t in range(NTYPE)]
+        outs.append(jnp.dot(jnp.concatenate(parts, axis=1), table, preferred_element_type=f32).astype(bf16))
+    return jnp.concatenate(outs, axis=0)
+
+
+def restrict_kernel(
+    x_ref, dest_ref, slot_ref, type_ref, table_ref, inv_hbm, local_ref, g0, g1, g2, g3, inv_ref, w_ref, acc_ref, sem
+):
     step = pl.program_id(0)
     rows_out = acc_ref.shape[0]
     coarse_count = rows_out - 4 * GHOST
 
+    load = pltpu.make_async_copy(inv_hbm, inv_ref, sem)
+
     @pl.when(step == 0)
     def _():
+        load.start()
         for t in range(NTYPE):
             w_ref[t * W : (t + 1) * W, :] = block_diagonal(table_ref[t], True)
         acc_ref[...] = jnp.zeros_like(acc_ref)
 
-    contrib = typed(x_ref[...], columns(type_ref[...]), w_ref[...]).astype(bf16)
+    contrib = typed(x_ref[...], columns(type_ref[...]), w_ref[...], RB)
     hits = one_hot_rows(targets(dest_ref[...], slot_ref[...], coarse_count), rows_out)
     acc_ref[...] += jnp.dot(hits, contrib, preferred_element_type=f32)
 
@@ -152,6 +163,7 @@
         for q, out in enumerate((g0, g1, g2, g3)):
             first = coarse_count + q * GHOST
             out[...] = acc_ref[first : first + GHOST, :].astype(bf16)
+        load.wait()
 
 
 def apply_blocks(inv_ref, v):
@@ -183,25 +195,27 @@
 
 def couple_kernel(
     coef_ref, fs_ref, h0, h1, h2, h3, nb_ref, ci_ref, face_ref, ghost_ref, inv_ref,
-    sol_ref, ans_ref, r0, r1, r2, r3, t_ref,
+    sol_ref, ans_ref, r0, r1, r2, r3,
 ):
     count = fs_ref.shape[0]
     own, even_x, even_y = position()
     nb = nb_ref[...]
     off = nb // count - own
     block = jnp.where(off == 0, 0, 1 + partner(off, even_x, even_y))
-    index = block * count + nb % count
+    index_t = (nb % count).T
+    block_t = block.T
     scale = jnp.zeros(nb.shape, f32)
     for k in range(KINDS):
         scale = jnp.where(ci_ref[...] == k, coef_ref[k], scale)
-    index_t = index.T
     scale_t = scale.T
-    for b, source in enumerate((fs_ref, h0, h1, h2, h3)):
-        t_ref[b * count : (b + 1) * count, :] = source[...]
     coupled = jnp.zeros((count, W), f32)
     for f in range(FACES):
         column = jnp.broadcast_to(index_t[:, f : f + 1], (count, LANES)).astype(i16)
-        beside = jnp.dot(one_hot_columns(column, 5 * count), t_ref[...], preferred_element_type=f32)
+        hits = one_hot_columns(column, count)
+        where = wide(jnp.broadcast_to(block_t[:, f : f + 1], (count, LANES)))
+        beside = jnp.dot(hits, fs_ref[...], preferred_element_type=f32)
+        for q, source in enumerate((h0, h1, h2, h3)):
+            beside = jnp.where(where == q + 1, jnp.dot(hits, source[...], preferred_element_type=f32), beside)
         term = jnp.dot(beside.astype(bf16), block_diagonal(face_ref[f], True), preferred_element_type=f32)
         coupled = coupled + term * wide(jnp.broadcast_to(scale_t[:, f : f + 1], (count, LANES)))
     correction = apply_blocks(inv_ref, coupled.astype(bf16))
@@ -231,33 +245,39 @@
 
     target = columns(targets(dest_ref[...], slot_ref[...], coarse_count))
     fetched = jnp.dot(one_hot_columns(target, rows_in), t_ref[...], preferred_element_type=f32).astype(bf16)
-    out_ref[...] = typed(fetched, columns(type_ref[...]), w_ref[...]).astype(bf16)
+    out_ref[...] = typed(fetched, columns(type_ref[...]), w_ref[...], PB)
 
 
 VMEM = pl.BlockSpec(memory_space=pltpu.VMEM)
 
 
+def in_hbm(x):
+    return pltpu.with_memory_space_constraint(x, pltpu.HBM)
+
+
 def ghost_shape():
-    return [jax.ShapeDtypeStruct((GHOST, W), bf16)] * 4
+    return [pltpu.VMEM((GHOST, W), bf16)] * 4
 
 
 def whole(shape):
     return pl.BlockSpec(shape, lambda *_: (0,) * len(shape))
 
 
-def restrict(x, meta, table, count):
+def restrict(x, meta, table, inverse):
+    count = inverse.shape[0]
     steps = x.shape[0] // CHUNK
     rows = count + 4 * GHOST
     meta_spec = pl.BlockSpec((CHUNK // LANES, LANES), lambda i: (i, 0))
     return pl.pallas_call(
         restrict_kernel,
         grid=(steps,),
-        in_specs=[pl.BlockSpec((CHUNK, W), lambda i: (i, 0)), meta_spec, meta_spec, meta_spec, whole(table.shape)],
-        out_specs=[VMEM] * 5,
-        out_shape=[jax.ShapeDtypeStruct((count, W), f32)] + ghost_shape(),
-        scratch_shapes=[pltpu.VMEM((NTYPE * W, W), bf16), pltpu.VMEM((rows, W), f32)],
+        in_specs=[pl.BlockSpec((CHUNK, W), lambda i: (i, 0)), meta_spec, meta_spec, meta_spec, whole(table.shape), pl.BlockSpec(memory_space=pltpu.HBM)],
+        out_specs=[VMEM] * 6,
+        out_shape=[pltpu.VMEM((count, W), f32)] + ghost_shape() + [pltpu.VMEM(inverse.shape, bf16)],
+        scratch_shapes=[pltpu.VMEM((NTYPE * W, W), bf16), pltpu.VMEM((rows, W), f32), pltpu.SemaphoreType.DMA],
+        compiler_params=pltpu.CompilerParams(vmem_limit_bytes=VMEM_BYTES),
         name="restrict",
-    )(x, *meta, table)
+    )(x, *meta, table, inverse)
 
 
 def sweep(local, incoming, ghost, inverse):
@@ -265,7 +285,8 @@
         sweep_kernel,
         in_specs=[VMEM] * 7,
         out_specs=VMEM,
-        out_shape=jax.ShapeDtypeStruct(local.shape, bf16),
+        out_shape=pltpu.VMEM(local.shape, bf16),
+        compiler_params=pltpu.CompilerParams(vmem_limit_bytes=VMEM_BYTES),
         name="sweep",
     )(local, *incoming, ghost, inverse)
 
@@ -276,8 +297,8 @@
         couple_kernel,
         in_specs=[pl.BlockSpec(memory_space=pltpu.SMEM)] + [VMEM] * 10,
         out_specs=[VMEM] * 6,
-        out_shape=[jax.ShapeDtypeStruct((count, W), f32), jax.ShapeDtypeStruct((count, W), bf16)] + ghost_shape(),
-        scratch_shapes=[pltpu.VMEM((5 * count, W), bf16)],
+        out_shape=[jax.ShapeDtypeStruct((count, W), f32), pltpu.VMEM((count, W), bf16)] + ghost_shape(),
+        compiler_params=pltpu.CompilerParams(vmem_limit_bytes=VMEM_BYTES),
         name="couple",
     )(coef, first_sweep, *halo, neighbours, coef_index, face_table, ghost, inverse)
 
@@ -293,6 +314,7 @@
         out_specs=pl.BlockSpec((CHUNK, W), lambda i: (i, 0)),
         out_shape=jax.ShapeDtypeStruct((fine_count, W), bf16),
         scratch_shapes=[pltpu.VMEM((NTYPE * W, W), bf16), pltpu.VMEM((rows, W), bf16)],
+        compiler_params=pltpu.CompilerParams(vmem_limit_bytes=VMEM_BYTES),
         name="prolong",
     )(answer, *returned, *meta, table)
 
@@ -302,15 +324,16 @@
     face_table, face_coef, coef_index, neighbours,
 ):
     fine_count = fine_residual.shape[0]
-    count = inverse_blocks.shape[0]
     perms = swap_pairs(lax.axis_size("px"), lax.axis_size("py"))
     meta = [m.reshape(fine_count // LANES, LANES) for m in (dest_owner, coarse_slot, child_type)]
-    local, *outgoing = restrict(fine_residual, meta, restrict_table, count)
+    local, *outgoing, inverse = restrict(
+        in_hbm(fine_residual), [in_hbm(m) for m in meta], in_hbm(restrict_table), in_hbm(inverse_blocks)
+    )
     incoming = exchange(outgoing, perms)
-    first_sweep = sweep(local, incoming, ghost_slot, inverse_blocks)
+    first_sweep = sweep(local, incoming, ghost_slot, inverse)
     halo = exchange([first_sweep] * 4, perms)
     coarse_solution, answer, *replies = couple(
-        face_coef, first_sweep, halo, neighbours, coef_index, face_table, ghost_slot, inverse_blocks
+        face_coef, first_sweep, halo, neighbours, coef_index, face_table, ghost_slot, inverse
     )
     returned = exchange(replies, perms)
     fine_correction = prolong(answer, returned, meta, restrict_table, fine_count)

time: 86.3 us -> 71.2 us (0.83)
  Pallas kernels: 50.8 us -> 36.2 us
    pallas_call x1, Pallas kernels: 17.4 us -> 12.7 us  [couple(): pl.pallas_call(couple_kernel, in_specs=[pl.BlockSpec(memory_space=pltpu.S...]
    pallas_call x1, Pallas kernels: 13.2 us -> 9.24 us  [prolong(): pl.pallas_call(prolong_kernel, grid=(fine_count // CHUNK,), in_specs=[VME...]
    pallas_call x1, Pallas kernels: 12.2 us -> 9.24 us  [restrict(): pl.pallas_call(restrict_kernel, grid=(steps,), in_specs=[pl.BlockSpec((CH...]
    pallas_call x1, Pallas kernels: 7.94 us -> 5.07 us  [sweep(): pl.pallas_call(sweep_kernel, in_specs=[VMEM] * 7, out_specs=VMEM, out_sha...]
where the time goes in v3:
time: 71.2 us; the launch traced here: 71.1 us
  Pallas kernels  36.2 us (51%)
  starting transfers between devices  19.5 us (27%)
  waiting for transfers between devices  14.6 us (21%)
  between operations  0.76 us (1%)
    ppermute x12, starting transfers between devices, exchange(): lax.ppermute(x, ('px', 'py'), perm)  19.5 us
    ppermute x12, waiting for transfers between devices, exchange(): lax.ppermute(x, ('px', 'py'), perm)  14.6 us
    pallas_call x1, Pallas kernels, couple(): pl.pallas_call(couple_kernel, in_specs=[pl.BlockSpec(memory_space=pltpu.S...  12.7 us
    pallas_call x1, Pallas kernels, prolong(): pl.pallas_call(prolong_kernel, grid=(fine_count // CHUNK,), in_specs=[VME...  9.24 us
    pallas_call x1, Pallas kernels, restrict(): pl.pallas_call(restrict_kernel, grid=(steps,), in_specs=[pl.BlockSpec((CH...  9.24 us
    pallas_call x1, Pallas kernels, sweep(): pl.pallas_call(sweep_kernel, in_specs=[VMEM] * 7, out_specs=VMEM, out_sha...  5.07 us
  transfers between devices with their start and end apart: 12, of which 5 were waited for; matrix products, arithmetic and copies ran while one was open for 0% of the time, Pallas kernels for 0%

profile of v3, /device:TPU:8, one launch (start us, length us, event | category | flops | bytes accessed | tf_op | source)
XLA Modules:
  0.0 71.1 jit_solution(9155095237375947082)
XLA Ops:
  0.6 0.0 copy-start.7
  0.6 0.0 copy-start.1
  0.7 0.0 copy-start.5
  0.7 0.0 copy-start.6
  0.7 0.0 copy-start.8
  0.7 9.2 %restrict.1 = (f32[512,256]{1,0:T(8,128)S(1)}, bf16[32,256]{1,0:T(8,128)(2,1)S(1)}, bf16[32,256]{1,0:T(8,128)(2,1)S(1)}, bf16[32,256]{1,0:T(8,128)(2,1)S(1)}, bf...) custom-call(bf16[4096,256]{1,0:T(8,128)(2,1)} %x_ref.1, s32[32,128]{1,0:T(8,128)} %bitcast.3, s32[32,128]{1,0:T(8,128)} %bitcast.5, ...), custom_call_target="tpu_custom_call" | custom-call | tf_op jit(solution)/shard_map/restrict/pallas_call | solution.py:271
  9.9 0.1 collective-permute-start
  10.0 0.4 collective-permute-start.1
  10.5 1.6 %collective-permute-start.2 = (bf16[32,256]{1,0:T(8,128)(2,1)S(1)}, bf16[32,256]{1,0:T(8,128)(2,1)S(1)}, u32[]{:S(2)}, u32[]{:S(2)}) collective-permute-start(bf16[32,256]{1,0:T(8,128)(2,1)S(1)} %get-tuple-element.17), channel_id=1, source_target_pairs={{0,1},{1,0},{2,3},{3,2},{4,5},{5,4},{6,7},{7,6},{8,9},{9,8},{10,11... | collective-permute-start | bytes 49160 | tf_op jit(solution)/shard_map/ppermute | solution.py:52
  12.1 5.6 %collective-permute-start.3 = (bf16[32,256]{1,0:T(8,128)(2,1)S(1)}, bf16[32,256]{1,0:T(8,128)(2,1)S(1)}, u32[]{:S(2)}, u32[]{:S(2)}) collective-permute-start(bf16[32,256]{1,0:T(8,128)(2,1)S(1)} %get-tuple-element.18), channel_id=1, source_target_pairs={{0,15},{1,2},{2,1},{3,4},{4,3},{5,6},{6,5},{7,8},{8,7},{9,10},{10,... | collective-permute-start | bytes 49160 | tf_op jit(solution)/shard_map/ppermute | solution.py:52
  17.6 0.0 collective-permute-done.i0
  17.6 0.0 collective-permute-done.1.i1
  17.6 0.0 collective-permute-done.2.i2
  17.6 1.7 %collective-permute-done.3.i3 = bf16[32,256]{1,0:T(8,128)(2,1)S(1)} collective-permute-done((bf16[32,256]{1,0:T(8,128)(2,1)S(1)}, bf16[32,256]{1,0:T(8,128)(2,1)S(1)}, u32[]{:S(2)}, u32[]{:S(2)}) %collective-permute-start.3) | collective-permute-done | bytes 16416 | tf_op jit(solution)/shard_map/ppermute | solution.py:52
  19.3 0.0 copy-done.7
  19.3 0.0 copy-start
  19.3 0.0 copy-start.2
  19.4 0.0 copy-start.3
  19.4 0.0 copy-start.4
  19.4 5.1 %sweep.1.fs_ref = bf16[512,256]{1,0:T(8,128)(2,1)S(1)} custom-call(f32[512,256]{1,0:T(8,128)S(1)} %get-tuple-element.14.local_ref, bf16[32,256]{1,0:T(8,128)(2,1)S(1)} %collective-permute-done.i0, bf16[32,256]{1,0:T(8,128)(2,1)S(1)} %collective-permute-done.1.i1, bf16[32,256]{1,0:T(8,128)(2,1)S(1)} %collective-permute-done.2.i2, ...), custom_call_target="tpu_custom_call" | custom-call | tf_op jit(solution)/shard_map/sweep/pallas_call | solution.py:284
  24.4 5.6 %collective-permute-start.7 = (bf16[512,256]{1,0:T(8,128)(2,1)S(1)}, bf16[512,256]{1,0:T(8,128)(2,1)S(1)}, u32[]{:S(2)}, u32[]{:S(2)}) collective-permute-start(bf16[512,256]{1,0:T(8,128)(2,1)S(1)} %sweep.1.fs_ref), channel_id=1, source_target_pairs={{0,15},{1,2},{2,1},{3,4},{4,3},{5,6},{6,5},{7,8},{8,7},{9,10},{10,... | collective-permute-start | bytes 786440 | tf_op jit(solution)/shard_map/ppermute | solution.py:52
  30.0 0.0 collective-permute-start.6
  30.0 0.0 collective-permute-start.5
  30.0 1.5 %collective-permute-start.4 = (bf16[512,256]{1,0:T(8,128)(2,1)S(1)}, bf16[512,256]{1,0:T(8,128)(2,1)S(1)}, u32[]{:S(2)}, u32[]{:S(2)}) collective-permute-start(bf16[512,256]{1,0:T(8,128)(2,1)S(1)} %sweep.1.fs_ref), channel_id=1, source_target_pairs={{0,16},{1,17},{2,18},{3,19},{4,20},{5,21},{6,22},{7,23},{8,24},{9,... | collective-permute-start | bytes 786440 | tf_op jit(solution)/shard_map/ppermute | solution.py:52
  31.6 5.0 %collective-permute-done.7.h3 = bf16[512,256]{1,0:T(8,128)(2,1)S(1)} collective-permute-done((bf16[512,256]{1,0:T(8,128)(2,1)S(1)}, bf16[512,256]{1,0:T(8,128)(2,1)S(1)}, u32[]{:S(2)}, u32[]{:S(2)}) %collective-permute-start.7) | collective-permute-done | bytes 262176 | tf_op jit(solution)/shard_map/ppermute | solution.py:52
  36.6 1.5 %collective-permute-done.6.h2 = bf16[512,256]{1,0:T(8,128)(2,1)S(1)} collective-permute-done((bf16[512,256]{1,0:T(8,128)(2,1)S(1)}, bf16[512,256]{1,0:T(8,128)(2,1)S(1)}, u32[]{:S(2)}, u32[]{:S(2)}) %collective-permute-start.6) | collective-permute-done | bytes 262176 | tf_op jit(solution)/shard_map/ppermute | solution.py:52
  38.0 0.0 collective-permute-done.5.h1
  38.0 0.0 collective-permute-done.4.h0
  38.0 0.0 copy-done.1
  38.0 0.0 copy-done.5
  38.0 0.0 copy-done.6
  38.1 0.0 copy-done.8
  38.1 12.7 %couple.1 = (f32[512,256]{1,0:T(8,128)}, bf16[512,256]{1,0:T(8,128)(2,1)S(1)}, bf16[32,256]{1,0:T(8,128)(2,1)S(1)}, bf16[32,256]{1,0:T(8,128)(2,1)S(1)}, bf16[32...) custom-call(f32[16]{0:T(128)S(1)} %copy-done.8, bf16[512,256]{1,0:T(8,128)(2,1)S(1)} %sweep.1.fs_ref, ...), custom_call_target="tpu_custom_call" | custom-call | tf_op jit(solution)/shard_map/couple/pallas_call | solution.py:296
  50.7 0.0 collective-permute-start.8
  50.7 2.0 %collective-permute-start.9 = (bf16[32,256]{1,0:T(8,128)(2,1)S(1)}, bf16[32,256]{1,0:T(8,128)(2,1)S(1)}, u32[]{:S(2)}, u32[]{:S(2)}) collective-permute-start(bf16[32,256]{1,0:T(8,128)(2,1)S(1)} %get-tuple-element.23), channel_id=1, source_target_pairs={{0,112},{1,113},{2,114},{3,115},{4,116},{5,117},{6,118},{7,119},{8... | collective-permute-start | bytes 49160 | tf_op jit(solution)/shard_map/ppermute | solution.py:52
  52.7 2.0 %collective-permute-start.10 = (bf16[32,256]{1,0:T(8,128)(2,1)S(1)}, bf16[32,256]{1,0:T(8,128)(2,1)S(1)}, u32[]{:S(2)}, u32[]{:S(2)}) collective-permute-start(bf16[32,256]{1,0:T(8,128)(2,1)S(1)} %get-tuple-element.24), channel_id=1, source_target_pairs={{0,1},{1,0},{2,3},{3,2},{4,5},{5,4},{6,7},{7,6},{8,9},{9,8},{10,11... | collective-permute-start | bytes 49160 | tf_op jit(solution)/shard_map/ppermute | solution.py:52
  54.8 0.7 collective-permute-start.11
  55.4 0.0 collective-permute-done.8.r0
  55.4 0.0 collective-permute-done.9.r1
  55.4 1.0 %collective-permute-done.10.r2 = bf16[32,256]{1,0:T(8,128)(2,1)S(1)} collective-permute-done((bf16[32,256]{1,0:T(8,128)(2,1)S(1)}, bf16[32,256]{1,0:T(8,128)(2,1)S(1)}, u32[]{:S(2)}, u32[]{:S(2)}) %collective-permute-start.10) | collective-permute-done | bytes 16416 | tf_op jit(solution)/shard_map/ppermute | solution.py:52
  56.5 5.3 %collective-permute-done.11.r3 = bf16[32,256]{1,0:T(8,128)(2,1)S(1)} collective-permute-done((bf16[32,256]{1,0:T(8,128)(2,1)S(1)}, bf16[32,256]{1,0:T(8,128)(2,1)S(1)}, u32[]{:S(2)}, u32[]{:S(2)}) %collective-permute-start.11) | collective-permute-done | bytes 16416 | tf_op jit(solution)/shard_map/ppermute | solution.py:52
  61.8 0.0 copy-done
  61.8 0.0 copy-done.2
  61.8 0.0 copy-done.3
  61.8 0.0 copy-done.4
  61.8 9.2 %prolong.1 = bf16[4096,256]{1,0:T(8,128)(2,1)} custom-call(bf16[512,256]{1,0:T(8,128)(2,1)S(1)} %get-tuple-element.21.ans_ref, bf16[32,256]{1,0:T(8,128)(2,1)S(1)} %collective-permute-done.8.r0, bf16[32,256]{1,0:T(8,128)(2,1)S(1)} %collective-permute-done.9.r1, bf16[32,256]{1,0:T(8,128)(2,1)S(1)} %collective-permute-done.10.r2, ...), custom_call_target="tpu_custom_call" | custom-call | tf_op jit(solution)/shard_map/prolong/pallas_call | solution.py:310
Async XLA Ops:
  0.6 18.7 %copy-start.7 = (s32[4,32]{1,0:T(4,128)S(1)}, s32[4,32]{1,0:T(4,128)}, u32[]{:S(2)}) copy-start(s32[4,32]{1,0:T(4,128)} %ghost_ref.3) | copy-start | bytes 1540
  0.6 37.4 %copy-start.1 = (bf16[6,64,64]{2,1,0:T(8,128)(2,1)S(1)}, bf16[6,64,64]{2,1,0:T(8,128)(2,1)}, u32[]{:S(2)}) copy-start(bf16[6,64,64]{2,1,0:T(8,128)(2,1)} %face_ref.1) | copy-start | bytes 147460
  0.7 37.4 %copy-start.5 = (s32[6,512]{1,0:T(8,128)S(1)}, s32[6,512]{1,0:T(8,128)}, u32[]{:S(2)}) copy-start(s32[6,512]{1,0:T(8,128)} %nb_ref.1) | copy-start | bytes 36868
  0.7 37.4 %copy-start.6 = (s32[6,512]{1,0:T(8,128)S(1)}, s32[6,512]{1,0:T(8,128)}, u32[]{:S(2)}) copy-start(s32[6,512]{1,0:T(8,128)} %ci_ref.1) | copy-start | bytes 36868
  0.7 37.4 %copy-start.8 = (f32[16]{0:T(128)S(1)}, f32[16]{0:T(128)}, u32[]{:S(2)}) copy-start(f32[16]{0:T(128)} %coef_ref.1) | copy-start | bytes 196
  9.9 7.7 %collective-permute-start = (bf16[32,256]{1,0:T(8,128)(2,1)S(1)}, bf16[32,256]{1,0:T(8,128)(2,1)S(1)}, u32[]{:S(2)}, u32[]{:S(2)}) collective-permute-start(bf16[32,256]{1,0:T(8,128)(2,1)S(1)} %get-tuple-element.15), channel_id=1, source_target_pairs={{0,16},{1,17},{2,18},{3,19},{4,20},{5,21},{6,22},{7,23},{8,24},{9,... | collective-permute-start | bytes 49160 | tf_op jit(solution)/shard_map/ppermute | solution.py:52
  10.0 7.6 %collective-permute-start.1 = (bf16[32,256]{1,0:T(8,128)(2,1)S(1)}, bf16[32,256]{1,0:T(8,128)(2,1)S(1)}, u32[]{:S(2)}, u32[]{:S(2)}) collective-permute-start(bf16[32,256]{1,0:T(8,128)(2,1)S(1)} %get-tuple-element.16), channel_id=1, source_target_pairs={{0,112},{1,113},{2,114},{3,115},{4,116},{5,117},{6,118},{7,119},{8... | collective-permute-start | bytes 49160 | tf_op jit(solution)/shard_map/ppermute | solution.py:52
  10.5 7.2 %collective-permute-start.2 = (bf16[32,256]{1,0:T(8,128)(2,1)S(1)}, bf16[32,256]{1,0:T(8,128)(2,1)S(1)}, u32[]{:S(2)}, u32[]{:S(2)}) collective-permute-start(bf16[32,256]{1,0:T(8,128)(2,1)S(1)} %get-tuple-element.17), channel_id=1, source_target_pairs={{0,1},{1,0},{2,3},{3,2},{4,5},{5,4},{6,7},{7,6},{8,9},{9,8},{10,11... | collective-permute-start | bytes 49160 | tf_op jit(solution)/shard_map/ppermute | solution.py:52
  12.1 7.3 %collective-permute-start.3 = (bf16[32,256]{1,0:T(8,128)(2,1)S(1)}, bf16[32,256]{1,0:T(8,128)(2,1)S(1)}, u32[]{:S(2)}, u32[]{:S(2)}) collective-permute-start(bf16[32,256]{1,0:T(8,128)(2,1)S(1)} %get-tuple-element.18), channel_id=1, source_target_pairs={{0,15},{1,2},{2,1},{3,4},{4,3},{5,6},{6,5},{7,8},{8,7},{9,10},{10,... | collective-permute-start | bytes 49160 | tf_op jit(solution)/shard_map/ppermute | solution.py:52
  19.3 42.5 %copy-start = (bf16[8,64,64]{2,1,0:T(8,128)(2,1)S(1)}, bf16[8,64,64]{2,1,0:T(8,128)(2,1)}, u32[]{:S(2)}) copy-start(bf16[8,64,64]{2,1,0:T(8,128)(2,1)} %table_ref.3) | copy-start | bytes 196612
  19.3 42.5 %copy-start.2 = (s32[4096]{0:T(1024)S(1)}, s32[4096]{0:T(1024)}, u32[]{:S(2)}) copy-start(s32[4096]{0:T(1024)} %param.12) | copy-start | bytes 49156
  19.4 42.5 %copy-start.3 = (s32[4096]{0:T(1024)S(1)}, s32[4096]{0:T(1024)}, u32[]{:S(2)}) copy-start(s32[4096]{0:T(1024)} %param.13) | copy-start | bytes 49156
  19.4 42.5 %copy-start.4 = (s32[4096]{0:T(1024)S(1)}, s32[4096]{0:T(1024)}, u32[]{:S(2)}) copy-start(s32[4096]{0:T(1024)} %param.15) | copy-start | bytes 49156
  24.4 12.1 %collective-permute-start.7 = (bf16[512,256]{1,0:T(8,128)(2,1)S(1)}, bf16[512,256]{1,0:T(8,128)(2,1)S(1)}, u32[]{:S(2)}, u32[]{:S(2)}) collective-permute-start(bf16[512,256]{1,0:T(8,128)(2,1)S(1)} %sweep.1.fs_ref), channel_id=1, source_target_pairs={{0,15},{1,2},{2,1},{3,4},{4,3},{5,6},{6,5},{7,8},{8,7},{9,10},{10,... | collective-permute-start | bytes 786440 | tf_op jit(solution)/shard_map/ppermute | solution.py:52
  30.0 8.0 %collective-permute-start.6 = (bf16[512,256]{1,0:T(8,128)(2,1)S(1)}, bf16[512,256]{1,0:T(8,128)(2,1)S(1)}, u32[]{:S(2)}, u32[]{:S(2)}) collective-permute-start(bf16[512,256]{1,0:T(8,128)(2,1)S(1)} %sweep.1.fs_ref), channel_id=1, source_target_pairs={{0,1},{1,0},{2,3},{3,2},{4,5},{5,4},{6,7},{7,6},{8,9},{9,8},{10,11... | collective-permute-start | bytes 786440 | tf_op jit(solution)/shard_map/ppermute | solution.py:52
  30.0 8.0 %collective-permute-start.5 = (bf16[512,256]{1,0:T(8,128)(2,1)S(1)}, bf16[512,256]{1,0:T(8,128)(2,1)S(1)}, u32[]{:S(2)}, u32[]{:S(2)}) collective-permute-start(bf16[512,256]{1,0:T(8,128)(2,1)S(1)} %sweep.1.fs_ref), channel_id=1, source_target_pairs={{0,112},{1,113},{2,114},{3,115},{4,116},{5,117},{6,118},{7,119},{8... | collective-permute-start | bytes 786440 | tf_op jit(solution)/shard_map/ppermute | solution.py:52
  30.0 8.0 %collective-permute-start.4 = (bf16[512,256]{1,0:T(8,128)(2,1)S(1)}, bf16[512,256]{1,0:T(8,128)(2,1)S(1)}, u32[]{:S(2)}, u32[]{:S(2)}) collective-permute-start(bf16[512,256]{1,0:T(8,128)(2,1)S(1)} %sweep.1.fs_ref), channel_id=1, source_target_pairs={{0,16},{1,17},{2,18},{3,19},{4,20},{5,21},{6,22},{7,23},{8,24},{9,... | collective-permute-start | bytes 786440 | tf_op jit(solution)/shard_map/ppermute | solution.py:52
  50.7 4.7 %collective-permute-start.8 = (bf16[32,256]{1,0:T(8,128)(2,1)S(1)}, bf16[32,256]{1,0:T(8,128)(2,1)S(1)}, u32[]{:S(2)}, u32[]{:S(2)}) collective-permute-start(bf16[32,256]{1,0:T(8,128)(2,1)S(1)} %get-tuple-element.22), channel_id=1, source_target_pairs={{0,16},{1,17},{2,18},{3,19},{4,20},{5,21},{6,22},{7,23},{8,24},{9,... | collective-permute-start | bytes 49160 | tf_op jit(solution)/shard_map/ppermute | solution.py:52
  50.7 4.7 %collective-permute-start.9 = (bf16[32,256]{1,0:T(8,128)(2,1)S(1)}, bf16[32,256]{1,0:T(8,128)(2,1)S(1)}, u32[]{:S(2)}, u32[]{:S(2)}) collective-permute-start(bf16[32,256]{1,0:T(8,128)(2,1)S(1)} %get-tuple-element.23), channel_id=1, source_target_pairs={{0,112},{1,113},{2,114},{3,115},{4,116},{5,117},{6,118},{7,119},{8... | collective-permute-start | bytes 49160 | tf_op jit(solution)/shard_map/ppermute | solution.py:52
  52.7 3.8 %collective-permute-start.10 = (bf16[32,256]{1,0:T(8,128)(2,1)S(1)}, bf16[32,256]{1,0:T(8,128)(2,1)S(1)}, u32[]{:S(2)}, u32[]{:S(2)}) collective-permute-start(bf16[32,256]{1,0:T(8,128)(2,1)S(1)} %get-tuple-element.24), channel_id=1, source_target_pairs={{0,1},{1,0},{2,3},{3,2},{4,5},{5,4},{6,7},{7,6},{8,9},{9,8},{10,11... | collective-permute-start | bytes 49160 | tf_op jit(solution)/shard_map/ppermute | solution.py:52
  54.8 7.1 %collective-permute-start.11 = (bf16[32,256]{1,0:T(8,128)(2,1)S(1)}, bf16[32,256]{1,0:T(8,128)(2,1)S(1)}, u32[]{:S(2)}, u32[]{:S(2)}) collective-permute-start(bf16[32,256]{1,0:T(8,128)(2,1)S(1)} %get-tuple-element.25), channel_id=1, source_target_pairs={{0,15},{1,2},{2,1},{3,4},{4,3},{5,6},{6,5},{7,8},{8,7},{9,10},{10,... | collective-permute-start | bytes 49160 | tf_op jit(solution)/shard_map/ppermute | solution.py:52

commit v4 on v3

--- a/solution.py
+++ b/solution.py
@@ -1,3 +1,5 @@
+import functools
+
 import jax
 import jax.numpy as jnp
 from jax import lax
@@ -193,30 +195,39 @@
     out_ref[...] = apply_blocks(inv_ref, rhs.astype(bf16)).astype(bf16)
 
 
+def own_rows_kernel(fs_ref, nb_ref, face_ref, hits_ref, own_ref, faces_ref):
+    count = fs_ref.shape[0]
+    index_t = (nb_ref[...] % count).T
+    for f in range(FACES):
+        column = jnp.broadcast_to(index_t[:, f : f + 1], (count, LANES)).astype(i16)
+        hits = one_hot_columns(column, count)
+        rows = slice(f * count, (f + 1) * count)
+        hits_ref[rows, :] = hits
+        own_ref[rows, :] = jnp.dot(hits, fs_ref[...], preferred_element_type=f32).astype(bf16)
+        faces_ref[f * W : (f + 1) * W, :] = block_diagonal(face_ref[f], True)
+
+
 def couple_kernel(
-    coef_ref, fs_ref, h0, h1, h2, h3, nb_ref, ci_ref, face_ref, ghost_ref, inv_ref,
+    coef_ref, fs_ref, h0, h1, h2, h3, nb_ref, ci_ref, hits_ref, own_ref, faces_ref, ghost_ref, inv_ref,
     sol_ref, ans_ref, r0, r1, r2, r3,
 ):
     count = fs_ref.shape[0]
     own, even_x, even_y = position()
-    nb = nb_ref[...]
-    off = nb // count - own
-    block = jnp.where(off == 0, 0, 1 + partner(off, even_x, even_y))
-    index_t = (nb % count).T
-    block_t = block.T
-    scale = jnp.zeros(nb.shape, f32)
+    off = nb_ref[...] // count - own
+    block_t = jnp.where(off == 0, 0, 1 + partner(off, even_x, even_y)).T
+    scale = jnp.zeros(off.shape, f32)
     for k in range(KINDS):
         scale = jnp.where(ci_ref[...] == k, coef_ref[k], scale)
     scale_t = scale.T
     coupled = jnp.zeros((count, W), f32)
     for f in range(FACES):
-        column = jnp.broadcast_to(index_t[:, f : f + 1], (count, LANES)).astype(i16)
-        hits = one_hot_columns(column, count)
-        where = wide(jnp.broadcast_to(block_t[:, f : f + 1], (count, LANES)))
-        beside = jnp.dot(hits, fs_ref[...], preferred_element_type=f32)
+        rows = slice(f * count, (f + 1) * count)
+        where = wide(jnp.broadcast_to(block_t[:, f : f + 1], (count, LANES)).astype(i16))
+        beside = own_ref[rows, :]
         for q, source in enumerate((h0, h1, h2, h3)):
-            beside = jnp.where(where == q + 1, jnp.dot(hits, source[...], preferred_element_type=f32), beside)
-        term = jnp.dot(beside.astype(bf16), block_diagonal(face_ref[f], True), preferred_element_type=f32)
+            found = jnp.dot(hits_ref[rows, :], source[...], preferred_element_type=f32).astype(bf16)
+            beside = jnp.where(where == jnp.asarray(q + 1, i16), found, beside)
+        term = jnp.dot(beside, faces_ref[f * W : (f + 1) * W, :], preferred_element_type=f32)
         coupled = coupled + term * wide(jnp.broadcast_to(scale_t[:, f : f + 1], (count, LANES)))
     correction = apply_blocks(inv_ref, coupled.astype(bf16))
     solution_rows = fs_ref[...].astype(f32) - OMEGA * correction
@@ -229,22 +240,26 @@
         out[...] = replies[q * GHOST : (q + 1) * GHOST, :]
 
 
-def prolong_kernel(ans_ref, r0, r1, r2, r3, dest_ref, slot_ref, type_ref, table_ref, out_ref, w_ref, t_ref):
+def fetch_kernel(ans_ref, dest_ref, slot_ref, table_ref, out_ref, w_ref):
+    count = ans_ref.shape[0]
+    for t in range(NTYPE):
+        w_ref[t * W : (t + 1) * W, :] = block_diagonal(table_ref[t], False)
+    target = targets(dest_ref[...], slot_ref[...], count)
+    for g in range(out_ref.shape[0] // CHUNK):
+        column = columns(target[g * (CHUNK // LANES) : (g + 1) * (CHUNK // LANES), :])
+        for r in range(0, CHUNK, PB):
+            hits = one_hot_columns(column[r : r + PB, :], count)
+            first = g * CHUNK + r
+            out_ref[first : first + PB, :] = jnp.dot(hits, ans_ref[...], preferred_element_type=f32).astype(bf16)
+
+
+def prolong_kernel(count, local_ref, r0, r1, r2, r3, w_ref, dest_ref, slot_ref, type_ref, out_ref):
     step = pl.program_id(0)
-    rows_in = t_ref.shape[0]
-    coarse_count = rows_in - 4 * GHOST
-
-    @pl.when(step == 0)
-    def _():
-        for t in range(NTYPE):
-            w_ref[t * W : (t + 1) * W, :] = block_diagonal(table_ref[t], False)
-        t_ref[:coarse_count, :] = ans_ref[...]
-        for q, r in enumerate((r0, r1, r2, r3)):
-            first = coarse_count + q * GHOST
-            t_ref[first : first + GHOST, :] = r[...]
-
-    target = columns(targets(dest_ref[...], slot_ref[...], coarse_count))
-    fetched = jnp.dot(one_hot_columns(target, rows_in), t_ref[...], preferred_element_type=f32).astype(bf16)
+    target = columns(targets(dest_ref[...], slot_ref[...], count) - count)
+    returned = jnp.concatenate([r0[...], r1[...], r2[...], r3[...]], axis=0)
+    remote = jnp.dot(one_hot_columns(target, 4 * GHOST), returned, preferred_element_type=f32)
+    local = local_ref[pl.ds(pl.multiple_of(step * CHUNK, CHUNK), CHUNK), :]
+    fetched = (local.astype(f32) + remote).astype(bf16)
     out_ref[...] = typed(fetched, columns(type_ref[...]), w_ref[...], PB)
 
 
@@ -291,32 +306,56 @@
     )(local, *incoming, ghost, inverse)
 
 
-def couple(coef, first_sweep, halo, neighbours, coef_index, face_table, ghost, inverse):
+def own_rows(first_sweep, neighbours, face_table):
     count = first_sweep.shape[0]
     return pl.pallas_call(
+        own_rows_kernel,
+        in_specs=[VMEM] * 3,
+        out_specs=[VMEM] * 3,
+        out_shape=[
+            pltpu.VMEM((FACES * count, count), bf16), pltpu.VMEM((FACES * count, W), bf16), pltpu.VMEM((FACES * W, W), bf16)
+        ],
+        compiler_params=pltpu.CompilerParams(vmem_limit_bytes=VMEM_BYTES),
+        name="own_rows",
+    )(first_sweep, neighbours, face_table)
+
+
+def couple(coef, first_sweep, halo, neighbours, coef_index, prepared, ghost, inverse):
+    count = first_sweep.shape[0]
+    return pl.pallas_call(
         couple_kernel,
-        in_specs=[pl.BlockSpec(memory_space=pltpu.SMEM)] + [VMEM] * 10,
+        in_specs=[pl.BlockSpec(memory_space=pltpu.SMEM)] + [VMEM] * 12,
         out_specs=[VMEM] * 6,
         out_shape=[jax.ShapeDtypeStruct((count, W), f32), pltpu.VMEM((count, W), bf16)] + ghost_shape(),
         compiler_params=pltpu.CompilerParams(vmem_limit_bytes=VMEM_BYTES),
         name="couple",
-    )(coef, first_sweep, *halo, neighbours, coef_index, face_table, ghost, inverse)
-
-
-def prolong(answer, returned, meta, table, fine_count):
-    count = answer.shape[0]
-    rows = count + 4 * GHOST
+    )(coef, first_sweep, *halo, neighbours, coef_index, *prepared, ghost, inverse)
+
+
+def fetch(answer, meta, table):
+    fine_count = meta[0].shape[0] * LANES
+    return pl.pallas_call(
+        fetch_kernel,
+        in_specs=[VMEM] * 4,
+        out_specs=[VMEM] * 2,
+        out_shape=[pltpu.VMEM((fine_count, W), bf16), pltpu.VMEM((NTYPE * W, W), bf16)],
+        compiler_params=pltpu.CompilerParams(vmem_limit_bytes=VMEM_BYTES),
+        name="fetch",
+    )(answer, meta[0], meta[1], table)
+
+
+def prolong(local, returned, table, meta, count):
+    fine_count = local.shape[0]
     meta_spec = pl.BlockSpec((CHUNK // LANES, LANES), lambda i: (i, 0))
     return pl.pallas_call(
-        prolong_kernel,
+        functools.partial(prolong_kernel, count),
         grid=(fine_count // CHUNK,),
-        in_specs=[VMEM] * 5 + [meta_spec, meta_spec, meta_spec, whole(table.shape)],
+        in_specs=[VMEM] * 6 + [meta_spec, meta_spec, meta_spec],
         out_specs=pl.BlockSpec((CHUNK, W), lambda i: (i, 0)),
         out_shape=jax.ShapeDtypeStruct((fine_count, W), bf16),
-        scratch_shapes=[pltpu.VMEM((NTYPE * W, W), bf16), pltpu.VMEM((rows, W), bf16)],
         compiler_params=pltpu.CompilerParams(vmem_limit_bytes=VMEM_BYTES),
         name="prolong",
-    )(answer, *returned, *meta, table)
+    )(local, *returned, table, *meta)
 
 
 def shards(
@@ -332,11 +371,13 @@
     incoming = exchange(outgoing, perms)
     first_sweep = sweep(local, incoming, ghost_slot, inverse)
     halo = exchange([first_sweep] * 4, perms)
+    prepared = own_rows(first_sweep, neighbours, face_table)
     coarse_solution, answer, *replies = couple(
-        face_coef, first_sweep, halo, neighbours, coef_index, face_table, ghost_slot, inverse
+        face_coef, first_sweep, halo, neighbours, coef_index, prepared, ghost_slot, inverse
     )
     returned = exchange(replies, perms)
-    fine_correction = prolong(answer, returned, meta, restrict_table, fine_count)
+    fetched, table = fetch(answer, meta, restrict_table)
+    fine_correction = prolong(fetched, returned, table, meta, inverse_blocks.shape[0])
     return (coarse_solution, fine_correction)
 
 

time: 71.2 us -> 67.7 us (0.951)
  waiting for transfers between devices: 14.6 us -> 10.4 us
    ppermute x12, waiting for transfers between devices: 14.6 us -> 10.4 us  [exchange(): lax.ppermute(x, ('px', 'py'), perm)]
    pallas_call x1 -> x3, Pallas kernels: 9.24 us -> 11.8 us  [the longest x1 7.78 us: prolong(): pl.pallas_call(functools.partial(prolong_kernel, count), grid=(fine_count...]
    pallas_call x1, Pallas kernels: 12.7 us -> 10.7 us  [couple(): pl.pallas_call(couple_kernel, in_specs=[pl.BlockSpec(memory_space=pltpu.S...]
  transfers between devices with their start and end apart: 12 -> 12, of which waited for: 5 -> 4; matrix products, arithmetic and copies ran while one was open for 0% -> 0% of each run, Pallas kernels for 0% -> 6%
where the time goes in v4:
time: 67.7 us; the launch traced here: 67.6 us
  Pallas kernels  36.8 us (54%)
  starting transfers between devices  19.5 us (29%)
  waiting for transfers between devices  10.4 us (15%)
  between operations  0.77 us (1%)
    ppermute x12, starting transfers between devices, exchange(): lax.ppermute(x, ('px', 'py'), perm)  19.5 us
    pallas_call x1, Pallas kernels, couple(): pl.pallas_call(couple_kernel, in_specs=[pl.BlockSpec(memory_space=pltpu.S...  10.7 us
    ppermute x12, waiting for transfers between devices, exchange(): lax.ppermute(x, ('px', 'py'), perm)  10.4 us
    pallas_call x1, Pallas kernels, restrict(): pl.pallas_call(restrict_kernel, grid=(steps,), in_specs=[pl.BlockSpec((CH...  9.2 us
    pallas_call x1, Pallas kernels, prolong(): pl.pallas_call(functools.partial(prolong_kernel, count), grid=(fine_count...  7.78 us
    pallas_call x1, Pallas kernels, sweep(): pl.pallas_call(sweep_kernel, in_specs=[VMEM] * 7, out_specs=VMEM, out_sha...  5.07 us
    pallas_call x1, Pallas kernels, fetch(): pl.pallas_call(fetch_kernel, in_specs=[VMEM] * 4, out_specs=[VMEM] * 2, o...  2.18 us
    pallas_call x1, Pallas kernels, own_rows(): pl.pallas_call(own_rows_kernel, in_specs=[VMEM] * 3, out_specs=[VMEM] * 3...  1.88 us
  transfers between devices with their start and end apart: 12, of which 4 were waited for; matrix products, arithmetic and copies ran while one was open for 0% of the time, Pallas kernels for 6%

profile of v4, /device:TPU:8, one launch (start us, length us, event | category | flops | bytes accessed | tf_op | source)
XLA Modules:
  0.0 67.6 jit_solution(6757546548716780873)
XLA Ops:
  0.6 0.0 copy-start.7
  0.6 9.2 %restrict.1 = (f32[512,256]{1,0:T(8,128)S(1)}, bf16[32,256]{1,0:T(8,128)(2,1)S(1)}, bf16[32,256]{1,0:T(8,128)(2,1)S(1)}, bf16[32,256]{1,0:T(8,128)(2,1)S(1)}, bf...) custom-call(bf16[4096,256]{1,0:T(8,128)(2,1)} %x_ref.1, s32[32,128]{1,0:T(8,128)} %bitcast.3, s32[32,128]{1,0:T(8,128)} %bitcast.6, ...), custom_call_target="tpu_custom_call" | custom-call | tf_op jit(solution)/shard_map/restrict/pallas_call | solution.py:286
  9.8 0.1 collective-permute-start
  9.9 0.4 collective-permute-start.1
  10.4 1.6 %collective-permute-start.2 = (bf16[32,256]{1,0:T(8,128)(2,1)S(1)}, bf16[32,256]{1,0:T(8,128)(2,1)S(1)}, u32[]{:S(2)}, u32[]{:S(2)}) collective-permute-start(bf16[32,256]{1,0:T(8,128)(2,1)S(1)} %get-tuple-element.22), channel_id=1, source_target_pairs={{0,1},{1,0},{2,3},{3,2},{4,5},{5,4},{6,7},{7,6},{8,9},{9,8},{10,11... | collective-permute-start | bytes 49160 | tf_op jit(solution)/shard_map/ppermute | solution.py:54
  12.0 5.6 %collective-permute-start.3 = (bf16[32,256]{1,0:T(8,128)(2,1)S(1)}, bf16[32,256]{1,0:T(8,128)(2,1)S(1)}, u32[]{:S(2)}, u32[]{:S(2)}) collective-permute-start(bf16[32,256]{1,0:T(8,128)(2,1)S(1)} %get-tuple-element.23), channel_id=1, source_target_pairs={{0,15},{1,2},{2,1},{3,4},{4,3},{5,6},{6,5},{7,8},{8,7},{9,10},{10,... | collective-permute-start | bytes 49160 | tf_op jit(solution)/shard_map/ppermute | solution.py:54
  17.6 0.0 collective-permute-done.i0
  17.6 0.0 collective-permute-done.1.i1
  17.6 0.0 collective-permute-done.2.i2
  17.6 1.7 %collective-permute-done.3.i3 = bf16[32,256]{1,0:T(8,128)(2,1)S(1)} collective-permute-done((bf16[32,256]{1,0:T(8,128)(2,1)S(1)}, bf16[32,256]{1,0:T(8,128)(2,1)S(1)}, u32[]{:S(2)}, u32[]{:S(2)}) %collective-permute-start.3) | collective-permute-done | bytes 16416 | tf_op jit(solution)/shard_map/ppermute | solution.py:54
  19.3 0.0 copy-done.7
  19.3 0.0 copy-start.3
  19.3 0.0 copy-start.5
  19.3 0.0 copy-start.6
  19.3 0.0 copy-start.8
  19.3 5.1 %sweep.1.fs_ref = bf16[512,256]{1,0:T(8,128)(2,1)S(1)} custom-call(f32[512,256]{1,0:T(8,128)S(1)} %get-tuple-element.19.local_ref, bf16[32,256]{1,0:T(8,128)(2,1)S(1)} %collective-permute-done.i0, bf16[32,256]{1,0:T(8,128)(2,1)S(1)} %collective-permute-done.1.i1, bf16[32,256]{1,0:T(8,128)(2,1)S(1)} %collective-permute-done.2.i2, ...), custom_call_target="tpu_custom_call" | custom-call | tf_op jit(solution)/shard_map/sweep/pallas_call | solution.py:299
  24.4 5.6 %collective-permute-start.7 = (bf16[512,256]{1,0:T(8,128)(2,1)S(1)}, bf16[512,256]{1,0:T(8,128)(2,1)S(1)}, u32[]{:S(2)}, u32[]{:S(2)}) collective-permute-start(bf16[512,256]{1,0:T(8,128)(2,1)S(1)} %sweep.1.fs_ref), channel_id=1, source_target_pairs={{0,15},{1,2},{2,1},{3,4},{4,3},{5,6},{6,5},{7,8},{8,7},{9,10},{10,... | collective-permute-start | bytes 786440 | tf_op jit(solution)/shard_map/ppermute | solution.py:54
  29.9 0.0 collective-permute-start.6
  29.9 0.0 collective-permute-start.5
  29.9 1.5 %collective-permute-start.4 = (bf16[512,256]{1,0:T(8,128)(2,1)S(1)}, bf16[512,256]{1,0:T(8,128)(2,1)S(1)}, u32[]{:S(2)}, u32[]{:S(2)}) collective-permute-start(bf16[512,256]{1,0:T(8,128)(2,1)S(1)} %sweep.1.fs_ref), channel_id=1, source_target_pairs={{0,16},{1,17},{2,18},{3,19},{4,20},{5,21},{6,22},{7,23},{8,24},{9,... | collective-permute-start | bytes 786440 | tf_op jit(solution)/shard_map/ppermute | solution.py:54
  31.5 0.0 copy-done.3
  31.5 0.0 copy-done.5
  31.5 1.9 %own_rows.1 = (bf16[3072,512]{1,0:T(8,128)(2,1)S(1)}, bf16[3072,256]{1,0:T(8,128)(2,1)S(1)}, bf16[1536,256]{1,0:T(8,128)(2,1)S(1)}) custom-call(bf16[512,256]{1,0:T(8,128)(2,1)S(1)} %sweep.1.fs_ref, s32[6,512]{1,0:T(8,128)S(1)} %copy-done.5, bf16[6,64,64]{2,1,0:T(8,128)(2,1)S(1)} %copy-done.3), custom_call_target="tpu_custom_call" | custom-call | tf_op jit(solution)/shard_map/own_rows/pallas_call | solution.py:311
  33.4 3.1 %collective-permute-done.7.h3 = bf16[512,256]{1,0:T(8,128)(2,1)S(1)} collective-permute-done((bf16[512,256]{1,0:T(8,128)(2,1)S(1)}, bf16[512,256]{1,0:T(8,128)(2,1)S(1)}, u32[]{:S(2)}, u32[]{:S(2)}) %collective-permute-start.7) | collective-permute-done | bytes 262176 | tf_op jit(solution)/shard_map/ppermute | solution.py:54
  36.5 1.5 %collective-permute-done.6.h2 = bf16[512,256]{1,0:T(8,128)(2,1)S(1)} collective-permute-done((bf16[512,256]{1,0:T(8,128)(2,1)S(1)}, bf16[512,256]{1,0:T(8,128)(2,1)S(1)}, u32[]{:S(2)}, u32[]{:S(2)}) %collective-permute-start.6) | collective-permute-done | bytes 262176 | tf_op jit(solution)/shard_map/ppermute | solution.py:54
  37.9 0.0 collective-permute-done.5.h1
  37.9 0.0 collective-permute-done.4.h0
  38.0 0.0 copy-done.6
  38.0 0.0 copy-done.8
  38.0 0.0 copy-start
  38.0 0.0 copy-start.1
  38.0 0.0 copy-start.2
  38.0 0.0 copy-start.4
  38.0 10.7 %couple.1 = (f32[512,256]{1,0:T(8,128)}, bf16[512,256]{1,0:T(8,128)(2,1)S(1)}, bf16[32,256]{1,0:T(8,128)(2,1)S(1)}, bf16[32,256]{1,0:T(8,128)(2,1)S(1)}, bf16[32...) custom-call(f32[16]{0:T(128)S(1)} %copy-done.8, bf16[512,256]{1,0:T(8,128)(2,1)S(1)} %sweep.1.fs_ref, ...), custom_call_target="tpu_custom_call" | custom-call | tf_op jit(solution)/shard_map/couple/pallas_call | solution.py:325
  48.8 0.0 collective-permute-start.8
  48.8 2.0 %collective-permute-start.9 = (bf16[32,256]{1,0:T(8,128)(2,1)S(1)}, bf16[32,256]{1,0:T(8,128)(2,1)S(1)}, u32[]{:S(2)}, u32[]{:S(2)}) collective-permute-start(bf16[32,256]{1,0:T(8,128)(2,1)S(1)} %get-tuple-element.32), channel_id=1, source_target_pairs={{0,112},{1,113},{2,114},{3,115},{4,116},{5,117},{6,118},{7,119},{8... | collective-permute-start | bytes 49160 | tf_op jit(solution)/shard_map/ppermute | solution.py:54
  50.7 2.0 %collective-permute-start.10 = (bf16[32,256]{1,0:T(8,128)(2,1)S(1)}, bf16[32,256]{1,0:T(8,128)(2,1)S(1)}, u32[]{:S(2)}, u32[]{:S(2)}) collective-permute-start(bf16[32,256]{1,0:T(8,128)(2,1)S(1)} %get-tuple-element.33), channel_id=1, source_target_pairs={{0,1},{1,0},{2,3},{3,2},{4,5},{5,4},{6,7},{7,6},{8,9},{9,8},{10,11... | collective-permute-start | bytes 49160 | tf_op jit(solution)/shard_map/ppermute | solution.py:54
  52.8 0.7 %collective-permute-start.11 = (bf16[32,256]{1,0:T(8,128)(2,1)S(1)}, bf16[32,256]{1,0:T(8,128)(2,1)S(1)}, u32[]{:S(2)}, u32[]{:S(2)}) collective-permute-start(bf16[32,256]{1,0:T(8,128)(2,1)S(1)} %get-tuple-element.34), channel_id=1, source_target_pairs={{0,15},{1,2},{2,1},{3,4},{4,3},{5,6},{6,5},{7,8},{8,7},{9,10},{10,... | collective-permute-start | bytes 49160 | tf_op jit(solution)/shard_map/ppermute | solution.py:54
  53.4 0.0 copy-done
  53.5 0.0 copy-done.1
  53.5 0.0 copy-done.2
  53.5 2.2 %fetch.1 = (bf16[4096,256]{1,0:T(8,128)(2,1)S(1)}, bf16[2048,256]{1,0:T(8,128)(2,1)S(1)}) custom-call(bf16[512,256]{1,0:T(8,128)(2,1)S(1)} %get-tuple-element.29.ans_ref, s32[32,128]{1,0:T(8,128)S(1)} %bitcast.4, s32[32,128]{1,0:T(8,128)S(1)} %bitcast.7, bf16[8,64,64]{2,1,0:T(8,128)(2,1)S(1)} %copy-done), custom_call_target="tpu_custom_call" | custom-call | tf_op jit(solution)/shard_map/fetch/pallas_call | solution.py:337
  55.6 0.0 collective-permute-done.8.r0
  55.6 0.0 collective-permute-done.9.r1
  55.7 0.0 collective-permute-done.10.r2
  55.7 4.2 %collective-permute-done.11.r3 = bf16[32,256]{1,0:T(8,128)(2,1)S(1)} collective-permute-done((bf16[32,256]{1,0:T(8,128)(2,1)S(1)}, bf16[32,256]{1,0:T(8,128)(2,1)S(1)}, u32[]{:S(2)}, u32[]{:S(2)}) %collective-permute-start.11) | collective-permute-done | bytes 16416 | tf_op jit(solution)/shard_map/ppermute | solution.py:54
  59.8 0.0 copy-done.4
  59.8 7.8 %prolong.1 = bf16[4096,256]{1,0:T(8,128)(2,1)} custom-call(bf16[4096,256]{1,0:T(8,128)(2,1)S(1)} %get-tuple-element.30.local_ref, bf16[32,256]{1,0:T(8,128)(2,1)S(1)} %collective-permute-done.8.r0, bf16[32,256]{1,0:T(8,128)(2,1)S(1)} %collective-permute-done.9.r1, bf16[32,256]{1,0:T(8,128)(2,1)S(1)} %collective-permute-done.10.r2, ...), custom_call_target="tpu_custom_call" | custom-call | tf_op jit(solution)/shard_map/prolong/pallas_call | solution.py:350
Async XLA Ops:
  0.6 18.6 %copy-start.7 = (s32[4,32]{1,0:T(4,128)S(1)}, s32[4,32]{1,0:T(4,128)}, u32[]{:S(2)}) copy-start(s32[4,32]{1,0:T(4,128)} %ghost_ref.3) | copy-start | bytes 1540
  9.8 7.7 %collective-permute-start = (bf16[32,256]{1,0:T(8,128)(2,1)S(1)}, bf16[32,256]{1,0:T(8,128)(2,1)S(1)}, u32[]{:S(2)}, u32[]{:S(2)}) collective-permute-start(bf16[32,256]{1,0:T(8,128)(2,1)S(1)} %get-tuple-element.20), channel_id=1, source_target_pairs={{0,16},{1,17},{2,18},{3,19},{4,20},{5,21},{6,22},{7,23},{8,24},{9,... | collective-permute-start | bytes 49160 | tf_op jit(solution)/shard_map/ppermute | solution.py:54
  9.9 7.6 %collective-permute-start.1 = (bf16[32,256]{1,0:T(8,128)(2,1)S(1)}, bf16[32,256]{1,0:T(8,128)(2,1)S(1)}, u32[]{:S(2)}, u32[]{:S(2)}) collective-permute-start(bf16[32,256]{1,0:T(8,128)(2,1)S(1)} %get-tuple-element.21), channel_id=1, source_target_pairs={{0,112},{1,113},{2,114},{3,115},{4,116},{5,117},{6,118},{7,119},{8... | collective-permute-start | bytes 49160 | tf_op jit(solution)/shard_map/ppermute | solution.py:54
  10.4 7.2 %collective-permute-start.2 = (bf16[32,256]{1,0:T(8,128)(2,1)S(1)}, bf16[32,256]{1,0:T(8,128)(2,1)S(1)}, u32[]{:S(2)}, u32[]{:S(2)}) collective-permute-start(bf16[32,256]{1,0:T(8,128)(2,1)S(1)} %get-tuple-element.22), channel_id=1, source_target_pairs={{0,1},{1,0},{2,3},{3,2},{4,5},{5,4},{6,7},{7,6},{8,9},{9,8},{10,11... | collective-permute-start | bytes 49160 | tf_op jit(solution)/shard_map/ppermute | solution.py:54
  12.0 7.3 %collective-permute-start.3 = (bf16[32,256]{1,0:T(8,128)(2,1)S(1)}, bf16[32,256]{1,0:T(8,128)(2,1)S(1)}, u32[]{:S(2)}, u32[]{:S(2)}) collective-permute-start(bf16[32,256]{1,0:T(8,128)(2,1)S(1)} %get-tuple-element.23), channel_id=1, source_target_pairs={{0,15},{1,2},{2,1},{3,4},{4,3},{5,6},{6,5},{7,8},{8,7},{9,10},{10,... | collective-permute-start | bytes 49160 | tf_op jit(solution)/shard_map/ppermute | solution.py:54
  19.3 12.2 %copy-start.3 = (bf16[6,64,64]{2,1,0:T(8,128)(2,1)S(1)}, bf16[6,64,64]{2,1,0:T(8,128)(2,1)}, u32[]{:S(2)}) copy-start(bf16[6,64,64]{2,1,0:T(8,128)(2,1)} %face_ref.1) | copy-start | bytes 147460
  19.3 12.2 %copy-start.5 = (s32[6,512]{1,0:T(8,128)S(1)}, s32[6,512]{1,0:T(8,128)}, u32[]{:S(2)}) copy-start(s32[6,512]{1,0:T(8,128)} %nb_ref.3) | copy-start | bytes 36868
  19.3 18.7 %copy-start.6 = (s32[6,512]{1,0:T(8,128)S(1)}, s32[6,512]{1,0:T(8,128)}, u32[]{:S(2)}) copy-start(s32[6,512]{1,0:T(8,128)} %ci_ref.1) | copy-start | bytes 36868
  19.3 18.7 %copy-start.8 = (f32[16]{0:T(128)S(1)}, f32[16]{0:T(128)}, u32[]{:S(2)}) copy-start(f32[16]{0:T(128)} %coef_ref.1) | copy-start | bytes 196
  24.4 12.1 %collective-permute-start.7 = (bf16[512,256]{1,0:T(8,128)(2,1)S(1)}, bf16[512,256]{1,0:T(8,128)(2,1)S(1)}, u32[]{:S(2)}, u32[]{:S(2)}) collective-permute-start(bf16[512,256]{1,0:T(8,128)(2,1)S(1)} %sweep.1.fs_ref), channel_id=1, source_target_pairs={{0,15},{1,2},{2,1},{3,4},{4,3},{5,6},{6,5},{7,8},{8,7},{9,10},{10,... | collective-permute-start | bytes 786440 | tf_op jit(solution)/shard_map/ppermute | solution.py:54
  29.9 8.0 %collective-permute-start.6 = (bf16[512,256]{1,0:T(8,128)(2,1)S(1)}, bf16[512,256]{1,0:T(8,128)(2,1)S(1)}, u32[]{:S(2)}, u32[]{:S(2)}) collective-permute-start(bf16[512,256]{1,0:T(8,128)(2,1)S(1)} %sweep.1.fs_ref), channel_id=1, source_target_pairs={{0,1},{1,0},{2,3},{3,2},{4,5},{5,4},{6,7},{7,6},{8,9},{9,8},{10,11... | collective-permute-start | bytes 786440 | tf_op jit(solution)/shard_map/ppermute | solution.py:54
  29.9 8.0 %collective-permute-start.5 = (bf16[512,256]{1,0:T(8,128)(2,1)S(1)}, bf16[512,256]{1,0:T(8,128)(2,1)S(1)}, u32[]{:S(2)}, u32[]{:S(2)}) collective-permute-start(bf16[512,256]{1,0:T(8,128)(2,1)S(1)} %sweep.1.fs_ref), channel_id=1, source_target_pairs={{0,112},{1,113},{2,114},{3,115},{4,116},{5,117},{6,118},{7,119},{8... | collective-permute-start | bytes 786440 | tf_op jit(solution)/shard_map/ppermute | solution.py:54
  29.9 8.0 %collective-permute-start.4 = (bf16[512,256]{1,0:T(8,128)(2,1)S(1)}, bf16[512,256]{1,0:T(8,128)(2,1)S(1)}, u32[]{:S(2)}, u32[]{:S(2)}) collective-permute-start(bf16[512,256]{1,0:T(8,128)(2,1)S(1)} %sweep.1.fs_ref), channel_id=1, source_target_pairs={{0,16},{1,17},{2,18},{3,19},{4,20},{5,21},{6,22},{7,23},{8,24},{9,... | collective-permute-start | bytes 786440 | tf_op jit(solution)/shard_map/ppermute | solution.py:54
  38.0 15.5 %copy-start = (bf16[8,64,64]{2,1,0:T(8,128)(2,1)S(1)}, bf16[8,64,64]{2,1,0:T(8,128)(2,1)}, u32[]{:S(2)}) copy-start(bf16[8,64,64]{2,1,0:T(8,128)(2,1)} %table_ref.3) | copy-start | bytes 196612
  38.0 15.5 %copy-start.1 = (s32[4096]{0:T(1024)S(1)}, s32[4096]{0:T(1024)}, u32[]{:S(2)}) copy-start(s32[4096]{0:T(1024)} %param.12) | copy-start | bytes 49156
  38.0 15.5 %copy-start.2 = (s32[4096]{0:T(1024)S(1)}, s32[4096]{0:T(1024)}, u32[]{:S(2)}) copy-start(s32[4096]{0:T(1024)} %param.13) | copy-start | bytes 49156
  38.0 21.8 %copy-start.4 = (s32[4096]{0:T(1024)S(1)}, s32[4096]{0:T(1024)}, u32[]{:S(2)}) copy-start(s32[4096]{0:T(1024)} %param.15) | copy-start | bytes 49156
  48.8 6.9 %collective-permute-start.8 = (bf16[32,256]{1,0:T(8,128)(2,1)S(1)}, bf16[32,256]{1,0:T(8,128)(2,1)S(1)}, u32[]{:S(2)}, u32[]{:S(2)}) collective-permute-start(bf16[32,256]{1,0:T(8,128)(2,1)S(1)} %get-tuple-element.31), channel_id=1, source_target_pairs={{0,16},{1,17},{2,18},{3,19},{4,20},{5,21},{6,22},{7,23},{8,24},{9,... | collective-permute-start | bytes 49160 | tf_op jit(solution)/shard_map/ppermute | solution.py:54
  48.8 6.9 %collective-permute-start.9 = (bf16[32,256]{1,0:T(8,128)(2,1)S(1)}, bf16[32,256]{1,0:T(8,128)(2,1)S(1)}, u32[]{:S(2)}, u32[]{:S(2)}) collective-permute-start(bf16[32,256]{1,0:T(8,128)(2,1)S(1)} %get-tuple-element.32), channel_id=1, source_target_pairs={{0,112},{1,113},{2,114},{3,115},{4,116},{5,117},{6,118},{7,119},{8... | collective-permute-start | bytes 49160 | tf_op jit(solution)/shard_map/ppermute | solution.py:54
  50.7 4.9 %collective-permute-start.10 = (bf16[32,256]{1,0:T(8,128)(2,1)S(1)}, bf16[32,256]{1,0:T(8,128)(2,1)S(1)}, u32[]{:S(2)}, u32[]{:S(2)}) collective-permute-start(bf16[32,256]{1,0:T(8,128)(2,1)S(1)} %get-tuple-element.33), channel_id=1, source_target_pairs={{0,1},{1,0},{2,3},{3,2},{4,5},{5,4},{6,7},{7,6},{8,9},{9,8},{10,11... | collective-permute-start | bytes 49160 | tf_op jit(solution)/shard_map/ppermute | solution.py:54
  52.8 7.1 %collective-permute-start.11 = (bf16[32,256]{1,0:T(8,128)(2,1)S(1)}, bf16[32,256]{1,0:T(8,128)(2,1)S(1)}, u32[]{:S(2)}, u32[]{:S(2)}) collective-permute-start(bf16[32,256]{1,0:T(8,128)(2,1)S(1)} %get-tuple-element.34), channel_id=1, source_target_pairs={{0,15},{1,2},{2,1},{3,4},{4,3},{5,6},{6,5},{7,8},{8,7},{9,10},{10,... | collective-permute-start | bytes 49160 | tf_op jit(solution)/shard_map/ppermute | solution.py:54

commit v5 on v4

--- a/solution.py
+++ b/solution.py
@@ -140,11 +140,10 @@
 
 
 def restrict_kernel(
-    x_ref, dest_ref, slot_ref, type_ref, table_ref, inv_hbm, local_ref, g0, g1, g2, g3, inv_ref, w_ref, acc_ref, sem
+    x_ref, dest_ref, slot_ref, type_ref, table_ref, inv_hbm, contrib_ref, g0, g1, g2, g3, inv_ref, w_ref, acc_ref, sem
 ):
     step = pl.program_id(0)
-    rows_out = acc_ref.shape[0]
-    coarse_count = rows_out - 4 * GHOST
+    coarse_count = inv_ref.shape[0]
 
     load = pltpu.make_async_copy(inv_hbm, inv_ref, sem)
 
@@ -156,16 +155,26 @@
         acc_ref[...] = jnp.zeros_like(acc_ref)
 
     contrib = typed(x_ref[...], columns(type_ref[...]), w_ref[...], RB)
-    hits = one_hot_rows(targets(dest_ref[...], slot_ref[...], coarse_count), rows_out)
-    acc_ref[...] += jnp.dot(hits, contrib, preferred_element_type=f32)
+    contrib_ref[pl.ds(pl.multiple_of(step * CHUNK, CHUNK), CHUNK), :] = contrib
+    remote = targets(dest_ref[...], slot_ref[...], coarse_count) - coarse_count
+    acc_ref[...] += jnp.dot(one_hot_rows(remote, 4 * GHOST), contrib, preferred_element_type=f32)
 
     @pl.when(step == pl.num_programs(0) - 1)
     def _():
-        local_ref[...] = acc_ref[:coarse_count, :]
         for q, out in enumerate((g0, g1, g2, g3)):
-            first = coarse_count + q * GHOST
-            out[...] = acc_ref[first : first + GHOST, :].astype(bf16)
+            out[...] = acc_ref[q * GHOST : (q + 1) * GHOST, :].astype(bf16)
         load.wait()
+
+
+def local_kernel(contrib_ref, dest_ref, slot_ref, out_ref):
+    count = out_ref.shape[0]
+    target = targets(dest_ref[...], slot_ref[...], count)
+    group = CHUNK // LANES
+    total = jnp.zeros(out_ref.shape, f32)
+    for g in range(contrib_ref.shape[0] // CHUNK):
+        hits = one_hot_rows(target[g * group : (g + 1) * group, :], count)
+        total = total + jnp.dot(hits, contrib_ref[g * CHUNK : (g + 1) * CHUNK, :], preferred_element_type=f32)
+    out_ref[...] = total
 
 
 def apply_blocks(inv_ref, v):
@@ -195,9 +204,18 @@
     out_ref[...] = apply_blocks(inv_ref, rhs.astype(bf16)).astype(bf16)
 
 
-def own_rows_kernel(fs_ref, nb_ref, face_ref, hits_ref, own_ref, faces_ref):
+def own_rows_kernel(
+    coef_ref, fs_ref, nb_ref, ci_ref, face_ref, table_ref, hits_ref, own_ref, faces_ref, where_ref, scale_ref, w_ref
+):
     count = fs_ref.shape[0]
+    own, even_x, even_y = position()
+    off = nb_ref[...] // count - own
     index_t = (nb_ref[...] % count).T
+    block_t = jnp.where(off == 0, 0, 1 + partner(off, even_x, even_y)).T
+    scale = jnp.zeros(off.shape, f32)
+    for k in range(KINDS):
+        scale = jnp.where(ci_ref[...] == k, coef_ref[k], scale)
+    scale_t = scale.T
     for f in range(FACES):
         column = jnp.broadcast_to(index_t[:, f : f + 1], (count, LANES)).astype(i16)
         hits = one_hot_columns(column, count)
@@ -205,30 +223,27 @@
         hits_ref[rows, :] = hits
         own_ref[rows, :] = jnp.dot(hits, fs_ref[...], preferred_element_type=f32).astype(bf16)
         faces_ref[f * W : (f + 1) * W, :] = block_diagonal(face_ref[f], True)
+        where_ref[rows, :] = jnp.broadcast_to(block_t[:, f : f + 1], (count, LANES)).astype(i16)
+        scale_ref[rows, :] = jnp.broadcast_to(scale_t[:, f : f + 1], (count, LANES))
+    for t in range(NTYPE):
+        w_ref[t * W : (t + 1) * W, :] = block_diagonal(table_ref[t], False)
 
 
 def couple_kernel(
-    coef_ref, fs_ref, h0, h1, h2, h3, nb_ref, ci_ref, hits_ref, own_ref, faces_ref, ghost_ref, inv_ref,
+    fs_ref, h0, h1, h2, h3, hits_ref, own_ref, faces_ref, where_ref, scale_ref, ghost_ref, inv_ref,
     sol_ref, ans_ref, r0, r1, r2, r3,
 ):
     count = fs_ref.shape[0]
-    own, even_x, even_y = position()
-    off = nb_ref[...] // count - own
-    block_t = jnp.where(off == 0, 0, 1 + partner(off, even_x, even_y)).T
-    scale = jnp.zeros(off.shape, f32)
-    for k in range(KINDS):
-        scale = jnp.where(ci_ref[...] == k, coef_ref[k], scale)
-    scale_t = scale.T
     coupled = jnp.zeros((count, W), f32)
     for f in range(FACES):
         rows = slice(f * count, (f + 1) * count)
-        where = wide(jnp.broadcast_to(block_t[:, f : f + 1], (count, LANES)).astype(i16))
+        where = wide(where_ref[rows, :])
         beside = own_ref[rows, :]
         for q, source in enumerate((h0, h1, h2, h3)):
             found = jnp.dot(hits_ref[rows, :], source[...], preferred_element_type=f32).astype(bf16)
             beside = jnp.where(where == jnp.asarray(q + 1, i16), found, beside)
         term = jnp.dot(beside, faces_ref[f * W : (f + 1) * W, :], preferred_element_type=f32)
-        coupled = coupled + term * wide(jnp.broadcast_to(scale_t[:, f : f + 1], (count, LANES)))
+        coupled = coupled + term * wide(scale_ref[rows, :])
     correction = apply_blocks(inv_ref, coupled.astype(bf16))
     solution_rows = fs_ref[...].astype(f32) - OMEGA * correction
     sol_ref[...] = solution_rows
@@ -240,10 +255,10 @@
         out[...] = replies[q * GHOST : (q + 1) * GHOST, :]
 
 
-def fetch_kernel(ans_ref, dest_ref, slot_ref, table_ref, out_ref, w_ref):
+def fetch_kernel(ans_ref, dest_ref, slot_ref, sol_ref, out_ref, sol_hbm, sem):
+    store = pltpu.make_async_copy(sol_ref, sol_hbm, sem)
+    store.start()
     count = ans_ref.shape[0]
-    for t in range(NTYPE):
-        w_ref[t * W : (t + 1) * W, :] = block_diagonal(table_ref[t], False)
     target = targets(dest_ref[...], slot_ref[...], count)
     for g in range(out_ref.shape[0] // CHUNK):
         column = columns(target[g * (CHUNK // LANES) : (g + 1) * (CHUNK // LANES), :])
@@ -251,6 +266,7 @@
             hits = one_hot_columns(column[r : r + PB, :], count)
             first = g * CHUNK + r
             out_ref[first : first + PB, :] = jnp.dot(hits, ans_ref[...], preferred_element_type=f32).astype(bf16)
+    store.wait()
 
 
 def prolong_kernel(count, local_ref, r0, r1, r2, r3, w_ref, dest_ref, slot_ref, type_ref, out_ref):
@@ -279,20 +295,29 @@
 
 
 def restrict(x, meta, table, inverse):
-    count = inverse.shape[0]
     steps = x.shape[0] // CHUNK
-    rows = count + 4 * GHOST
     meta_spec = pl.BlockSpec((CHUNK // LANES, LANES), lambda i: (i, 0))
     return pl.pallas_call(
         restrict_kernel,
         grid=(steps,),
         in_specs=[pl.BlockSpec((CHUNK, W), lambda i: (i, 0)), meta_spec, meta_spec, meta_spec, whole(table.shape), pl.BlockSpec(memory_space=pltpu.HBM)],
         out_specs=[VMEM] * 6,
-        out_shape=[pltpu.VMEM((count, W), f32)] + ghost_shape() + [pltpu.VMEM(inverse.shape, bf16)],
-        scratch_shapes=[pltpu.VMEM((NTYPE * W, W), bf16), pltpu.VMEM((rows, W), f32), pltpu.SemaphoreType.DMA],
+        out_shape=[pltpu.VMEM(x.shape, bf16)] + ghost_shape() + [pltpu.VMEM(inverse.shape, bf16)],
+        scratch_shapes=[pltpu.VMEM((NTYPE * W, W), bf16), pltpu.VMEM((4 * GHOST, W), f32), pltpu.SemaphoreType.DMA],
         compiler_params=pltpu.CompilerParams(vmem_limit_bytes=VMEM_BYTES),
         name="restrict",
     )(x, *meta, table, inverse)
+
+
+def local_sums(contrib, meta, count):
+    return pl.pallas_call(
+        local_kernel,
+        in_specs=[VMEM] * 3,
+        out_specs=VMEM,
+        out_shape=pltpu.VMEM((count, W), f32),
+        compiler_params=pltpu.CompilerParams(vmem_limit_bytes=VMEM_BYTES),
+        name="local_sums",
+    )(contrib, meta[0], meta[1])
 
 
 def sweep(local, incoming, ghost, inverse):
@@ -306,42 +331,45 @@
     )(local, *incoming, ghost, inverse)
 
 
-def own_rows(first_sweep, neighbours, face_table):
+def own_rows(coef, first_sweep, neighbours, coef_index, face_table, table):
     count = first_sweep.shape[0]
+    rows = FACES * count
     return pl.pallas_call(
         own_rows_kernel,
-        in_specs=[VMEM] * 3,
-        out_specs=[VMEM] * 3,
+        in_specs=[pl.BlockSpec(memory_space=pltpu.SMEM)] + [VMEM] * 5,
+        out_specs=[VMEM] * 6,
         out_shape=[
-            pltpu.VMEM((FACES * count, count), bf16), pltpu.VMEM((FACES * count, W), bf16), pltpu.VMEM((FACES * W, W), bf16)
+            pltpu.VMEM((rows, count), bf16), pltpu.VMEM((rows, W), bf16), pltpu.VMEM((FACES * W, W), bf16),
+            pltpu.VMEM((rows, LANES), i16), pltpu.VMEM((rows, LANES), f32), pltpu.VMEM((NTYPE * W, W), bf16),
         ],
         compiler_params=pltpu.CompilerParams(vmem_limit_bytes=VMEM_BYTES),
         name="own_rows",
-    )(first_sweep, neighbours, face_table)
-
-
-def couple(coef, first_sweep, halo, neighbours, coef_index, prepared, ghost, inverse):
+    )(coef, first_sweep, neighbours, coef_index, face_table, table)
+
+
+def couple(first_sweep, halo, prepared, ghost, inverse):
     count = first_sweep.shape[0]
     return pl.pallas_call(
         couple_kernel,
-        in_specs=[pl.BlockSpec(memory_space=pltpu.SMEM)] + [VMEM] * 12,
+        in_specs=[VMEM] * 12,
         out_specs=[VMEM] * 6,
-        out_shape=[jax.ShapeDtypeStruct((count, W), f32), pltpu.VMEM((count, W), bf16)] + ghost_shape(),
+        out_shape=[pltpu.VMEM((count, W), f32), pltpu.VMEM((count, W), bf16)] + ghost_shape(),
         compiler_params=pltpu.CompilerParams(vmem_limit_bytes=VMEM_BYTES),
         name="couple",
-    )(coef, first_sweep, *halo, neighbours, coef_index, *prepared, ghost, inverse)
-
-
-def fetch(answer, meta, table):
+    )(first_sweep, *halo, *prepared, ghost, inverse)
+
+
+def fetch(answer, meta, solution_rows):
     fine_count = meta[0].shape[0] * LANES
     return pl.pallas_call(
         fetch_kernel,
         in_specs=[VMEM] * 4,
-        out_specs=[VMEM] * 2,
-        out_shape=[pltpu.VMEM((fine_count, W), bf16), pltpu.VMEM((NTYPE * W, W), bf16)],
+        out_specs=[VMEM, pl.BlockSpec(memory_space=pltpu.HBM)],
+        out_shape=[pltpu.VMEM((fine_count, W), bf16), jax.ShapeDtypeStruct(solution_rows.shape, f32)],
+        scratch_shapes=[pltpu.SemaphoreType.DMA],
         compiler_params=pltpu.CompilerParams(vmem_limit_bytes=VMEM_BYTES),
         name="fetch",
-    )(answer, meta[0], meta[1], table)
+    )(answer, meta[0], meta[1], solution_rows)
 
 
 def prolong(local, returned, table, meta, count):
@@ -365,18 +393,19 @@
     fine_count = fine_residual.shape[0]
     perms = swap_pairs(lax.axis_size("px"), lax.axis_size("py"))
     meta = [m.reshape(fine_count // LANES, LANES) for m in (dest_owner, coarse_slot, child_type)]
-    local, *outgoing, inverse = restrict(
+    contrib, *outgoing, inverse = restrict(
         in_hbm(fine_residual), [in_hbm(m) for m in meta], in_hbm(restrict_table), in_hbm(inverse_blocks)
     )
     incoming = exchange(outgoing, perms)
+    local = local_sums(contrib, meta, inverse_blocks.shape[0])
     first_sweep = sweep(local, incoming, ghost_slot, inverse)
     halo = exchange([first_sweep] * 4, perms)
-    prepared = own_rows(first_sweep, neighbours, face_table)
-    coarse_solution, answer, *replies = couple(
-        face_coef, first_sweep, halo, neighbours, coef_index, prepared, ghost_slot, inverse
+    *prepared, table = own_rows(
+        face_coef, first_sweep, neighbours, coef_index, face_table, restrict_table
     )
+    solution_rows, answer, *replies = couple(first_sweep, halo, prepared, ghost_slot, inverse)
     returned = exchange(replies, perms)
-    fetched, table = fetch(answer, meta, restrict_table)
+    fetched, coarse_solution = fetch(answer, meta, solution_rows)
     fine_correction = prolong(fetched, returned, table, meta, inverse_blocks.shape[0])
     return (coarse_solution, fine_correction)
 

time: 67.7 us -> 65.7 us (0.970)
  waiting for transfers between devices: 10.4 us -> 8.25 us
    ppermute x12, waiting for transfers between devices: 10.4 us -> 8.25 us  [exchange(): lax.ppermute(x, ('px', 'py'), perm)]
    pallas_call x3 -> x4, Pallas kernels: 14.8 us -> 15.4 us  [the longest x1 9.23 us: couple(): pl.pallas_call(couple_kernel, in_specs=[VMEM] * 12, out_specs=[VMEM] * 6,...]
  transfers between devices with their start and end apart: 12 -> 12, of which waited for: 4 -> 4; matrix products, arithmetic and copies ran while one was open for 0% -> 0% of each run, Pallas kernels for 6% -> 9%
where the time goes in v5:
time: 65.7 us; the launch traced here: 65.6 us
  Pallas kernels  36.9 us (56%)
  starting transfers between devices  19.6 us (30%)
  waiting for transfers between devices  8.25 us (13%)
  between operations  0.81 us (1%)
    ppermute x12, starting transfers between devices, exchange(): lax.ppermute(x, ('px', 'py'), perm)  19.6 us
    pallas_call x1, Pallas kernels, couple(): pl.pallas_call(couple_kernel, in_specs=[VMEM] * 12, out_specs=[VMEM] * 6,...  9.23 us
    pallas_call x1, Pallas kernels, restrict(): pl.pallas_call(restrict_kernel, grid=(steps,), in_specs=[pl.BlockSpec((CH...  8.62 us
    ppermute x12, waiting for transfers between devices, exchange(): lax.ppermute(x, ('px', 'py'), perm)  8.25 us
    pallas_call x1, Pallas kernels, prolong(): pl.pallas_call(functools.partial(prolong_kernel, count), grid=(fine_count...  7.78 us
    pallas_call x1, Pallas kernels, sweep(): pl.pallas_call(sweep_kernel, in_specs=[VMEM] * 7, out_specs=VMEM, out_sha...  5.06 us
    pallas_call x1, Pallas kernels, own_rows(): pl.pallas_call(own_rows_kernel, in_specs=[pl.BlockSpec(memory_space=pltpu...  3.31 us
    pallas_call x1, Pallas kernels, fetch(): pl.pallas_call(fetch_kernel, in_specs=[VMEM] * 4, out_specs=[VMEM, pl.Blo...  1.65 us
  transfers between devices with their start and end apart: 12, of which 4 were waited for; matrix products, arithmetic and copies ran while one was open for 0% of the time, Pallas kernels for 9%

profile of v5, /device:TPU:8, one launch (start us, length us, event | category | flops | bytes accessed | tf_op | source)
XLA Modules:
  0.0 65.6 jit_solution(7009637736096788479)
XLA Ops:
  0.6 0.0 copy-start.1
  0.6 0.0 copy-start.2
  0.7 8.6 %restrict.1 = (bf16[4096,256]{1,0:T(8,128)(2,1)S(1)}, bf16[32,256]{1,0:T(8,128)(2,1)S(1)}, bf16[32,256]{1,0:T(8,128)(2,1)S(1)}, bf16[32,256]{1,0:T(8,128)(2,1)S(...) custom-call(bf16[4096,256]{1,0:T(8,128)(2,1)} %x_ref.1, s32[32,128]{1,0:T(8,128)} %bitcast.3, ...), custom_call_target="tpu_custom_call" | custom-call | tf_op jit(solution)/shard_map/restrict/pallas_call | solution.py:300
  9.3 0.0 copy-start.7
  9.3 0.1 collective-permute-start
  9.4 0.4 collective-permute-start.1
  9.8 1.6 %collective-permute-start.2 = (bf16[32,256]{1,0:T(8,128)(2,1)S(1)}, bf16[32,256]{1,0:T(8,128)(2,1)S(1)}, u32[]{:S(2)}, u32[]{:S(2)}) collective-permute-start(bf16[32,256]{1,0:T(8,128)(2,1)S(1)} %get-tuple-element.25), channel_id=1, source_target_pairs={{0,1},{1,0},{2,3},{3,2},{4,5},{5,4},{6,7},{7,6},{8,9},{9,8},{10,11... | collective-permute-start | bytes 49160 | tf_op jit(solution)/shard_map/ppermute | solution.py:54
  11.4 5.6 %collective-permute-start.3 = (bf16[32,256]{1,0:T(8,128)(2,1)S(1)}, bf16[32,256]{1,0:T(8,128)(2,1)S(1)}, u32[]{:S(2)}, u32[]{:S(2)}) collective-permute-start(bf16[32,256]{1,0:T(8,128)(2,1)S(1)} %get-tuple-element.26), channel_id=1, source_target_pairs={{0,15},{1,2},{2,1},{3,4},{4,3},{5,6},{6,5},{7,8},{8,7},{9,10},{10,... | collective-permute-start | bytes 49160 | tf_op jit(solution)/shard_map/ppermute | solution.py:54
  17.0 0.0 copy-done.1
  17.0 0.0 copy-done.2
  17.0 1.2 %local_sums.1.local_ref = f32[512,256]{1,0:T(8,128)S(1)} custom-call(bf16[4096,256]{1,0:T(8,128)(2,1)S(1)} %get-tuple-element.22.contrib_ref, s32[32,128]{1,0:T(8,128)S(1)} %bitcast.4, s32[32,128]{1,0:T(8,128)S(1)} %bitcast.8), custom_call_target="tpu_custom_call" | custom-call | tf_op jit(solution)/shard_map/local_sums/pallas_call | solution.py:313
  18.3 0.0 collective-permute-done.i0
  18.3 0.0 collective-permute-done.1.i1
  18.3 0.0 collective-permute-done.2.i2
  18.3 0.4 collective-permute-done.3.i3
  18.7 0.0 copy-done.7
  18.7 0.0 copy-start
  18.7 0.0 copy-start.3
  18.7 0.0 copy-start.5
  18.7 0.0 copy-start.6
  18.7 0.0 copy-start.8
  18.8 5.1 %sweep.1.fs_ref = bf16[512,256]{1,0:T(8,128)(2,1)S(1)} custom-call(f32[512,256]{1,0:T(8,128)S(1)} %local_sums.1.local_ref, bf16[32,256]{1,0:T(8,128)(2,1)S(1)} %collective-permute-done.i0, bf16[32,256]{1,0:T(8,128)(2,1)S(1)} %collective-permute-done.1.i1, bf16[32,256]{1,0:T(8,128)(2,1)S(1)} %collective-permute-done.2.i2, ...), custom_call_target="tpu_custom_call" | custom-call | tf_op jit(solution)/shard_map/sweep/pallas_call | solution.py:324
  23.8 5.6 %collective-permute-start.7 = (bf16[512,256]{1,0:T(8,128)(2,1)S(1)}, bf16[512,256]{1,0:T(8,128)(2,1)S(1)}, u32[]{:S(2)}, u32[]{:S(2)}) collective-permute-start(bf16[512,256]{1,0:T(8,128)(2,1)S(1)} %sweep.1.fs_ref), channel_id=1, source_target_pairs={{0,15},{1,2},{2,1},{3,4},{4,3},{5,6},{6,5},{7,8},{8,7},{9,10},{10,... | collective-permute-start | bytes 786440 | tf_op jit(solution)/shard_map/ppermute | solution.py:54
  29.4 0.0 collective-permute-start.6
  29.4 0.0 collective-permute-start.5
  29.4 1.6 %collective-permute-start.4 = (bf16[512,256]{1,0:T(8,128)(2,1)S(1)}, bf16[512,256]{1,0:T(8,128)(2,1)S(1)}, u32[]{:S(2)}, u32[]{:S(2)}) collective-permute-start(bf16[512,256]{1,0:T(8,128)(2,1)S(1)} %sweep.1.fs_ref), channel_id=1, source_target_pairs={{0,16},{1,17},{2,18},{3,19},{4,20},{5,21},{6,22},{7,23},{8,24},{9,... | collective-permute-start | bytes 786440 | tf_op jit(solution)/shard_map/ppermute | solution.py:54
  30.9 0.0 copy-done
  30.9 0.0 copy-done.3
  30.9 0.0 copy-done.5
  30.9 0.0 copy-done.6
  30.9 0.0 copy-done.8
  31.0 3.3 %own_rows.1 = (bf16[3072,512]{1,0:T(8,128)(2,1)S(1)}, bf16[3072,256]{1,0:T(8,128)(2,1)S(1)}, bf16[1536,256]{1,0:T(8,128)(2,1)S(1)}, s16[3072,128]{1,0:T(8,128)(2...) custom-call(f32[16]{0:T(128)S(1)} %copy-done.8, bf16[512,256]{1,0:T(8,128)(2,1)S(1)} %sweep.1.fs_ref, ...), custom_call_target="tpu_custom_call" | custom-call | tf_op jit(solution)/shard_map/own_rows/pallas_call | solution.py:337
  34.3 1.7 %collective-permute-done.7.h3 = bf16[512,256]{1,0:T(8,128)(2,1)S(1)} collective-permute-done((bf16[512,256]{1,0:T(8,128)(2,1)S(1)}, bf16[512,256]{1,0:T(8,128)(2,1)S(1)}, u32[]{:S(2)}, u32[]{:S(2)}) %collective-permute-start.7) | collective-permute-done | bytes 262176 | tf_op jit(solution)/shard_map/ppermute | solution.py:54
  35.9 1.5 %collective-permute-done.6.h2 = bf16[512,256]{1,0:T(8,128)(2,1)S(1)} collective-permute-done((bf16[512,256]{1,0:T(8,128)(2,1)S(1)}, bf16[512,256]{1,0:T(8,128)(2,1)S(1)}, u32[]{:S(2)}, u32[]{:S(2)}) %collective-permute-start.6) | collective-permute-done | bytes 262176 | tf_op jit(solution)/shard_map/ppermute | solution.py:54
  37.4 0.0 collective-permute-done.5.h1
  37.4 0.0 collective-permute-done.4.h0
  37.4 9.2 %couple.1 = (f32[512,256]{1,0:T(8,128)S(1)}, bf16[512,256]{1,0:T(8,128)(2,1)S(1)}, bf16[32,256]{1,0:T(8,128)(2,1)S(1)}, bf16[32,256]{1,0:T(8,128)(2,1)S(1)}, bf1...) custom-call(bf16[512,256]{1,0:T(8,128)(2,1)S(1)} %sweep.1.fs_ref, bf16[512,256]{1,0:T(8,128)(2,1)S(1)} %collective-permute-done.4.h0, ...), custom_call_target="tpu_custom_call" | custom-call | tf_op jit(solution)/shard_map/couple/pallas_call | solution.py:352
  46.6 0.1 collective-permute-start.8
  46.7 2.0 %collective-permute-start.9 = (bf16[32,256]{1,0:T(8,128)(2,1)S(1)}, bf16[32,256]{1,0:T(8,128)(2,1)S(1)}, u32[]{:S(2)}, u32[]{:S(2)}) collective-permute-start(bf16[32,256]{1,0:T(8,128)(2,1)S(1)} %get-tuple-element.38), channel_id=1, source_target_pairs={{0,112},{1,113},{2,114},{3,115},{4,116},{5,117},{6,118},{7,119},{8... | collective-permute-start | bytes 49160 | tf_op jit(solution)/shard_map/ppermute | solution.py:54
  48.7 2.0 %collective-permute-start.10 = (bf16[32,256]{1,0:T(8,128)(2,1)S(1)}, bf16[32,256]{1,0:T(8,128)(2,1)S(1)}, u32[]{:S(2)}, u32[]{:S(2)}) collective-permute-start(bf16[32,256]{1,0:T(8,128)(2,1)S(1)} %get-tuple-element.39), channel_id=1, source_target_pairs={{0,1},{1,0},{2,3},{3,2},{4,5},{5,4},{6,7},{7,6},{8,9},{9,8},{10,11... | collective-permute-start | bytes 49160 | tf_op jit(solution)/shard_map/ppermute | solution.py:54
  50.7 0.7 %collective-permute-start.11 = (bf16[32,256]{1,0:T(8,128)(2,1)S(1)}, bf16[32,256]{1,0:T(8,128)(2,1)S(1)}, u32[]{:S(2)}, u32[]{:S(2)}) collective-permute-start(bf16[32,256]{1,0:T(8,128)(2,1)S(1)} %get-tuple-element.40), channel_id=1, source_target_pairs={{0,15},{1,2},{2,1},{3,4},{4,3},{5,6},{6,5},{7,8},{8,7},{9,10},{10,... | collective-permute-start | bytes 49160 | tf_op jit(solution)/shard_map/ppermute | solution.py:54
  51.4 1.7 %fetch.1 = (bf16[4096,256]{1,0:T(8,128)(2,1)S(1)}, f32[512,256]{1,0:T(8,128)}) custom-call(bf16[512,256]{1,0:T(8,128)(2,1)S(1)} %get-tuple-element.33.ans_ref, s32[32,128]{1,0:T(8,128)S(1)} %bitcast.5, s32[32,128]{1,0:T(8,128)S(1)} %bitcast.9, f32[512,256]{1,0:T(8,128)S(1)} %get-tuple-element.34.sol_ref), custom_call_target="tpu_custom_call" | custom-call | tf_op jit(solution)/shard_map/fetch/pallas_call | solution.py:364
  53.1 0.0 collective-permute-done.8.r0
  53.1 0.0 collective-permute-done.9.r1
  53.1 0.0 collective-permute-done.10.r2
  53.1 4.7 %collective-permute-done.11.r3 = bf16[32,256]{1,0:T(8,128)(2,1)S(1)} collective-permute-done((bf16[32,256]{1,0:T(8,128)(2,1)S(1)}, bf16[32,256]{1,0:T(8,128)(2,1)S(1)}, u32[]{:S(2)}, u32[]{:S(2)}) %collective-permute-start.11) | collective-permute-done | bytes 16416 | tf_op jit(solution)/shard_map/ppermute | solution.py:54
  57.8 0.0 copy-done.4
  57.8 7.8 %prolong.1 = bf16[4096,256]{1,0:T(8,128)(2,1)} custom-call(bf16[4096,256]{1,0:T(8,128)(2,1)S(1)} %get-tuple-element.36.local_ref, bf16[32,256]{1,0:T(8,128)(2,1)S(1)} %collective-permute-done.8.r0, bf16[32,256]{1,0:T(8,128)(2,1)S(1)} %collective-permute-done.9.r1, bf16[32,256]{1,0:T(8,128)(2,1)S(1)} %collective-permute-done.10.r2, ...), custom_call_target="tpu_custom_call" | custom-call | tf_op jit(solution)/shard_map/prolong/pallas_call | solution.py:378
  (1 shorter events, 0.0 us)
Async XLA Ops:
  0.6 16.4 %copy-start.1 = (s32[4096]{0:T(1024)S(1)}, s32[4096]{0:T(1024)}, u32[]{:S(2)}) copy-start(s32[4096]{0:T(1024)} %param.12) | copy-start | bytes 49156
  0.6 16.4 %copy-start.2 = (s32[4096]{0:T(1024)S(1)}, s32[4096]{0:T(1024)}, u32[]{:S(2)}) copy-start(s32[4096]{0:T(1024)} %param.13) | copy-start | bytes 49156
  9.3 9.4 %copy-start.7 = (s32[4,32]{1,0:T(4,128)S(1)}, s32[4,32]{1,0:T(4,128)}, u32[]{:S(2)}) copy-start(s32[4,32]{1,0:T(4,128)} %ghost_ref.3) | copy-start | bytes 1540
  9.3 9.0 %collective-permute-start = (bf16[32,256]{1,0:T(8,128)(2,1)S(1)}, bf16[32,256]{1,0:T(8,128)(2,1)S(1)}, u32[]{:S(2)}, u32[]{:S(2)}) collective-permute-start(bf16[32,256]{1,0:T(8,128)(2,1)S(1)} %get-tuple-element.23), channel_id=1, source_target_pairs={{0,16},{1,17},{2,18},{3,19},{4,20},{5,21},{6,22},{7,23},{8,24},{9,... | collective-permute-start | bytes 49160 | tf_op jit(solution)/shard_map/ppermute | solution.py:54
  9.4 8.9 %collective-permute-start.1 = (bf16[32,256]{1,0:T(8,128)(2,1)S(1)}, bf16[32,256]{1,0:T(8,128)(2,1)S(1)}, u32[]{:S(2)}, u32[]{:S(2)}) collective-permute-start(bf16[32,256]{1,0:T(8,128)(2,1)S(1)} %get-tuple-element.24), channel_id=1, source_target_pairs={{0,112},{1,113},{2,114},{3,115},{4,116},{5,117},{6,118},{7,119},{8... | collective-permute-start | bytes 49160 | tf_op jit(solution)/shard_map/ppermute | solution.py:54
  9.8 8.5 %collective-permute-start.2 = (bf16[32,256]{1,0:T(8,128)(2,1)S(1)}, bf16[32,256]{1,0:T(8,128)(2,1)S(1)}, u32[]{:S(2)}, u32[]{:S(2)}) collective-permute-start(bf16[32,256]{1,0:T(8,128)(2,1)S(1)} %get-tuple-element.25), channel_id=1, source_target_pairs={{0,1},{1,0},{2,3},{3,2},{4,5},{5,4},{6,7},{7,6},{8,9},{9,8},{10,11... | collective-permute-start | bytes 49160 | tf_op jit(solution)/shard_map/ppermute | solution.py:54
  11.4 7.3 %collective-permute-start.3 = (bf16[32,256]{1,0:T(8,128)(2,1)S(1)}, bf16[32,256]{1,0:T(8,128)(2,1)S(1)}, u32[]{:S(2)}, u32[]{:S(2)}) collective-permute-start(bf16[32,256]{1,0:T(8,128)(2,1)S(1)} %get-tuple-element.26), channel_id=1, source_target_pairs={{0,15},{1,2},{2,1},{3,4},{4,3},{5,6},{6,5},{7,8},{8,7},{9,10},{10,... | collective-permute-start | bytes 49160 | tf_op jit(solution)/shard_map/ppermute | solution.py:54
  18.7 12.2 %copy-start = (bf16[8,64,64]{2,1,0:T(8,128)(2,1)S(1)}, bf16[8,64,64]{2,1,0:T(8,128)(2,1)}, u32[]{:S(2)}) copy-start(bf16[8,64,64]{2,1,0:T(8,128)(2,1)} %table_ref.3) | copy-start | bytes 196612
  18.7 12.2 %copy-start.3 = (bf16[6,64,64]{2,1,0:T(8,128)(2,1)S(1)}, bf16[6,64,64]{2,1,0:T(8,128)(2,1)}, u32[]{:S(2)}) copy-start(bf16[6,64,64]{2,1,0:T(8,128)(2,1)} %face_ref.1) | copy-start | bytes 147460
  18.7 12.2 %copy-start.5 = (s32[6,512]{1,0:T(8,128)S(1)}, s32[6,512]{1,0:T(8,128)}, u32[]{:S(2)}) copy-start(s32[6,512]{1,0:T(8,128)} %nb_ref.1) | copy-start | bytes 36868
  18.7 12.2 %copy-start.6 = (s32[6,512]{1,0:T(8,128)S(1)}, s32[6,512]{1,0:T(8,128)}, u32[]{:S(2)}) copy-start(s32[6,512]{1,0:T(8,128)} %ci_ref.1) | copy-start | bytes 36868
  18.7 12.2 %copy-start.8 = (f32[16]{0:T(128)S(1)}, f32[16]{0:T(128)}, u32[]{:S(2)}) copy-start(f32[16]{0:T(128)} %coef_ref.1) | copy-start | bytes 196
  23.8 12.1 %collective-permute-start.7 = (bf16[512,256]{1,0:T(8,128)(2,1)S(1)}, bf16[512,256]{1,0:T(8,128)(2,1)S(1)}, u32[]{:S(2)}, u32[]{:S(2)}) collective-permute-start(bf16[512,256]{1,0:T(8,128)(2,1)S(1)} %sweep.1.fs_ref), channel_id=1, source_target_pairs={{0,15},{1,2},{2,1},{3,4},{4,3},{5,6},{6,5},{7,8},{8,7},{9,10},{10,... | collective-permute-start | bytes 786440 | tf_op jit(solution)/shard_map/ppermute | solution.py:54
  29.4 8.0 %collective-permute-start.6 = (bf16[512,256]{1,0:T(8,128)(2,1)S(1)}, bf16[512,256]{1,0:T(8,128)(2,1)S(1)}, u32[]{:S(2)}, u32[]{:S(2)}) collective-permute-start(bf16[512,256]{1,0:T(8,128)(2,1)S(1)} %sweep.1.fs_ref), channel_id=1, source_target_pairs={{0,1},{1,0},{2,3},{3,2},{4,5},{5,4},{6,7},{7,6},{8,9},{9,8},{10,11... | collective-permute-start | bytes 786440 | tf_op jit(solution)/shard_map/ppermute | solution.py:54
  29.4 8.0 %collective-permute-start.5 = (bf16[512,256]{1,0:T(8,128)(2,1)S(1)}, bf16[512,256]{1,0:T(8,128)(2,1)S(1)}, u32[]{:S(2)}, u32[]{:S(2)}) collective-permute-start(bf16[512,256]{1,0:T(8,128)(2,1)S(1)} %sweep.1.fs_ref), channel_id=1, source_target_pairs={{0,112},{1,113},{2,114},{3,115},{4,116},{5,117},{6,118},{7,119},{8... | collective-permute-start | bytes 786440 | tf_op jit(solution)/shard_map/ppermute | solution.py:54
  29.4 8.0 %collective-permute-start.4 = (bf16[512,256]{1,0:T(8,128)(2,1)S(1)}, bf16[512,256]{1,0:T(8,128)(2,1)S(1)}, u32[]{:S(2)}, u32[]{:S(2)}) collective-permute-start(bf16[512,256]{1,0:T(8,128)(2,1)S(1)} %sweep.1.fs_ref), channel_id=1, source_target_pairs={{0,16},{1,17},{2,18},{3,19},{4,20},{5,21},{6,22},{7,23},{8,24},{9,... | collective-permute-start | bytes 786440 | tf_op jit(solution)/shard_map/ppermute | solution.py:54
  37.4 20.4 %copy-start.4 = (s32[4096]{0:T(1024)S(1)}, s32[4096]{0:T(1024)}, u32[]{:S(2)}) copy-start(s32[4096]{0:T(1024)} %param.15) | copy-start | bytes 49156
  46.6 6.4 %collective-permute-start.8 = (bf16[32,256]{1,0:T(8,128)(2,1)S(1)}, bf16[32,256]{1,0:T(8,128)(2,1)S(1)}, u32[]{:S(2)}, u32[]{:S(2)}) collective-permute-start(bf16[32,256]{1,0:T(8,128)(2,1)S(1)} %get-tuple-element.37), channel_id=1, source_target_pairs={{0,16},{1,17},{2,18},{3,19},{4,20},{5,21},{6,22},{7,23},{8,24},{9,... | collective-permute-start | bytes 49160 | tf_op jit(solution)/shard_map/ppermute | solution.py:54
  46.7 6.4 %collective-permute-start.9 = (bf16[32,256]{1,0:T(8,128)(2,1)S(1)}, bf16[32,256]{1,0:T(8,128)(2,1)S(1)}, u32[]{:S(2)}, u32[]{:S(2)}) collective-permute-start(bf16[32,256]{1,0:T(8,128)(2,1)S(1)} %get-tuple-element.38), channel_id=1, source_target_pairs={{0,112},{1,113},{2,114},{3,115},{4,116},{5,117},{6,118},{7,119},{8... | collective-permute-start | bytes 49160 | tf_op jit(solution)/shard_map/ppermute | solution.py:54
  48.7 4.4 %collective-permute-start.10 = (bf16[32,256]{1,0:T(8,128)(2,1)S(1)}, bf16[32,256]{1,0:T(8,128)(2,1)S(1)}, u32[]{:S(2)}, u32[]{:S(2)}) collective-permute-start(bf16[32,256]{1,0:T(8,128)(2,1)S(1)} %get-tuple-element.39), channel_id=1, source_target_pairs={{0,1},{1,0},{2,3},{3,2},{4,5},{5,4},{6,7},{7,6},{8,9},{9,8},{10,11... | collective-permute-start | bytes 49160 | tf_op jit(solution)/shard_map/ppermute | solution.py:54
  50.7 7.1 %collective-permute-start.11 = (bf16[32,256]{1,0:T(8,128)(2,1)S(1)}, bf16[32,256]{1,0:T(8,128)(2,1)S(1)}, u32[]{:S(2)}, u32[]{:S(2)}) collective-permute-start(bf16[32,256]{1,0:T(8,128)(2,1)S(1)} %get-tuple-element.40), channel_id=1, source_target_pairs={{0,15},{1,2},{2,1},{3,4},{4,3},{5,6},{6,5},{7,8},{8,7},{9,10},{10,... | collective-permute-start | bytes 49160 | tf_op jit(solution)/shard_map/ppermute | solution.py:54

commit v6 on v5

--- a/solution.py
+++ b/solution.py
@@ -269,14 +269,32 @@
     store.wait()
 
 
-def prolong_kernel(count, local_ref, r0, r1, r2, r3, w_ref, dest_ref, slot_ref, type_ref, out_ref):
-    step = pl.program_id(0)
-    target = columns(targets(dest_ref[...], slot_ref[...], count) - count)
+def prolong_kernel(
+    count, local_ref, r0, r1, r2, r3, w_ref, dest_ref, slot_ref, type_ref, out_hbm, out_ref, sems
+):
+    chunks = local_ref.shape[0] // CHUNK
+    group = CHUNK // LANES
     returned = jnp.concatenate([r0[...], r1[...], r2[...], r3[...]], axis=0)
-    remote = jnp.dot(one_hot_columns(target, 4 * GHOST), returned, preferred_element_type=f32)
-    local = local_ref[pl.ds(pl.multiple_of(step * CHUNK, CHUNK), CHUNK), :]
-    fetched = (local.astype(f32) + remote).astype(bf16)
-    out_ref[...] = typed(fetched, columns(type_ref[...]), w_ref[...], PB)
+
+    def store_rows(k):
+        rows = pl.ds(pl.multiple_of(k * PB, PB), PB)
+        return pltpu.make_async_copy(out_ref.at[rows, :], out_hbm.at[rows, :], sems.at[k])
+
+    def one_chunk(g, carry):
+        lines = pl.ds(pl.multiple_of(g * group, group), group)
+        target = columns(targets(dest_ref[lines, :], slot_ref[lines, :], count) - count)
+        kinds = columns(type_ref[lines, :])
+        for r in range(0, CHUNK, PB):
+            rows = pl.ds(pl.multiple_of(g * CHUNK + r, PB), PB)
+            remote = jnp.dot(one_hot_columns(target[r : r + PB], 4 * GHOST), returned, preferred_element_type=f32)
+            fetched = (local_ref[rows, :].astype(f32) + remote).astype(bf16)
+            out_ref[rows, :] = typed(fetched, kinds[r : r + PB], w_ref[...], PB)
+            store_rows(g * (CHUNK // PB) + r // PB).start()
+        return carry
+
+    lax.fori_loop(0, chunks, one_chunk, 0, unroll=True)
+    for k in range(local_ref.shape[0] // PB):
+        store_rows(k).wait()
 
 
 VMEM = pl.BlockSpec(memory_space=pltpu.VMEM)
@@ -374,13 +392,12 @@
 
 def prolong(local, returned, table, meta, count):
     fine_count = local.shape[0]
-    meta_spec = pl.BlockSpec((CHUNK // LANES, LANES), lambda i: (i, 0))
     return pl.pallas_call(
         functools.partial(prolong_kernel, count),
-        grid=(fine_count // CHUNK,),
-        in_specs=[VMEM] * 6 + [meta_spec, meta_spec, meta_spec],
-        out_specs=pl.BlockSpec((CHUNK, W), lambda i: (i, 0)),
+        in_specs=[VMEM] * 9,
+        out_specs=pl.BlockSpec(memory_space=pltpu.HBM),
         out_shape=jax.ShapeDtypeStruct((fine_count, W), bf16),
+        scratch_shapes=[pltpu.VMEM((fine_count, W), bf16), pltpu.SemaphoreType.DMA((fine_count // PB,))],
         compiler_params=pltpu.CompilerParams(vmem_limit_bytes=VMEM_BYTES),
         name="prolong",
     )(local, *returned, table, *meta)

time: 65.7 us -> 64.6 us (0.983)
  Pallas kernels: 36.9 us -> 35.6 us
    pallas_call x1, Pallas kernels: 7.78 us -> 6.53 us  [prolong(): pl.pallas_call(functools.partial(prolong_kernel, count), in_specs=[VMEM]...]
  transfers between devices with their start and end apart: 12 -> 12, of which waited for: 4 -> 4; matrix products, arithmetic and copies ran while one was open for 0% -> 0% of each run, Pallas kernels for 9% -> 10%
where the time goes in v6:
time: 64.6 us; the launch traced here: 64.5 us
  Pallas kernels  35.6 us (55%)
  starting transfers between devices  19.6 us (30%)
  waiting for transfers between devices  8.25 us (13%)
  between operations  0.99 us (2%)
    ppermute x12, starting transfers between devices, exchange(): lax.ppermute(x, ('px', 'py'), perm)  19.6 us
    pallas_call x1, Pallas kernels, couple(): pl.pallas_call(couple_kernel, in_specs=[VMEM] * 12, out_specs=[VMEM] * 6,...  9.23 us
    pallas_call x1, Pallas kernels, restrict(): pl.pallas_call(restrict_kernel, grid=(steps,), in_specs=[pl.BlockSpec((CH...  8.62 us
    ppermute x12, waiting for transfers between devices, exchange(): lax.ppermute(x, ('px', 'py'), perm)  8.25 us
    pallas_call x1, Pallas kernels, prolong(): pl.pallas_call(functools.partial(prolong_kernel, count), in_specs=[VMEM]...  6.53 us
    pallas_call x1, Pallas kernels, sweep(): pl.pallas_call(sweep_kernel, in_specs=[VMEM] * 7, out_specs=VMEM, out_sha...  5.06 us
    pallas_call x1, Pallas kernels, own_rows(): pl.pallas_call(own_rows_kernel, in_specs=[pl.BlockSpec(memory_space=pltpu...  3.31 us
    pallas_call x1, Pallas kernels, fetch(): pl.pallas_call(fetch_kernel, in_specs=[VMEM] * 4, out_specs=[VMEM, pl.Blo...  1.65 us
  transfers between devices with their start and end apart: 12, of which 4 were waited for; matrix products, arithmetic and copies ran while one was open for 0% of the time, Pallas kernels for 10%

profile of v6, /device:TPU:8, one launch (start us, length us, event | category | flops | bytes accessed | tf_op | source)
XLA Modules:
  0.0 64.5 jit_solution(5040017521255348148)
XLA Ops:
  0.6 0.0 copy-start.1
  0.6 0.0 copy-start.2
  0.7 8.6 %restrict.1 = (bf16[4096,256]{1,0:T(8,128)(2,1)S(1)}, bf16[32,256]{1,0:T(8,128)(2,1)S(1)}, bf16[32,256]{1,0:T(8,128)(2,1)S(1)}, bf16[32,256]{1,0:T(8,128)(2,1)S(...) custom-call(bf16[4096,256]{1,0:T(8,128)(2,1)} %x_ref.1, s32[32,128]{1,0:T(8,128)} %bitcast.3, ...), custom_call_target="tpu_custom_call" | custom-call | tf_op jit(solution)/shard_map/restrict/pallas_call | solution.py:318
  9.3 0.0 copy-start.7
  9.3 0.1 collective-permute-start
  9.4 0.4 collective-permute-start.1
  9.8 1.6 %collective-permute-start.2 = (bf16[32,256]{1,0:T(8,128)(2,1)S(1)}, bf16[32,256]{1,0:T(8,128)(2,1)S(1)}, u32[]{:S(2)}, u32[]{:S(2)}) collective-permute-start(bf16[32,256]{1,0:T(8,128)(2,1)S(1)} %get-tuple-element.25), channel_id=1, source_target_pairs={{0,1},{1,0},{2,3},{3,2},{4,5},{5,4},{6,7},{7,6},{8,9},{9,8},{10,11... | collective-permute-start | bytes 49160 | tf_op jit(solution)/shard_map/ppermute | solution.py:54
  11.4 5.6 %collective-permute-start.3 = (bf16[32,256]{1,0:T(8,128)(2,1)S(1)}, bf16[32,256]{1,0:T(8,128)(2,1)S(1)}, u32[]{:S(2)}, u32[]{:S(2)}) collective-permute-start(bf16[32,256]{1,0:T(8,128)(2,1)S(1)} %get-tuple-element.26), channel_id=1, source_target_pairs={{0,15},{1,2},{2,1},{3,4},{4,3},{5,6},{6,5},{7,8},{8,7},{9,10},{10,... | collective-permute-start | bytes 49160 | tf_op jit(solution)/shard_map/ppermute | solution.py:54
  17.0 0.0 copy-done.1
  17.0 0.0 copy-done.2
  17.0 1.2 %local_sums.1.local_ref = f32[512,256]{1,0:T(8,128)S(1)} custom-call(bf16[4096,256]{1,0:T(8,128)(2,1)S(1)} %get-tuple-element.22.contrib_ref, s32[32,128]{1,0:T(8,128)S(1)} %bitcast.4, s32[32,128]{1,0:T(8,128)S(1)} %bitcast.8), custom_call_target="tpu_custom_call" | custom-call | tf_op jit(solution)/shard_map/local_sums/pallas_call | solution.py:331
  18.3 0.0 collective-permute-done.i0
  18.3 0.0 collective-permute-done.1.i1
  18.3 0.0 collective-permute-done.2.i2
  18.3 0.4 collective-permute-done.3.i3
  18.7 0.0 copy-done.7
  18.7 0.0 copy-start
  18.7 0.0 copy-start.3
  18.7 0.0 copy-start.5
  18.7 0.0 copy-start.6
  18.7 0.0 copy-start.8
  18.8 5.1 %sweep.1.fs_ref = bf16[512,256]{1,0:T(8,128)(2,1)S(1)} custom-call(f32[512,256]{1,0:T(8,128)S(1)} %local_sums.1.local_ref, bf16[32,256]{1,0:T(8,128)(2,1)S(1)} %collective-permute-done.i0, bf16[32,256]{1,0:T(8,128)(2,1)S(1)} %collective-permute-done.1.i1, bf16[32,256]{1,0:T(8,128)(2,1)S(1)} %collective-permute-done.2.i2, ...), custom_call_target="tpu_custom_call" | custom-call | tf_op jit(solution)/shard_map/sweep/pallas_call | solution.py:342
  23.8 5.6 %collective-permute-start.7 = (bf16[512,256]{1,0:T(8,128)(2,1)S(1)}, bf16[512,256]{1,0:T(8,128)(2,1)S(1)}, u32[]{:S(2)}, u32[]{:S(2)}) collective-permute-start(bf16[512,256]{1,0:T(8,128)(2,1)S(1)} %sweep.1.fs_ref), channel_id=1, source_target_pairs={{0,15},{1,2},{2,1},{3,4},{4,3},{5,6},{6,5},{7,8},{8,7},{9,10},{10,... | collective-permute-start | bytes 786440 | tf_op jit(solution)/shard_map/ppermute | solution.py:54
  29.4 0.0 collective-permute-start.6
  29.4 0.0 collective-permute-start.5
  29.4 1.6 %collective-permute-start.4 = (bf16[512,256]{1,0:T(8,128)(2,1)S(1)}, bf16[512,256]{1,0:T(8,128)(2,1)S(1)}, u32[]{:S(2)}, u32[]{:S(2)}) collective-permute-start(bf16[512,256]{1,0:T(8,128)(2,1)S(1)} %sweep.1.fs_ref), channel_id=1, source_target_pairs={{0,16},{1,17},{2,18},{3,19},{4,20},{5,21},{6,22},{7,23},{8,24},{9,... | collective-permute-start | bytes 786440 | tf_op jit(solution)/shard_map/ppermute | solution.py:54
  30.9 0.0 copy-done
  30.9 0.0 copy-done.3
  30.9 0.0 copy-done.5
  30.9 0.0 copy-done.6
  30.9 0.0 copy-done.8
  31.0 3.3 %own_rows.1 = (bf16[3072,512]{1,0:T(8,128)(2,1)S(1)}, bf16[3072,256]{1,0:T(8,128)(2,1)S(1)}, bf16[1536,256]{1,0:T(8,128)(2,1)S(1)}, s16[3072,128]{1,0:T(8,128)(2...) custom-call(f32[16]{0:T(128)S(1)} %copy-done.8, bf16[512,256]{1,0:T(8,128)(2,1)S(1)} %sweep.1.fs_ref, ...), custom_call_target="tpu_custom_call" | custom-call | tf_op jit(solution)/shard_map/own_rows/pallas_call | solution.py:355
  34.3 1.7 %collective-permute-done.7.h3 = bf16[512,256]{1,0:T(8,128)(2,1)S(1)} collective-permute-done((bf16[512,256]{1,0:T(8,128)(2,1)S(1)}, bf16[512,256]{1,0:T(8,128)(2,1)S(1)}, u32[]{:S(2)}, u32[]{:S(2)}) %collective-permute-start.7) | collective-permute-done | bytes 262176 | tf_op jit(solution)/shard_map/ppermute | solution.py:54
  35.9 1.5 %collective-permute-done.6.h2 = bf16[512,256]{1,0:T(8,128)(2,1)S(1)} collective-permute-done((bf16[512,256]{1,0:T(8,128)(2,1)S(1)}, bf16[512,256]{1,0:T(8,128)(2,1)S(1)}, u32[]{:S(2)}, u32[]{:S(2)}) %collective-permute-start.6) | collective-permute-done | bytes 262176 | tf_op jit(solution)/shard_map/ppermute | solution.py:54
  37.4 0.0 collective-permute-done.5.h1
  37.4 0.0 collective-permute-done.4.h0
  37.4 9.2 %couple.1 = (f32[512,256]{1,0:T(8,128)S(1)}, bf16[512,256]{1,0:T(8,128)(2,1)S(1)}, bf16[32,256]{1,0:T(8,128)(2,1)S(1)}, bf16[32,256]{1,0:T(8,128)(2,1)S(1)}, bf1...) custom-call(bf16[512,256]{1,0:T(8,128)(2,1)S(1)} %sweep.1.fs_ref, bf16[512,256]{1,0:T(8,128)(2,1)S(1)} %collective-permute-done.4.h0, ...), custom_call_target="tpu_custom_call" | custom-call | tf_op jit(solution)/shard_map/couple/pallas_call | solution.py:370
  46.6 0.1 collective-permute-start.8
  46.7 2.0 %collective-permute-start.9 = (bf16[32,256]{1,0:T(8,128)(2,1)S(1)}, bf16[32,256]{1,0:T(8,128)(2,1)S(1)}, u32[]{:S(2)}, u32[]{:S(2)}) collective-permute-start(bf16[32,256]{1,0:T(8,128)(2,1)S(1)} %get-tuple-element.38), channel_id=1, source_target_pairs={{0,112},{1,113},{2,114},{3,115},{4,116},{5,117},{6,118},{7,119},{8... | collective-permute-start | bytes 49160 | tf_op jit(solution)/shard_map/ppermute | solution.py:54
  48.7 2.0 %collective-permute-start.10 = (bf16[32,256]{1,0:T(8,128)(2,1)S(1)}, bf16[32,256]{1,0:T(8,128)(2,1)S(1)}, u32[]{:S(2)}, u32[]{:S(2)}) collective-permute-start(bf16[32,256]{1,0:T(8,128)(2,1)S(1)} %get-tuple-element.39), channel_id=1, source_target_pairs={{0,1},{1,0},{2,3},{3,2},{4,5},{5,4},{6,7},{7,6},{8,9},{9,8},{10,11... | collective-permute-start | bytes 49160 | tf_op jit(solution)/shard_map/ppermute | solution.py:54
  50.7 0.7 %collective-permute-start.11 = (bf16[32,256]{1,0:T(8,128)(2,1)S(1)}, bf16[32,256]{1,0:T(8,128)(2,1)S(1)}, u32[]{:S(2)}, u32[]{:S(2)}) collective-permute-start(bf16[32,256]{1,0:T(8,128)(2,1)S(1)} %get-tuple-element.40), channel_id=1, source_target_pairs={{0,15},{1,2},{2,1},{3,4},{4,3},{5,6},{6,5},{7,8},{8,7},{9,10},{10,... | collective-permute-start | bytes 49160 | tf_op jit(solution)/shard_map/ppermute | solution.py:54
  51.4 1.7 %fetch.1 = (bf16[4096,256]{1,0:T(8,128)(2,1)S(1)}, f32[512,256]{1,0:T(8,128)}) custom-call(bf16[512,256]{1,0:T(8,128)(2,1)S(1)} %get-tuple-element.33.ans_ref, s32[32,128]{1,0:T(8,128)S(1)} %bitcast.5, s32[32,128]{1,0:T(8,128)S(1)} %bitcast.9, f32[512,256]{1,0:T(8,128)S(1)} %get-tuple-element.34.sol_ref), custom_call_target="tpu_custom_call" | custom-call | tf_op jit(solution)/shard_map/fetch/pallas_call | solution.py:382
  53.1 0.0 collective-permute-done.8.r0
  53.1 0.0 collective-permute-done.9.r1
  53.1 0.0 collective-permute-done.10.r2
  53.1 4.7 %collective-permute-done.11.r3 = bf16[32,256]{1,0:T(8,128)(2,1)S(1)} collective-permute-done((bf16[32,256]{1,0:T(8,128)(2,1)S(1)}, bf16[32,256]{1,0:T(8,128)(2,1)S(1)}, u32[]{:S(2)}, u32[]{:S(2)}) %collective-permute-start.11) | collective-permute-done | bytes 16416 | tf_op jit(solution)/shard_map/ppermute | solution.py:54
  57.8 0.0 copy-done.4
  57.8 6.5 %prolong.1 = bf16[4096,256]{1,0:T(8,128)(2,1)} custom-call(bf16[4096,256]{1,0:T(8,128)(2,1)S(1)} %get-tuple-element.36.local_ref, bf16[32,256]{1,0:T(8,128)(2,1)S(1)} %collective-permute-done.8.r0, bf16[32,256]{1,0:T(8,128)(2,1)S(1)} %collective-permute-done.9.r1, bf16[32,256]{1,0:T(8,128)(2,1)S(1)} %collective-permute-done.10.r2, ...), custom_call_target="tpu_custom_call" | custom-call | tf_op jit(solution)/shard_map/prolong/pallas_call | solution.py:395
  (1 shorter events, 0.0 us)
Async XLA Ops:
  0.6 16.4 %copy-start.1 = (s32[4096]{0:T(1024)S(1)}, s32[4096]{0:T(1024)}, u32[]{:S(2)}) copy-start(s32[4096]{0:T(1024)} %param.12) | copy-start | bytes 49156
  0.6 16.4 %copy-start.2 = (s32[4096]{0:T(1024)S(1)}, s32[4096]{0:T(1024)}, u32[]{:S(2)}) copy-start(s32[4096]{0:T(1024)} %param.13) | copy-start | bytes 49156
  9.3 9.4 %copy-start.7 = (s32[4,32]{1,0:T(4,128)S(1)}, s32[4,32]{1,0:T(4,128)}, u32[]{:S(2)}) copy-start(s32[4,32]{1,0:T(4,128)} %ghost_ref.3) | copy-start | bytes 1540
  9.3 9.0 %collective-permute-start = (bf16[32,256]{1,0:T(8,128)(2,1)S(1)}, bf16[32,256]{1,0:T(8,128)(2,1)S(1)}, u32[]{:S(2)}, u32[]{:S(2)}) collective-permute-start(bf16[32,256]{1,0:T(8,128)(2,1)S(1)} %get-tuple-element.23), channel_id=1, source_target_pairs={{0,16},{1,17},{2,18},{3,19},{4,20},{5,21},{6,22},{7,23},{8,24},{9,... | collective-permute-start | bytes 49160 | tf_op jit(solution)/shard_map/ppermute | solution.py:54
  9.4 8.9 %collective-permute-start.1 = (bf16[32,256]{1,0:T(8,128)(2,1)S(1)}, bf16[32,256]{1,0:T(8,128)(2,1)S(1)}, u32[]{:S(2)}, u32[]{:S(2)}) collective-permute-start(bf16[32,256]{1,0:T(8,128)(2,1)S(1)} %get-tuple-element.24), channel_id=1, source_target_pairs={{0,112},{1,113},{2,114},{3,115},{4,116},{5,117},{6,118},{7,119},{8... | collective-permute-start | bytes 49160 | tf_op jit(solution)/shard_map/ppermute | solution.py:54
  9.8 8.5 %collective-permute-start.2 = (bf16[32,256]{1,0:T(8,128)(2,1)S(1)}, bf16[32,256]{1,0:T(8,128)(2,1)S(1)}, u32[]{:S(2)}, u32[]{:S(2)}) collective-permute-start(bf16[32,256]{1,0:T(8,128)(2,1)S(1)} %get-tuple-element.25), channel_id=1, source_target_pairs={{0,1},{1,0},{2,3},{3,2},{4,5},{5,4},{6,7},{7,6},{8,9},{9,8},{10,11... | collective-permute-start | bytes 49160 | tf_op jit(solution)/shard_map/ppermute | solution.py:54
  11.4 7.3 %collective-permute-start.3 = (bf16[32,256]{1,0:T(8,128)(2,1)S(1)}, bf16[32,256]{1,0:T(8,128)(2,1)S(1)}, u32[]{:S(2)}, u32[]{:S(2)}) collective-permute-start(bf16[32,256]{1,0:T(8,128)(2,1)S(1)} %get-tuple-element.26), channel_id=1, source_target_pairs={{0,15},{1,2},{2,1},{3,4},{4,3},{5,6},{6,5},{7,8},{8,7},{9,10},{10,... | collective-permute-start | bytes 49160 | tf_op jit(solution)/shard_map/ppermute | solution.py:54
  18.7 12.2 %copy-start = (bf16[8,64,64]{2,1,0:T(8,128)(2,1)S(1)}, bf16[8,64,64]{2,1,0:T(8,128)(2,1)}, u32[]{:S(2)}) copy-start(bf16[8,64,64]{2,1,0:T(8,128)(2,1)} %table_ref.3) | copy-start | bytes 196612
  18.7 12.2 %copy-start.3 = (bf16[6,64,64]{2,1,0:T(8,128)(2,1)S(1)}, bf16[6,64,64]{2,1,0:T(8,128)(2,1)}, u32[]{:S(2)}) copy-start(bf16[6,64,64]{2,1,0:T(8,128)(2,1)} %face_ref.1) | copy-start | bytes 147460
  18.7 12.2 %copy-start.5 = (s32[6,512]{1,0:T(8,128)S(1)}, s32[6,512]{1,0:T(8,128)}, u32[]{:S(2)}) copy-start(s32[6,512]{1,0:T(8,128)} %nb_ref.1) | copy-start | bytes 36868
  18.7 12.2 %copy-start.6 = (s32[6,512]{1,0:T(8,128)S(1)}, s32[6,512]{1,0:T(8,128)}, u32[]{:S(2)}) copy-start(s32[6,512]{1,0:T(8,128)} %ci_ref.1) | copy-start | bytes 36868
  18.7 12.2 %copy-start.8 = (f32[16]{0:T(128)S(1)}, f32[16]{0:T(128)}, u32[]{:S(2)}) copy-start(f32[16]{0:T(128)} %coef_ref.1) | copy-start | bytes 196
  23.8 12.1 %collective-permute-start.7 = (bf16[512,256]{1,0:T(8,128)(2,1)S(1)}, bf16[512,256]{1,0:T(8,128)(2,1)S(1)}, u32[]{:S(2)}, u32[]{:S(2)}) collective-permute-start(bf16[512,256]{1,0:T(8,128)(2,1)S(1)} %sweep.1.fs_ref), channel_id=1, source_target_pairs={{0,15},{1,2},{2,1},{3,4},{4,3},{5,6},{6,5},{7,8},{8,7},{9,10},{10,... | collective-permute-start | bytes 786440 | tf_op jit(solution)/shard_map/ppermute | solution.py:54
  29.4 8.0 %collective-permute-start.6 = (bf16[512,256]{1,0:T(8,128)(2,1)S(1)}, bf16[512,256]{1,0:T(8,128)(2,1)S(1)}, u32[]{:S(2)}, u32[]{:S(2)}) collective-permute-start(bf16[512,256]{1,0:T(8,128)(2,1)S(1)} %sweep.1.fs_ref), channel_id=1, source_target_pairs={{0,1},{1,0},{2,3},{3,2},{4,5},{5,4},{6,7},{7,6},{8,9},{9,8},{10,11... | collective-permute-start | bytes 786440 | tf_op jit(solution)/shard_map/ppermute | solution.py:54
  29.4 8.0 %collective-permute-start.5 = (bf16[512,256]{1,0:T(8,128)(2,1)S(1)}, bf16[512,256]{1,0:T(8,128)(2,1)S(1)}, u32[]{:S(2)}, u32[]{:S(2)}) collective-permute-start(bf16[512,256]{1,0:T(8,128)(2,1)S(1)} %sweep.1.fs_ref), channel_id=1, source_target_pairs={{0,112},{1,113},{2,114},{3,115},{4,116},{5,117},{6,118},{7,119},{8... | collective-permute-start | bytes 786440 | tf_op jit(solution)/shard_map/ppermute | solution.py:54
  29.4 8.0 %collective-permute-start.4 = (bf16[512,256]{1,0:T(8,128)(2,1)S(1)}, bf16[512,256]{1,0:T(8,128)(2,1)S(1)}, u32[]{:S(2)}, u32[]{:S(2)}) collective-permute-start(bf16[512,256]{1,0:T(8,128)(2,1)S(1)} %sweep.1.fs_ref), channel_id=1, source_target_pairs={{0,16},{1,17},{2,18},{3,19},{4,20},{5,21},{6,22},{7,23},{8,24},{9,... | collective-permute-start | bytes 786440 | tf_op jit(solution)/shard_map/ppermute | solution.py:54
  37.4 20.4 %copy-start.4 = (s32[4096]{0:T(1024)S(1)}, s32[4096]{0:T(1024)}, u32[]{:S(2)}) copy-start(s32[4096]{0:T(1024)} %param.15) | copy-start | bytes 49156
  46.6 6.4 %collective-permute-start.8 = (bf16[32,256]{1,0:T(8,128)(2,1)S(1)}, bf16[32,256]{1,0:T(8,128)(2,1)S(1)}, u32[]{:S(2)}, u32[]{:S(2)}) collective-permute-start(bf16[32,256]{1,0:T(8,128)(2,1)S(1)} %get-tuple-element.37), channel_id=1, source_target_pairs={{0,16},{1,17},{2,18},{3,19},{4,20},{5,21},{6,22},{7,23},{8,24},{9,... | collective-permute-start | bytes 49160 | tf_op jit(solution)/shard_map/ppermute | solution.py:54
  46.7 6.4 %collective-permute-start.9 = (bf16[32,256]{1,0:T(8,128)(2,1)S(1)}, bf16[32,256]{1,0:T(8,128)(2,1)S(1)}, u32[]{:S(2)}, u32[]{:S(2)}) collective-permute-start(bf16[32,256]{1,0:T(8,128)(2,1)S(1)} %get-tuple-element.38), channel_id=1, source_target_pairs={{0,112},{1,113},{2,114},{3,115},{4,116},{5,117},{6,118},{7,119},{8... | collective-permute-start | bytes 49160 | tf_op jit(solution)/shard_map/ppermute | solution.py:54
  48.7 4.4 %collective-permute-start.10 = (bf16[32,256]{1,0:T(8,128)(2,1)S(1)}, bf16[32,256]{1,0:T(8,128)(2,1)S(1)}, u32[]{:S(2)}, u32[]{:S(2)}) collective-permute-start(bf16[32,256]{1,0:T(8,128)(2,1)S(1)} %get-tuple-element.39), channel_id=1, source_target_pairs={{0,1},{1,0},{2,3},{3,2},{4,5},{5,4},{6,7},{7,6},{8,9},{9,8},{10,11... | collective-permute-start | bytes 49160 | tf_op jit(solution)/shard_map/ppermute | solution.py:54
  50.7 7.1 %collective-permute-start.11 = (bf16[32,256]{1,0:T(8,128)(2,1)S(1)}, bf16[32,256]{1,0:T(8,128)(2,1)S(1)}, u32[]{:S(2)}, u32[]{:S(2)}) collective-permute-start(bf16[32,256]{1,0:T(8,128)(2,1)S(1)} %get-tuple-element.40), channel_id=1, source_target_pairs={{0,15},{1,2},{2,1},{3,4},{4,3},{5,6},{6,5},{7,8},{8,7},{9,10},{10,... | collective-permute-start | bytes 49160 | tf_op jit(solution)/shard_map/ppermute | solution.py:54
